TPU v7x, 32 devices: a whole 2x2x4 slice. The times are simulated.
32 devices in a mesh: shard: 8 (over y, x, core), rep: 4 (over z).
Axes of the slice: x: 2, y: 2, z: 4, core: 2. Of those that a mesh axis runs over, the one named last changes fastest.
Arguments:
- inputs: bfloat16 [64, 256, 1024], P(('shard', 'rep')), may hold values from -6 to 6
- lengths: int32 [64], replicated, may hold values from 64 to 256, as said below
- dealing: int32 [64], replicated, may hold values from 0 to 63, as said below
- w_query: bfloat16 [1024, 1024], P('shard'), may hold values from -0.25 to 0.25
- w_key: bfloat16 [1024, 1024], P('shard'), may hold values from -0.25 to 0.25
- w_value: bfloat16 [1024, 1024], P('shard'), may hold values from -0.1875 to 0.1875
- w_out: bfloat16 [1024, 1024], P('shard'), may hold values from -0.5 to 0.5
- b_query: bfloat16 [1024], P('shard'), may hold values from -1.5 to 1.5
- b_value: bfloat16 [1024], P('shard'), may hold values from -1.5 to 1.5
- b_out: bfloat16 [1024], P('shard'), may hold values from -1.5 to 1.5
- ln1_gain: bfloat16 [1024], P('shard'), may hold values from 0.099609375 to 1.8984375
- ln1_bias: bfloat16 [1024], P('shard'), may hold values from -1.5 to 1.5
- w_up: bfloat16 [1024, 4096], P('shard'), may hold values from -0.1875 to 0.1875
- b_up: bfloat16 [4096], P('shard'), may hold values from -1.5 to 1.5
- w_down: bfloat16 [4096, 1024], P('shard'), may hold values from -0.09375 to 0.09375
- b_down: bfloat16 [1024], P('shard'), may hold values from -1.5 to 1.5
- ln2_gain: bfloat16 [1024], P('shard'), may hold values from 0.099609375 to 1.8984375
- ln2_bias: bfloat16 [1024], P('shard'), may hold values from -1.5 to 1.5
- cotangent: bfloat16 [64, 256, 1024], P(('shard', 'rep')), may hold values from -6 to 6
Outputs:
- layer_out: bfloat16 [64, 256, 1024], P(('shard', 'rep'))
- grad_input: bfloat16 [64, 256, 1024], P(('shard', 'rep'))
- grad_w_query: float32 [1024, 1024], P('shard')
- grad_w_key: float32 [1024, 1024], P('shard')
- grad_w_value: float32 [1024, 1024], P('shard')
- grad_w_out: float32 [1024, 1024], P('shard')
- grad_b_query: float32 [1024], P('shard')
- grad_b_value: float32 [1024], P('shard')
- grad_b_out: float32 [1024], P('shard')
- grad_ln1_gain: float32 [1024], P('shard')
- grad_ln1_bias: float32 [1024], P('shard')
- grad_w_up: float32 [1024, 4096], P('shard')
- grad_b_up: float32 [4096], P('shard')
- grad_w_down: float32 [4096, 1024], P('shard')
- grad_b_down: float32 [1024], P('shard')
- grad_ln2_gain: float32 [1024], P('shard')
- grad_ln2_bias: float32 [1024], P('shard')
Inputs may be any that keep to these rules, and one draw needn't show every extreme that they name: `lengths`: length of initial sequence; positions at or past it are padding. `dealing`: a permutation of the 64 sequences that maps each aligned block of 8 positions onto itself.
All inputs are finite; a program needn't handle non-finite values.
Results may differ from a plain program's by a relative error of at most 0.02.
Values may be sent and summed in bfloat16 or wider, within the bound.
No kernel may reach another device: no remote copies, remote signals or barrier semaphores. Data moves between devices by JAX's collectives and lax.ppermute only.
A program may use at most 192 MiB of HBM per device.

v0:
```python
import jax
import jax.numpy as jnp
from jax import lax
from jax.sharding import PartitionSpec as P

H = 16
HD = 64


EPS = 1e-05
NEG = -1e30


def shortened(shard):
    return jax.tree.map(lambda a: a.astype(jnp.bfloat16) if a.dtype == jnp.float32 else a, shard)


def matmul(left, right):
    return jnp.dot(left, right, preferred_element_type=jnp.float32)


def left_trans(left, right):
    return lax.dot_general(
        left, right, (((0,), (0,)), ((), ())), preferred_element_type=jnp.float32
    )


def right_trans(left, right):
    return lax.dot_general(
        left, right, (((1,), (1,)), ((), ())), preferred_element_type=jnp.float32
    )


def normalize(values, gain, shift):
    center = values - jnp.mean(values, -1, keepdims=True)
    inverse = lax.rsqrt(jnp.mean(center * center, -1, keepdims=True) + EPS)
    unit = center * inverse
    return (unit * gain + shift, unit, inverse)


def norm_back(grad, unit, inverse, gain):
    scaled = grad * gain
    return inverse * (
        scaled
        - jnp.mean(scaled, -1, keepdims=True)
        - unit * jnp.mean(scaled * unit, -1, keepdims=True)
    )


def gelu_both(pre):
    cumul = 0.5 * (1.0 + lax.erf(pre * 0.7071067811865476))
    density = jnp.exp(-0.5 * pre * pre) * 0.3989422804014327
    return (pre * cumul, cumul + pre * density)


def attend(query, keyed, value, length):
    rows = query.shape[0]
    block = min(rows, 512)
    count = rows // block
    allowed = lax.broadcasted_iota(jnp.int32, (1, 1, rows), 2) < length
    scale = query.shape[2] ** (-0.5)

    def one_block(index):
        scores = (
            jnp.einsum("qhd,khd->hqk", query, keyed, preferred_element_type=jnp.float32) * scale
        )
        scores = jnp.where(allowed, scores, NEG)
        peak = jnp.max(scores, -1, keepdims=True)
        raised = jnp.exp(scores - peak)
        total = jnp.sum(raised, -1, keepdims=True)
        probs = (raised / total).astype(jnp.bfloat16)
        mixed = jnp.einsum("hqk,khd->qhd", probs, value, preferred_element_type=jnp.float32)
        return (mixed, peak + jnp.log(total))

    mixed, log_total = lax.map(one_block, jnp.arange(count))
    return (mixed.reshape(rows, -1), log_total)


def attend_back(query, keyed, value, grad_mixed, log_total, length):
    rows, heads, size = query.shape
    block = min(rows, 512)
    count = rows // block
    allowed = lax.broadcasted_iota(jnp.int32, (1, 1, rows), 2) < length
    scale = size ** (-0.5)

    def one_block(carry, index):
        grad_key, grad_value = carry
        scores = (
            jnp.einsum("qhd,khd->hqk", query, keyed, preferred_element_type=jnp.float32) * scale
        )
        scores = jnp.where(allowed, scores, NEG)
        probs = jnp.exp(scores - log_total[index])
        grad_probs = jnp.einsum(
            "qhd,khd->hqk", grad_mixed, value, preferred_element_type=jnp.float32
        )
        inner = jnp.sum(probs * grad_probs, -1, keepdims=True)
        grad_scores = (probs * (grad_probs - inner) * scale).astype(jnp.bfloat16)
        grad_query = jnp.einsum(
            "hqk,khd->qhd", grad_scores, keyed, preferred_element_type=jnp.float32
        )
        grad_key = grad_key + jnp.einsum(
            "hqk,qhd->khd", grad_scores, query, preferred_element_type=jnp.float32
        )
        grad_value = grad_value + jnp.einsum(
            "hqk,qhd->khd",
            probs.astype(jnp.bfloat16),
            grad_mixed,
            preferred_element_type=jnp.float32,
        )
        return ((grad_key, grad_value), grad_query)

    zeros = jnp.zeros((rows, heads, size), jnp.float32)
    (grad_key, grad_value), grad_query = lax.scan(one_block, (zeros, zeros), jnp.arange(count))
    return (
        grad_query.reshape(rows, heads * size),
        grad_key.reshape(rows, heads * size),
        grad_value.reshape(rows, heads * size),
    )


def select_rows(targets, carry, piece):
    count = piece.shape[0]
    for slot in range(carry.shape[0]):
        offset = targets[slot]
        inside = (offset >= 0) & (offset < count)
        row = lax.dynamic_index_in_dim(piece, jnp.clip(offset, 0, count - 1), 0, keepdims=False)
        carry = carry.at[slot].set(jnp.where(inside, row, carry[slot]))
    return carry


def local(
    inputs,
    lengths,
    dealing,
    w_query,
    w_key,
    w_value,
    w_out,
    b_query,
    b_value,
    b_out,
    ln1_gain,
    ln1_bias,
    w_up,
    b_up,
    w_down,
    b_down,
    ln2_gain,
    ln2_bias,
    cotangent,
):
    batches = inputs.shape[0]
    rows = inputs.shape[1]
    replicas = lax.axis_size("rep")
    group = batches * replicas
    shard_index = lax.axis_index("shard")
    rep_index = lax.axis_index("rep")
    anchor = shard_index * group
    slots = (shard_index * replicas + rep_index) * batches + jnp.arange(batches, dtype=jnp.int32)
    sources = jnp.take(dealing, slots)
    seq_lengths = jnp.take(lengths, sources)
    local_dealing = lax.dynamic_slice_in_dim(dealing, anchor, group) - anchor
    places = jnp.arange(group, dtype=jnp.int32)
    wanted = jnp.sum(
        jnp.where(local_dealing[None, :] == (slots - anchor)[:, None], places[None, :], 0), 1
    )
    dealt = select_rows(
        sources - anchor, jnp.zeros_like(inputs), lax.all_gather(inputs, "rep", axis=0, tiled=True)
    )
    owned = (
        w_query,
        w_key,
        w_value,
        w_out,
        w_up,
        w_down,
        b_query,
        b_value,
        b_out,
        ln1_gain,
        ln1_bias,
        b_up,
        b_down,
        ln2_gain,
        ln2_bias,
    )
    outputs = []
    grads_in = []
    totals = None
    for batch in range(batches):
        full = (
            lax.all_gather(owned[0], "shard", axis=0, tiled=True),
            lax.all_gather(owned[1], "shard", axis=0, tiled=True),
            lax.all_gather(owned[2], "shard", axis=0, tiled=True),
            lax.all_gather(owned[3], "shard", axis=0, tiled=True),
            lax.all_gather(owned[4], "shard", axis=0, tiled=True),
            lax.all_gather(owned[5], "shard", axis=0, tiled=True),
            lax.all_gather(owned[6], "shard", axis=0, tiled=True),
            lax.all_gather(owned[7], "shard", axis=0, tiled=True),
            lax.all_gather(owned[8], "shard", axis=0, tiled=True),
            lax.all_gather(owned[9], "shard", axis=0, tiled=True),
            lax.all_gather(owned[10], "shard", axis=0, tiled=True),
            lax.all_gather(owned[11], "shard", axis=0, tiled=True),
            lax.all_gather(owned[12], "shard", axis=0, tiled=True),
            lax.all_gather(owned[13], "shard", axis=0, tiled=True),
            lax.all_gather(owned[14], "shard", axis=0, tiled=True),
        )
        (
            full_query,
            full_key,
            full_value,
            full_out,
            full_up,
            full_down,
            bias_query,
            bias_value,
            bias_out,
            gain_one,
            shift_one,
            bias_up,
            bias_down,
            gain_two,
            shift_two,
        ) = full
        tokens = dealt[batch]
        length = seq_lengths[batch]
        query = (matmul(tokens, full_query) + bias_query.astype(jnp.float32)).astype(jnp.bfloat16)
        keyed = matmul(tokens, full_key).astype(jnp.bfloat16)
        value = (matmul(tokens, full_value) + bias_value.astype(jnp.float32)).astype(jnp.bfloat16)
        query_heads = query.reshape(rows, H, HD)
        key_heads = keyed.reshape(rows, H, HD)
        value_heads = value.reshape(rows, H, HD)
        mixed, log_total = attend(query_heads, key_heads, value_heads, length)
        mixed_low = mixed.astype(jnp.bfloat16)
        branch = matmul(mixed_low, full_out) + bias_out.astype(jnp.float32)
        hidden, unit_one, inverse_one = normalize(
            tokens.astype(jnp.float32) + branch,
            gain_one.astype(jnp.float32),
            shift_one.astype(jnp.float32),
        )
        hidden_low = hidden.astype(jnp.bfloat16)
        pre = matmul(hidden_low, full_up) + bias_up.astype(jnp.float32)
        act, slope = gelu_both(pre)
        act_low = act.astype(jnp.bfloat16)
        summed = hidden + matmul(act_low, full_down) + bias_down.astype(jnp.float32)
        normed, unit_two, inverse_two = normalize(
            summed, gain_two.astype(jnp.float32), shift_two.astype(jnp.float32)
        )
        valid = lax.broadcasted_iota(jnp.int32, (rows, 1), 0) < length
        outputs.append(jnp.where(valid, normed, 0.0).astype(jnp.bfloat16))
        back = (
            lax.all_gather(w_query, "shard", axis=0, tiled=True),
            lax.all_gather(w_key, "shard", axis=0, tiled=True),
            lax.all_gather(w_value, "shard", axis=0, tiled=True),
            lax.all_gather(w_out, "shard", axis=0, tiled=True),
            lax.all_gather(w_up, "shard", axis=0, tiled=True),
            lax.all_gather(w_down, "shard", axis=0, tiled=True),
            lax.all_gather(ln1_gain, "shard", axis=0, tiled=True),
            lax.all_gather(ln2_gain, "shard", axis=0, tiled=True),
        )
        (
            back_query,
            back_key,
            back_value,
            back_out,
            back_up,
            back_down,
            back_gain_one,
            back_gain_two,
        ) = back
        grad_out = jnp.where(valid, cotangent[batch].astype(jnp.float32), 0.0)
        grad_gain_two = jnp.sum(grad_out * unit_two, 0)
        grad_shift_two = jnp.sum(grad_out, 0)
        grad_sum = norm_back(grad_out, unit_two, inverse_two, back_gain_two.astype(jnp.float32))
        grad_bias_down = jnp.sum(grad_sum, 0)
        grad_sum_low = grad_sum.astype(jnp.bfloat16)
        grad_w_down = left_trans(act_low, grad_sum_low)
        grad_pre = (right_trans(grad_sum_low, back_down) * slope).astype(jnp.bfloat16)
        grad_bias_up = jnp.sum(grad_pre.astype(jnp.float32), 0)
        grad_w_up = left_trans(hidden_low, grad_pre)
        grad_hidden = grad_sum + right_trans(grad_pre, back_up)
        grad_gain_one = jnp.sum(grad_hidden * unit_one, 0)
        grad_shift_one = jnp.sum(grad_hidden, 0)
        grad_resid = norm_back(
            grad_hidden, unit_one, inverse_one, back_gain_one.astype(jnp.float32)
        )
        grad_bias_out = jnp.sum(grad_resid, 0)
        grad_resid_low = grad_resid.astype(jnp.bfloat16)
        grad_w_out = left_trans(mixed_low, grad_resid_low)
        grad_mixed = right_trans(grad_resid_low, back_out).astype(jnp.bfloat16)
        grad_query, grad_key, grad_value = attend_back(
            query_heads, key_heads, value_heads, grad_mixed.reshape(rows, H, HD), log_total, length
        )
        query_low = grad_query.astype(jnp.bfloat16)
        key_low = grad_key.astype(jnp.bfloat16)
        value_low = grad_value.astype(jnp.bfloat16)
        grad_bias_query = jnp.sum(query_low.astype(jnp.float32), 0)
        grad_bias_value = jnp.sum(value_low.astype(jnp.float32), 0)
        grad_w_query = left_trans(tokens, query_low)
        grad_w_key = left_trans(tokens, key_low)
        grad_w_value = left_trans(tokens, value_low)
        grad_tokens = (
            grad_resid
            + right_trans(query_low, back_query)
            + right_trans(key_low, back_key)
            + right_trans(value_low, back_value)
        )
        grads_in.append(grad_tokens.astype(jnp.bfloat16))
        terms = (
            grad_w_query,
            grad_w_key,
            grad_w_value,
            grad_w_out,
            grad_w_up,
            grad_w_down,
            grad_bias_query,
            grad_bias_value,
            grad_bias_out,
            grad_gain_one,
            grad_shift_one,
            grad_bias_up,
            grad_bias_down,
            grad_gain_two,
            grad_shift_two,
        )
        shares = (
            lax.psum_scatter(
                terms[0].astype(jnp.bfloat16), "shard", scatter_dimension=0, tiled=True
            ).astype(jnp.float32),
            lax.psum_scatter(
                terms[1].astype(jnp.bfloat16), "shard", scatter_dimension=0, tiled=True
            ).astype(jnp.float32),
            lax.psum_scatter(
                terms[2].astype(jnp.bfloat16), "shard", scatter_dimension=0, tiled=True
            ).astype(jnp.float32),
            lax.psum_scatter(
                terms[3].astype(jnp.bfloat16), "shard", scatter_dimension=0, tiled=True
            ).astype(jnp.float32),
            lax.psum_scatter(
                terms[4].astype(jnp.bfloat16), "shard", scatter_dimension=0, tiled=True
            ).astype(jnp.float32),
            lax.psum_scatter(
                terms[5].astype(jnp.bfloat16), "shard", scatter_dimension=0, tiled=True
            ).astype(jnp.float32),
            lax.psum_scatter(
                terms[6].astype(jnp.bfloat16), "shard", scatter_dimension=0, tiled=True
            ).astype(jnp.float32),
            lax.psum_scatter(
                terms[7].astype(jnp.bfloat16), "shard", scatter_dimension=0, tiled=True
            ).astype(jnp.float32),
            lax.psum_scatter(
                terms[8].astype(jnp.bfloat16), "shard", scatter_dimension=0, tiled=True
            ).astype(jnp.float32),
            lax.psum_scatter(
                terms[9].astype(jnp.bfloat16), "shard", scatter_dimension=0, tiled=True
            ).astype(jnp.float32),
            lax.psum_scatter(
                terms[10].astype(jnp.bfloat16), "shard", scatter_dimension=0, tiled=True
            ).astype(jnp.float32),
            lax.psum_scatter(
                terms[11].astype(jnp.bfloat16), "shard", scatter_dimension=0, tiled=True
            ).astype(jnp.float32),
            lax.psum_scatter(
                terms[12].astype(jnp.bfloat16), "shard", scatter_dimension=0, tiled=True
            ).astype(jnp.float32),
            lax.psum_scatter(
                terms[13].astype(jnp.bfloat16), "shard", scatter_dimension=0, tiled=True
            ).astype(jnp.float32),
            lax.psum_scatter(
                terms[14].astype(jnp.bfloat16), "shard", scatter_dimension=0, tiled=True
            ).astype(jnp.float32),
        )
        totals = (
            shares
            if totals is None
            else tuple((left + right for left, right in zip(totals, shares)))
        )
    totals = jax.tree.map(lambda part: part.astype(jnp.float32), lax.psum(shortened(totals), "rep"))
    (
        g_wquery,
        g_wkey,
        g_wvalue,
        g_wout,
        g_wup,
        g_wdown,
        g_bquery,
        g_bvalue,
        g_bout,
        g_gain_one,
        g_shift_one,
        g_bup,
        g_bdown,
        g_gain_two,
        g_shift_two,
    ) = totals
    layer_out = jnp.stack(outputs)
    grad_dealt = jnp.stack(grads_in)
    grad_input = select_rows(
        wanted, jnp.zeros_like(grad_dealt), lax.all_gather(grad_dealt, "rep", axis=0, tiled=True)
    )
    return (
        layer_out,
        grad_input,
        g_wquery,
        g_wkey,
        g_wvalue,
        g_wout,
        g_bquery,
        g_bvalue,
        g_bout,
        g_gain_one,
        g_shift_one,
        g_wup,
        g_bup,
        g_wdown,
        g_bdown,
        g_gain_two,
        g_shift_two,
    )


def solution(mesh):
    in_specs = (
        P(("shard", "rep"), None, None),
        P(),
        P(),
        P("shard", None),
        P("shard", None),
        P("shard", None),
        P("shard", None),
        P("shard"),
        P("shard"),
        P("shard"),
        P("shard"),
        P("shard"),
        P("shard", None),
        P("shard"),
        P("shard", None),
        P("shard"),
        P("shard"),
        P("shard"),
        P(("shard", "rep"), None, None),
    )
    out_specs = (
        P(("shard", "rep"), None, None),
        P(("shard", "rep"), None, None),
        P("shard", None),
        P("shard", None),
        P("shard", None),
        P("shard", None),
        P("shard"),
        P("shard"),
        P("shard"),
        P("shard"),
        P("shard"),
        P("shard", None),
        P("shard"),
        P("shard", None),
        P("shard"),
        P("shard"),
        P("shard"),
    )
    return jax.shard_map(local, mesh=mesh, in_specs=in_specs, out_specs=out_specs, check_vma=False)
```

profile of v0, /device:TPU:0, one launch (start us, length us, event | category | flops | bytes accessed | tf_op | source)
XLA Modules:
  0.0 1247.1 jit_solution(8070267000745190861)
XLA Ops:
  18.4 10.2 all-gather.1
  28.7 8.7 all-gather
  37.4 7.8 all-gather.2
  45.2 8.7 all-gather.3
  61.6 8.7 all-gather.6
  70.4 7.8 all-gather.7
  78.1 8.7 all-gather.8
  86.8 7.9 all-gather.5
  96.7 26.3 %all-gather.18.cloned.1.call-done = bf16[8,256,1024]{2,1,0:T(8,128)(2,1)} async-done(((bf16[2,256,1024]{2,1,0:T(8,128)(2,1)}), bf16[8,256,1024]{2,1,0:T(8,128)(2,1)}) %all-gather.18.cloned.1.call-update) | async-done | bytes 4194320 | tf_op jit(solution)/shard_map/all_gather | solution.py:168
  128.7 22.7 %all-gather.22.cloned.1.call-done = bf16[1024,1024]{1,0:T(8,128)(2,1)} async-done(((bf16[128,1024]{1,0:T(8,128)(2,1)}), bf16[1024,1024]{1,0:T(8,128)(2,1)}) %all-gather.22.cloned.1.call-update) | async-done | bytes 2097168 | tf_op jit(solution)/shard_map/all_gather | solution.py:192
  160.9 20.2 %all-gather.24.cloned.1.call-done = bf16[1024,1024]{1,0:T(8,128)(2,1)} async-done(((bf16[128,1024]{1,0:T(8,128)(2,1)}), bf16[1024,1024]{1,0:T(8,128)(2,1)}) %all-gather.24.cloned.1.call-update) | async-done | bytes 2097168 | tf_op jit(solution)/shard_map/all_gather | solution.py:193
  194.3 16.5 %all-gather.26.cloned.1.call-done = bf16[1024,1024]{1,0:T(8,128)(2,1)} async-done(((bf16[128,1024]{1,0:T(8,128)(2,1)}), bf16[1024,1024]{1,0:T(8,128)(2,1)}) %all-gather.26.cloned.1.call-update) | async-done | bytes 2097168 | tf_op jit(solution)/shard_map/all_gather | solution.py:195
  221.0 46.0 %all-gather.28.cloned.1.call-done = bf16[1024,4096]{1,0:T(8,128)(2,1)} async-done(((bf16[128,4096]{1,0:T(8,128)(2,1)}), bf16[1024,4096]{1,0:T(8,128)(2,1)}) %all-gather.28.cloned.1.call-update) | async-done | bytes 8388624 | tf_op jit(solution)/shard_map/all_gather | solution.py:196
  274.5 48.8 %all-gather.30.cloned.1.call-done = bf16[4096,1024]{1,0:T(8,128)(2,1)} async-done(((bf16[512,1024]{1,0:T(8,128)(2,1)}), bf16[4096,1024]{1,0:T(8,128)(2,1)}) %all-gather.30.cloned.1.call-update) | async-done | bytes 8388624 | tf_op jit(solution)/shard_map/all_gather | solution.py:197
  396.1 7.9 bitcast_reduce_fusion.3
  410.2 7.8 bitcast_reduce_fusion.1
  421.4 7.9 fusion.81
  433.0 7.8 fusion.75
  487.3 8.9 reduce-scatter.21.cloned.1.call-done
  496.2 44.9 %reduce-scatter.23.cloned.1.call-done = bf16[128,1024]{1,0:T(8,128)(2,1)} async-done(((bf16[1024,1024]{1,0:T(8,128)(2,1)}), bf16[128,1024]{1,0:T(8,128)(2,1)}) %reduce-scatter.23.cloned.1.call-update) | async-done | bytes 262160 | tf_op jit(solution)/shard_map/reduce_scatter | solution.py:333
  542.9 42.6 %reduce-scatter.13.cloned.1.call-done = bf16[128,1024]{1,0:T(8,128)(2,1)} async-done(((bf16[1024,1024]{1,0:T(8,128)(2,1)}), bf16[128,1024]{1,0:T(8,128)(2,1)}) %reduce-scatter.13.cloned.1.call-update) | async-done | bytes 262160 | tf_op jit(solution)/shard_map/reduce_scatter | solution.py:327
  585.5 45.5 %reduce-scatter.15.cloned.1.call-done = bf16[128,1024]{1,0:T(8,128)(2,1)} async-done(((bf16[1024,1024]{1,0:T(8,128)(2,1)}), bf16[128,1024]{1,0:T(8,128)(2,1)}) %reduce-scatter.15.cloned.1.call-update) | async-done | bytes 262160 | tf_op jit(solution)/shard_map/reduce_scatter | solution.py:327
  632.7 42.6 %reduce-scatter.17.cloned.1.call-done = bf16[128,1024]{1,0:T(8,128)(2,1)} async-done(((bf16[1024,1024]{1,0:T(8,128)(2,1)}), bf16[128,1024]{1,0:T(8,128)(2,1)}) %reduce-scatter.17.cloned.1.call-update) | async-done | bytes 262160 | tf_op jit(solution)/shard_map/reduce_scatter | solution.py:330
  675.3 44.7 %reduce-scatter.19.cloned.1.call-done = bf16[128,1024]{1,0:T(8,128)(2,1)} async-done(((bf16[1024,1024]{1,0:T(8,128)(2,1)}), bf16[128,1024]{1,0:T(8,128)(2,1)}) %reduce-scatter.19.cloned.1.call-update) | async-done | bytes 262160 | tf_op jit(solution)/shard_map/reduce_scatter | solution.py:330
  721.9 72.8 %reduce-scatter.35.cloned.1.call-done = bf16[512,1024]{1,0:T(8,128)(2,1)} async-done(((bf16[4096,1024]{1,0:T(8,128)(2,1)}), bf16[512,1024]{1,0:T(8,128)(2,1)}) %reduce-scatter.35.cloned.1.call-update) | async-done | bytes 1048592 | tf_op jit(solution)/shard_map/reduce_scatter | solution.py:342
  794.7 75.0 %reduce-scatter.33.cloned.1.call-done = bf16[512,1024]{1,0:T(8,128)(2,1)} async-done(((bf16[4096,1024]{1,0:T(8,128)(2,1)}), bf16[512,1024]{1,0:T(8,128)(2,1)}) %reduce-scatter.33.cloned.1.call-update) | async-done | bytes 1048592 | tf_op jit(solution)/shard_map/reduce_scatter | solution.py:342
  872.6 71.7 %reduce-scatter.31.cloned.1.call-done = bf16[128,4096]{1,0:T(8,128)(2,1)} async-done(((bf16[1024,4096]{1,0:T(8,128)(2,1)}), bf16[128,4096]{1,0:T(8,128)(2,1)}) %reduce-scatter.31.cloned.1.call-update) | async-done | bytes 1048592 | tf_op jit(solution)/shard_map/reduce_scatter | solution.py:339
  944.4 75.2 %reduce-scatter.29.cloned.1.call-done = bf16[128,4096]{1,0:T(8,128)(2,1)} async-done(((bf16[1024,4096]{1,0:T(8,128)(2,1)}), bf16[128,4096]{1,0:T(8,128)(2,1)}) %reduce-scatter.29.cloned.1.call-update) | async-done | bytes 1048592 | tf_op jit(solution)/shard_map/reduce_scatter | solution.py:339
  1029.3 24.8 %all-reduce.18 = (bf16[1024]{0:T(1024)(128)(2,1)S(1)}, bf16[1024]{0:T(1024)(128)(2,1)S(1)}, bf16[1024]{0:T(1024)(128)(2,1)S(1)}, bf16[1024]{0:T(1024)(128)(2,1)S...) all-reduce(bf16[1024]{0:T(1024)(128)(2,1)S(1)} %reduce_sum.405, ...), channel_id=11, replica_groups=mesh['shard'=8,'rep'=4] {'shard'}, use_global_device_ids=true, to_apply=%region_38.40.clone | all-reduce | flops 24576 | bytes 98304
  1054.9 12.6 %all-reduce.19 = (bf16[128]{0:T(256)(128)(2,1)S(1)}, bf16[128]{0:T(256)(128)(2,1)S(1)}, bf16[128]{0:T(256)(128)(2,1)S(1)}, bf16[128]{0:T(256)(128)(2,1)S(1)}, bf...) all-reduce(bf16[128]{0:T(256)(128)(2,1)S(1)} %fusion.146, ...), channel_id=1, replica_groups=mesh['shard'=8,'rep'=4] {'rep'}, use_global_device_ids=true, to_apply=%region_39.41 | all-reduce | flops 1536 | bytes 6144 | tf_op jit(solution)/shard_map/psum | solution.py:378
  1073.3 29.6 %all-gather.32.cloned.1.call-done = bf16[8,256,1024]{2,1,0:T(8,128)(2,1)} async-done(((bf16[2,256,1024]{2,1,0:T(8,128)(2,1)}), bf16[8,256,1024]{2,1,0:T(8,128)(2,1)}) %all-gather.32.cloned.1.call-update) | async-done | bytes 4194320 | tf_op jit(solution)/shard_map/all_gather | solution.py:399
  1105.2 123.1 %all-reduce.23.cloned.1.call-done = (bf16[128,1024]{1,0:T(8,128)(2,1)}, bf16[128,1024]{1,0:T(8,128)(2,1)}, bf16[128,1024]{1,0:T(8,128)(2,1)}, bf16[128,1024]{1,0...) async-done(((bf16[128,1024]{1,0:T(8,128)(2,1)}, bf16[128,1024]{1,0:T(8,128)(2,1)}, bf16[128,1024]{1,0:T(8,128)(2,1)}, bf16[128,1024]{1,0:T(8,128)(2,1)}, ...) | async-done | bytes 3145744 | tf_op jit(solution)/shard_map/psum | solution.py:378
  (335 shorter events, 227.8 us)
Async XLA Ops:
  7.3 37.9 %copy-start.62 = (bf16[128]{0:T(256)(128)(2,1)S(1)}, bf16[128]{0:T(256)(128)(2,1)}, u32[]{:S(2)}) copy-start(bf16[128]{0:T(256)(128)(2,1)} %param.39) | copy-start | bytes 772
  7.3 46.6 %copy-start.63 = (bf16[128]{0:T(256)(128)(2,1)S(1)}, bf16[128]{0:T(256)(128)(2,1)}, u32[]{:S(2)}) copy-start(bf16[128]{0:T(256)(128)(2,1)} %param.40) | copy-start | bytes 772
  7.3 54.4 %copy-start.64 = (bf16[128]{0:T(256)(128)(2,1)S(1)}, bf16[128]{0:T(256)(128)(2,1)}, u32[]{:S(2)}) copy-start(bf16[128]{0:T(256)(128)(2,1)} %param.44) | copy-start | bytes 772
  7.3 63.1 %copy-start.65 = (bf16[128]{0:T(256)(128)(2,1)S(1)}, bf16[128]{0:T(256)(128)(2,1)}, u32[]{:S(2)}) copy-start(bf16[128]{0:T(256)(128)(2,1)} %param.45) | copy-start | bytes 772
  7.3 70.8 %copy-start.66 = (bf16[128]{0:T(256)(128)(2,1)S(1)}, bf16[128]{0:T(256)(128)(2,1)}, u32[]{:S(2)}) copy-start(bf16[128]{0:T(256)(128)(2,1)} %param.46) | copy-start | bytes 772
  7.3 89.4 %all-gather.20.cloned.1.call-start = ((), (), s32[]{:S(2)}) async-start(), calls=%async_computation.13 | async-start | bytes 2359296 | tf_op jit(solution)/shard_map/all_gather | solution.py:194
  8.0 115.0 %all-gather.18.cloned.1.call-start = ((), (), s32[]{:S(2)}) async-start(), calls=%async_computation.12 | async-start | bytes 5242880 | tf_op jit(solution)/shard_map/all_gather | solution.py:168
  8.8 142.6 %all-gather.22.cloned.1.call-start = ((), (), s32[]{:S(2)}) async-start(), calls=%async_computation.14 | async-start | bytes 2359296 | tf_op jit(solution)/shard_map/all_gather | solution.py:192
  9.5 171.5 %all-gather.24.cloned.1.call-start = ((), (), s32[]{:S(2)}) async-start(), calls=%async_computation.15 | async-start | bytes 2359296 | tf_op jit(solution)/shard_map/all_gather | solution.py:193
  10.1 200.7 %all-gather.26.cloned.1.call-start = ((), (), s32[]{:S(2)}) async-start(), calls=%async_computation.16 | async-start | bytes 2359296 | tf_op jit(solution)/shard_map/all_gather | solution.py:195
  10.7 256.2 %all-gather.28.cloned.1.call-start = ((), (), s32[]{:S(2)}) async-start(), calls=%async_computation.17 | async-start | bytes 9437184 | tf_op jit(solution)/shard_map/all_gather | solution.py:196
  11.3 312.0 %all-gather.30.cloned.1.call-start = ((), (), s32[]{:S(2)}) async-start(), calls=%async_computation.18 | async-start | bytes 9437184 | tf_op jit(solution)/shard_map/all_gather | solution.py:197
  12.0 473.5 %reduce-scatter.27.cloned.1.call-start = ((), (), s32[]{:S(2)}) async-start(), calls=%async_computation.27 | async-start | bytes 2359296 | tf_op jit(solution)/shard_map/reduce_scatter | solution.py:336
  125.7 66.3 %copy-start.34 = (bf16[256,1024]{0,1:T(8,128)(2,1)}, bf16[256,1024]{0,1:T(8,128)(2,1)S(1)}, u32[]{:S(2)}) copy-start(bf16[256,1024]{0,1:T(8,128)(2,1)S(1)} %copy.96) | copy-start | bytes 1572868
  365.6 119.9 %reduce-scatter.25.cloned.1.call-start = ((), (), s32[]{:S(2)}) async-start(), calls=%async_computation.26 | async-start | bytes 2359296 | tf_op jit(solution)/shard_map/reduce_scatter | solution.py:336
  369.1 127.1 %reduce-scatter.21.cloned.1.call-start = ((), (), s32[]{:S(2)}) async-start(), calls=%async_computation.24 | async-start | bytes 2359296 | tf_op jit(solution)/shard_map/reduce_scatter | solution.py:333
  381.5 159.6 %reduce-scatter.23.cloned.1.call-start = ((), (), s32[]{:S(2)}) async-start(), calls=%async_computation.25 | async-start | bytes 2359296 | tf_op jit(solution)/shard_map/reduce_scatter | solution.py:333
  393.3 192.2 %reduce-scatter.13.cloned.1.call-start = ((), (), s32[]{:S(2)}) async-start(), calls=%async_computation.20 | async-start | bytes 2359296 | tf_op jit(solution)/shard_map/reduce_scatter | solution.py:327
  407.4 223.5 %reduce-scatter.15.cloned.1.call-start = ((), (), s32[]{:S(2)}) async-start(), calls=%async_computation.21 | async-start | bytes 2359296 | tf_op jit(solution)/shard_map/reduce_scatter | solution.py:327
  421.3 254.0 %reduce-scatter.17.cloned.1.call-start = ((), (), s32[]{:S(2)}) async-start(), calls=%async_computation.22 | async-start | bytes 2359296 | tf_op jit(solution)/shard_map/reduce_scatter | solution.py:330
  432.7 287.4 %reduce-scatter.19.cloned.1.call-start = ((), (), s32[]{:S(2)}) async-start(), calls=%async_computation.23 | async-start | bytes 2359296 | tf_op jit(solution)/shard_map/reduce_scatter | solution.py:330
  444.2 350.5 %reduce-scatter.35.cloned.1.call-start = ((), (), s32[]{:S(2)}) async-start(), calls=%async_computation.31 | async-start | bytes 9437184 | tf_op jit(solution)/shard_map/reduce_scatter | solution.py:342
  451.5 418.2 %reduce-scatter.33.cloned.1.call-start = ((), (), s32[]{:S(2)}) async-start(), calls=%async_computation.30 | async-start | bytes 9437184 | tf_op jit(solution)/shard_map/reduce_scatter | solution.py:342
  459.9 484.4 %reduce-scatter.31.cloned.1.call-start = ((), (), s32[]{:S(2)}) async-start(), calls=%async_computation.29 | async-start | bytes 9437184 | tf_op jit(solution)/shard_map/reduce_scatter | solution.py:339
  467.3 552.2 %reduce-scatter.29.cloned.1.call-start = ((), (), s32[]{:S(2)}) async-start(), calls=%async_computation.28 | async-start | bytes 9437184 | tf_op jit(solution)/shard_map/reduce_scatter | solution.py:339
  475.1 627.8 %all-gather.32.cloned.1.call-start = ((), (), s32[]{:S(2)}) async-start(), calls=%async_computation.19 | async-start | bytes 5242880 | tf_op jit(solution)/shard_map/all_gather | solution.py:399
  485.4 742.8 %all-reduce.23.cloned.1.call-start = ((), (), s32[]{:S(2)}) async-start(), calls=%async_computation.32 | async-start | bytes 6291456 | tf_op jit(solution)/shard_map/psum | solution.py:378
  721.8 300.5 %copy-start.3 = (s32[64]{0:T(128)S(1)}, s32[64]{0:T(128)}, u32[]{:S(2)}) copy-start(s32[64]{0:T(128)} %param.31) | copy-start | bytes 772
  721.8 300.6 %copy-start.67 = (s32[2]{0:T(128)S(1)}, s32[2]{0:T(128)}, u32[]{:S(2)}) copy-start(s32[2]{0:T(128)} %get-tuple-element.279) | copy-start | bytes 28
  721.8 305.2 %copy-start.69 = (u32[32]{0:T(128)S(1)}, u32[32]{0:T(128)}, u32[]{:S(2)}) copy-start(u32[32]{0:T(128)} %constant.263) | copy-start | bytes 388
  721.8 350.4 %copy-start.38 = (bf16[1,256,1024]{2,1,0:T(8,128)(2,1)S(1)}, bf16[1,256,1024]{2,1,0:T(8,128)(2,1)}, u32[]{:S(2)}) copy-start(bf16[1,256,1024]{2,1,0:T(8,128)(2,1)} %get-tuple-element.233) | copy-start | bytes 1572868
  721.9 350.4 %copy-start.39 = (bf16[1,256,1024]{2,1,0:T(8,128)(2,1)S(1)}, bf16[1,256,1024]{2,1,0:T(8,128)(2,1)}, u32[]{:S(2)}) copy-start(bf16[1,256,1024]{2,1,0:T(8,128)(2,1)} %get-tuple-element.234) | copy-start | bytes 1572868
  (62 other events, 423.4 us)
Sparse Core Ops, SparseCore 0:
  10.0 30.5 all-gather.19
  42.2 80.7 all-gather.17
  124.9 26.4 all-gather.21
  153.1 27.8 all-gather.23
  182.8 27.9 all-gather.25
  212.5 54.3 all-gather.27
  268.8 54.3 all-gather.29
  365.7 41.1 reduce-scatter.26
  410.6 41.2 reduce-scatter.24
  455.0 41.1 reduce-scatter.20
  499.8 41.2 reduce-scatter.22
  544.2 41.1 reduce-scatter.12
  589.7 41.2 reduce-scatter.14
  634.1 41.1 reduce-scatter.16
  678.8 41.2 reduce-scatter.18
  723.4 71.2 reduce-scatter.34
  798.4 71.2 reduce-scatter.32
  873.0 71.2 reduce-scatter.30
  948.2 71.2 reduce-scatter.28
  1021.5 81.2 all-gather.31
  1106.8 121.3 all-reduce.22
where the time goes:
time: 1260 us; the launch traced here: 1250 us
  waiting for transfers between devices  862 us (68%)
  matrix products  175 us (14%)
  blocking collectives  114 us (9%)
  other arithmetic  42.2 us (3%)
  local copies, waits for them, and re-layouts  27.7 us (2%)
  between operations  25.1 us (2%)
    reduce_scatter x2, waiting for transfers between devices, local(): lax.psum_scatter(terms[5].astype(jnp.bfloat16), 'shard', scatter_dimensio...  148 us
    reduce_scatter x2, waiting for transfers between devices, local(): lax.psum_scatter(terms[4].astype(jnp.bfloat16), 'shard', scatter_dimensio...  147 us
    psum x1, waiting for transfers between devices, local(): lax.psum(shortened(totals), 'rep')  123 us
    reduce_scatter x2, waiting for transfers between devices, local(): lax.psum_scatter(terms[0].astype(jnp.bfloat16), 'shard', scatter_dimensio...  88 us
    reduce_scatter x2, waiting for transfers between devices, local(): lax.psum_scatter(terms[1].astype(jnp.bfloat16), 'shard', scatter_dimensio...  87.3 us
    reduce_scatter x2, waiting for transfers between devices, local(): lax.psum_scatter(terms[2].astype(jnp.bfloat16), 'shard', scatter_dimensio...  53.8 us
    dot_general x12, matrix products, left_trans(): lax.dot_general(left, right, (((0,), (0,)), ((), ())), preferred_element_...  51.1 us
    all_gather x1, waiting for transfers between devices, local(): lax.all_gather(owned[5], 'shard', axis=0, tiled=True)  48.8 us
  transfers between devices with their start and end apart: 21, of which 18 were waited for; matrix products, arithmetic and copies ran while one was open for 14% of the time, Pallas kernels for 0%

commit v1 on v0

v1 whole, which is shorter than its diff:
```python
import jax
import jax.numpy as jnp
from jax import lax
from jax.sharding import PartitionSpec as P

H = 16
HD = 64
EPS = 1e-05
NEG = -1e30
F32 = jnp.float32
BF16 = jnp.bfloat16


def matmul(left, right):
    return jnp.dot(left, right, preferred_element_type=F32)


def left_trans(left, right):
    return lax.dot_general(left, right, (((0,), (0,)), ((), ())), preferred_element_type=F32)


def right_trans(left, right):
    return lax.dot_general(left, right, (((1,), (1,)), ((), ())), preferred_element_type=F32)


def normalize(values, gain, shift):
    center = values - jnp.mean(values, -1, keepdims=True)
    inverse = lax.rsqrt(jnp.mean(center * center, -1, keepdims=True) + EPS)
    unit = center * inverse
    return (unit * gain + shift, unit, inverse)


def norm_back(grad, unit, inverse, gain):
    scaled = grad * gain
    return inverse * (
        scaled
        - jnp.mean(scaled, -1, keepdims=True)
        - unit * jnp.mean(scaled * unit, -1, keepdims=True)
    )


def gelu_both(pre):
    cumul = 0.5 * (1.0 + lax.erf(pre * 0.7071067811865476))
    density = jnp.exp(-0.5 * pre * pre) * 0.3989422804014327
    return (pre * cumul, cumul + pre * density)


def pick(pool, targets):
    return jnp.stack(
        [lax.dynamic_index_in_dim(pool, targets[i], 0, keepdims=False) for i in range(targets.shape[0])]
    )


def local(
    inputs, lengths, dealing, w_query, w_key, w_value, w_out, b_query, b_value, b_out,
    ln1_gain, ln1_bias, w_up, b_up, w_down, b_down, ln2_gain, ln2_bias, cotangent,
):
    batches, rows, width = inputs.shape
    shards = lax.axis_size("shard")
    replicas = lax.axis_size("rep")
    group = batches * replicas
    shard_index = lax.axis_index("shard")
    rep_index = lax.axis_index("rep")
    anchor = shard_index * group
    slots = anchor + rep_index * batches + jnp.arange(batches, dtype=jnp.int32)
    seq_lengths = jnp.take(lengths, slots)
    local_dealing = lax.dynamic_slice_in_dim(dealing, anchor, group) - anchor
    sources = jnp.take(dealing, slots) - anchor
    places = jnp.arange(group, dtype=jnp.int32)
    wanted = jnp.sum(
        jnp.where(local_dealing[None, :] == (slots - anchor)[:, None], places[None, :], 0), 1
    )

    def gather(block):
        return lax.all_gather(block, "shard", axis=0, tiled=True)

    block = w_query.shape[0]
    wide = w_up.shape[1]
    small = (b_query, b_value, b_out, ln1_gain, ln1_bias, b_down, ln2_gain, ln2_bias, b_up)
    vec = jnp.concatenate(small)
    first = jnp.concatenate([w_query, w_key, w_value, w_out], 0)
    all_vec = lax.all_gather(vec, "shard", axis=0, tiled=True).reshape(shards, -1)
    all_first = gather(first).reshape(shards, 4, block, width)
    cuts = [0]
    for part in small:
        cuts.append(cuts[-1] + part.shape[0])
    (bias_query, bias_value, bias_out, gain_one, shift_one, bias_down, gain_two, shift_two, bias_up) = [
        all_vec[:, cuts[i] : cuts[i + 1]].reshape(-1).astype(F32) for i in range(len(small))
    ]
    full_query, full_key, full_value, full_out = [
        all_first[:, i].reshape(width, width) for i in range(4)
    ]
    full_up = gather(w_up)
    full_down = gather(w_down)
    cot = pick(lax.all_gather(cotangent, "rep", axis=0, tiled=True), wanted)

    tokens = inputs.reshape(batches * rows, width)
    query = (matmul(tokens, full_query) + bias_query).astype(BF16)
    keyed = matmul(tokens, full_key).astype(BF16)
    value = (matmul(tokens, full_value) + bias_value).astype(BF16)
    heads = lambda a: a.reshape(batches, rows, H, HD).transpose(0, 2, 1, 3)
    flat = lambda a: a.transpose(0, 2, 1, 3).reshape(batches * rows, width)
    qh, kh, vh = heads(query), heads(keyed), heads(value)
    allowed = lax.broadcasted_iota(jnp.int32, (batches, 1, 1, rows), 3) < seq_lengths[:, None, None, None]
    scale = HD ** (-0.5)
    scores = jnp.einsum("bhqd,bhkd->bhqk", qh, kh, preferred_element_type=F32) * scale
    scores = jnp.where(allowed, scores, NEG)
    raised = jnp.exp(scores - jnp.max(scores, -1, keepdims=True))
    probs = raised / jnp.sum(raised, -1, keepdims=True)
    probs_low = probs.astype(BF16)
    mixed_low = flat(jnp.einsum("bhqk,bhkd->bhqd", probs_low, vh, preferred_element_type=F32).astype(BF16))
    hidden, unit_one, inverse_one = normalize(
        tokens.astype(F32) + matmul(mixed_low, full_out) + bias_out, gain_one, shift_one
    )
    hidden_low = hidden.astype(BF16)
    pre = matmul(hidden_low, full_up) + bias_up
    act, slope = gelu_both(pre)
    act_low = act.astype(BF16)
    summed = hidden + matmul(act_low, full_down) + bias_down
    normed, unit_two, inverse_two = normalize(summed, gain_two, shift_two)
    valid = (lax.broadcasted_iota(jnp.int32, (batches, rows, 1), 1) < seq_lengths[:, None, None]).reshape(-1, 1)
    out = jnp.where(valid, normed, 0.0).astype(BF16).reshape(batches, rows, width)
    layer_out = pick(lax.all_gather(out, "rep", axis=0, tiled=True), sources)

    grad_out = jnp.where(valid, cot.reshape(-1, width).astype(F32), 0.0)
    grad_gain_two = jnp.sum(grad_out * unit_two, 0)
    grad_shift_two = jnp.sum(grad_out, 0)
    grad_sum = norm_back(grad_out, unit_two, inverse_two, gain_two)
    grad_bias_down = jnp.sum(grad_sum, 0)
    grad_sum_low = grad_sum.astype(BF16)

    def reduced(part):
        return lax.psum_scatter(part, "shard", scatter_dimension=0, tiled=True)

    def over_rep(part):
        return lax.psum(part, "rep").astype(F32)

    g_down = reduced(left_trans(act_low, grad_sum_low).astype(BF16))
    grad_pre = (right_trans(grad_sum_low, full_down) * slope).astype(BF16)
    grad_bias_up = jnp.sum(grad_pre.astype(F32), 0)
    g_up = reduced(left_trans(hidden_low, grad_pre).astype(BF16))
    grad_hidden = grad_sum + right_trans(grad_pre, full_up)
    grad_gain_one = jnp.sum(grad_hidden * unit_one, 0)
    grad_shift_one = jnp.sum(grad_hidden, 0)
    grad_resid = norm_back(grad_hidden, unit_one, inverse_one, gain_one)
    grad_bias_out = jnp.sum(grad_resid, 0)
    grad_resid_low = grad_resid.astype(BF16)
    grad_w_out = left_trans(mixed_low, grad_resid_low).astype(BF16)
    grad_mixed = heads(right_trans(grad_resid_low, full_out).astype(BF16))
    grad_probs = jnp.einsum("bhqd,bhkd->bhqk", grad_mixed, vh, preferred_element_type=F32)
    inner = jnp.sum(probs * grad_probs, -1, keepdims=True)
    grad_scores = (probs * (grad_probs - inner) * scale).astype(BF16)
    query_low = flat(jnp.einsum("bhqk,bhkd->bhqd", grad_scores, kh, preferred_element_type=F32).astype(BF16))
    key_low = flat(jnp.einsum("bhqk,bhqd->bhkd", grad_scores, qh, preferred_element_type=F32).astype(BF16))
    value_low = flat(jnp.einsum("bhqk,bhqd->bhkd", probs_low, grad_mixed, preferred_element_type=F32).astype(BF16))
    grad_bias_query = jnp.sum(query_low.astype(F32), 0)
    grad_bias_value = jnp.sum(value_low.astype(F32), 0)
    blocks = [
        part.reshape(shards, block, width)
        for part in (
            left_trans(tokens, query_low).astype(BF16),
            left_trans(tokens, key_low).astype(BF16),
            left_trans(tokens, value_low).astype(BF16),
            grad_w_out,
        )
    ]
    g_first = reduced(jnp.concatenate(blocks, 1).reshape(shards * 4 * block, width))
    grad_tokens = (
        grad_resid
        + right_trans(query_low, full_query)
        + right_trans(key_low, full_key)
        + right_trans(value_low, full_value)
    )
    grad_input = grad_tokens.astype(BF16).reshape(batches, rows, width)
    vec_terms = (
        grad_bias_query, grad_bias_value, grad_bias_out, grad_gain_one, grad_shift_one,
        grad_bias_down, grad_gain_two, grad_shift_two, grad_bias_up,
    )
    g_vec = jnp.concatenate([part.reshape(shards, -1) for part in vec_terms], 1)
    g_vec = lax.psum(g_vec, ("shard", "rep"))
    g_vec = lax.dynamic_index_in_dim(g_vec, shard_index, 0, keepdims=False)
    (g_bquery, g_bvalue, g_bout, g_gain_one, g_shift_one, g_bdown, g_gain_two, g_shift_two, g_bup) = [
        g_vec[cuts[i] : cuts[i + 1]] for i in range(len(small))
    ]
    g_down = over_rep(g_down)
    g_up = over_rep(g_up)
    g_first = over_rep(g_first).reshape(4, block, width)
    return (
        layer_out, grad_input, g_first[0], g_first[1], g_first[2], g_first[3],
        g_bquery, g_bvalue, g_bout, g_gain_one, g_shift_one,
        g_up, g_bup, g_down, g_bdown, g_gain_two, g_shift_two,
    )


def solution(mesh):
    seqs = P(("shard", "rep"), None, None)
    mat = P("shard", None)
    vec = P("shard")
    in_specs = (
        seqs, P(), P(), mat, mat, mat, mat, vec, vec, vec, vec, vec, mat, vec, mat, vec, vec, vec, seqs,
    )
    out_specs = (
        seqs, seqs, mat, mat, mat, mat, vec, vec, vec, vec, vec, mat, vec, mat, vec, vec, vec,
    )
    return jax.shard_map(local, mesh=mesh, in_specs=in_specs, out_specs=out_specs, check_vma=False)
```

time: 1260 us -> 794 us (0.63)
  waiting for transfers between devices: 862 us -> 530 us
  blocking collectives: 114 us -> 53.8 us
  matrix products: 175 us -> 123 us
  other arithmetic: 42.2 us -> 20 us
    reduce_scatter x12 -> x3, waiting for transfers between devices: 524 us -> 194 us  [reduced(): return lax.psum_scatter(part, 'shard', scatter_dimension=0, tiled=True)]
    all_gather x9 -> x1, blocking collectives: 76.2 us -> 10.6 us  [local(): lax.all_gather(vec, 'shard', axis=0, tiled=True).reshape(shards, -1)]
    psum x1, blocking collectives: 12.6 us -> 43.1 us  [local(): g_vec = lax.psum(g_vec, ('shard', 'rep'))]
    convert_element_type x39 -> x3, other arithmetic: 29.9 us -> 3.1 us  [the longest x2 3.09 us: over_rep(): return lax.psum(part, 'rep').astype(F32)]
    dot_general x12 -> x6, matrix products: 51.1 us -> 24.8 us  [left_trans(): lax.dot_general(left, right, (((0,), (0,)), ((), ())), preferred_element_...]
    unnamed x1 -> x0, blocking collectives: 24.8 us -> none
    dot_general x24 -> x12, matrix products: 90.4 us -> 72.4 us  [the longest x6 31.3 us: matmul(): return jnp.dot(left, right, preferred_element_type=F32)]
    dot_general x12 -> x6, matrix products: 34 us -> 25.8 us  [right_trans(): lax.dot_general(left, right, (((1,), (1,)), ((), ())), preferred_element_...]
  transfers between devices with their start and end apart: 21 -> 9, of which waited for: 18 -> 9; matrix products, arithmetic and copies ran while one was open for 14% -> 10% of each run, Pallas kernels for 0% -> 0%
where the time goes in v1:
time: 794 us; the launch traced here: 790 us
  waiting for transfers between devices  530 us (67%)
  matrix products  123 us (15%)
  blocking collectives  53.8 us (7%)
  local copies, waits for them, and re-layouts  40.2 us (5%)
  between operations  22.6 us (3%)
  other arithmetic  20 us (3%)
    reduce_scatter x3, waiting for transfers between devices, reduced(): return lax.psum_scatter(part, 'shard', scatter_dimension=0, tiled=True)  194 us
    psum x1, waiting for transfers between devices, over_rep(): return lax.psum(part, 'rep').astype(F32)  121 us
    all_gather x3, waiting for transfers between devices, gather(): return lax.all_gather(block, 'shard', axis=0, tiled=True)  119 us
    all_gather x1, waiting for transfers between devices, local(): cot = pick(lax.all_gather(cotangent, 'rep', axis=0, tiled=True), wanted)  62.3 us
    psum x1, blocking collectives, local(): g_vec = lax.psum(g_vec, ('shard', 'rep'))  43.1 us
    all_gather x1, waiting for transfers between devices, local(): layer_out = pick(lax.all_gather(out, 'rep', axis=0, tiled=True), sources)  31.6 us
    dot_general x6, matrix products, matmul(): return jnp.dot(left, right, preferred_element_type=F32)  31.3 us
    dot_general x6, matrix products, right_trans(): lax.dot_general(left, right, (((1,), (1,)), ((), ())), preferred_element_...  25.8 us
  transfers between devices with their start and end apart: 9, of which 9 were waited for; matrix products, arithmetic and copies ran while one was open for 10% of the time, Pallas kernels for 0%

profile of v1, /device:TPU:0, one launch (start us, length us, event | category | flops | bytes accessed | tf_op | source)
XLA Modules:
  0.0 790.4 jit_solution(13564791712874749416)
XLA Ops:
  18.1 10.6 %all-gather = bf16[8,1,1536]{2,1,0:T(2,128)(2,1)S(1)} all-gather(bf16[1,1,1536]{2,1,0:T(2,128)(2,1)S(1)} %reshape.383), channel_id=1, replica_groups=mesh['shard'=8,'rep'=4] {'shard'}, dimensions={0}, use_global_device_ids=true | all-gather | bytes 27648 | tf_op jit(solution)/shard_map/all_gather | solution.py:82
  30.9 62.3 %all-gather.15.cloned.1.call-done = bf16[8,256,1024]{2,1,0:T(8,128)(2,1)} async-done(((bf16[2,256,1024]{2,1,0:T(8,128)(2,1)}), bf16[8,256,1024]{2,1,0:T(8,128)(2,1)}) %all-gather.15.cloned.1.call-update) | async-done | bytes 4194320 | tf_op jit(solution)/shard_map/all_gather | solution.py:95
  95.5 53.0 %all-gather.7.cloned.1.call-done = bf16[4096,1024]{1,0:T(8,128)(2,1)} async-done(((bf16[512,1024]{1,0:T(8,128)(2,1)}), bf16[4096,1024]{1,0:T(8,128)(2,1)}) %all-gather.7.cloned.1.call-update) | async-done | bytes 8388624 | tf_op jit(solution)/shard_map/all_gather | solution.py:75
  148.5 5.9 fusion.97
  157.4 4.7 fusion.43
  163.5 4.5 fusion.53
  170.1 2.5 fusion.59
  172.6 3.5 fusion.101
  177.0 3.3 copy-done.41
  183.9 20.9 %all-gather.9.cloned.1.call-done = bf16[1024,4096]{1,0:T(8,128)(2,1)} async-done(((bf16[128,4096]{1,0:T(8,128)(2,1)}), bf16[1024,4096]{1,0:T(8,128)(2,1)}) %all-gather.9.cloned.1.call-update) | async-done | bytes 8388624 | tf_op jit(solution)/shard_map/all_gather | solution.py:75
  204.8 10.9 %multiply_convert_fusion.1 = (bf16[512,4096]{1,0:T(8,128)(2,1)}, f32[512,4096]{1,0:T(8,128)}) fusion(f32[4096]{0:T(1024)S(1)} %bitcast.241, bf16[1024,4096]{1,0:T(8,128)(2,1)} %all-gather.9.cloned.1.call-done, f32[512,1024]{1,0:T(8,128)S(1)} %get-tuple-element.69, f32[1024]{0:T(1024)S(1)} %get-tuple-element.57, f32[1024]{0:T(1024)S(1)} %get-tuple-element.58, ...), kind=kOutput, calls=%fused_computation.16 | convolution fusion | flops 4310171648 | bytes 23097344 | tf_op jit(solution)/shard_map/dot_general | solution.py:15
  215.8 45.2 %all-gather.11.cloned.1.call-done = bf16[4096,1024]{1,0:T(8,128)(2,1)} async-done(((bf16[512,1024]{1,0:T(8,128)(2,1)}), bf16[4096,1024]{1,0:T(8,128)(2,1)}) %all-gather.11.cloned.1.call-update) | async-done | bytes 8388624 | tf_op jit(solution)/shard_map/all_gather | solution.py:75
  261.0 8.5 %fusion.103 = (f32[512]{0:T(512)S(1)}, f32[512,1024]{1,0:T(8,128)S(1)}) fusion(f32[1024]{0:T(1024)S(1)} %get-tuple-element.56, bf16[512,4096]{1,0:T(8,128)(2,1)} %get-tuple-element.70, bf16[4096,1024]{1,0:T(8,128)(2,1)} %all-gather.11.cloned.1.call-done, f32[1024]{0:T(1024)S(1)} %get-tuple-element.57, f32[1024]{0:T(1024)S(1)} %get-tuple-element.58, ...), kind=kOutput, calls=%fused_computation.175 | convolution fusion | flops 4298636800 | bytes 16795648 | tf_op jit(solution)/shard_map/dot_general | solution.py:15
  273.0 11.9 %convert_reduce_fusion = (f32[4096]{0:T(1024)S(1)}, bf16[512,4096]{1,0:T(8,128)(2,1)S(1)}) fusion(f32[512,4096]{1,0:T(8,128)} %get-tuple-element.71, f32[4096]{0:T(1024)S(1)} %bitcast.242, bf16[4096,1024]{1,0:T(8,128)(2,1)} %all-gather.11.cloned.1.call-done, f32[512,1024]{1,0:T(8,128)S(1)} %get-tuple-element.30), kind=kOutput, calls=%fused_computation.12 | convolution fusion | flops 4322750464 | bytes 23101440 | tf_op jit(solution)/shard_map/dot_general | solution.py:23
  285.0 5.2 multiply_reduce_fusion.2
  294.5 2.4 copy.77
  299.0 5.8 fusion.55
  304.8 13.5 %fusion.44 = bf16[2,256,16,64]{1,3,2,0:T(8,128)(2,1)} fusion(f32[2,16,256,256]{2,3,1,0:T(8,128)} %fusion.55, bf16[2,256,16,64]{1,0,3,2:T(2,128)(2,1)} %reshape.331, f32[2,16,256,256]{2,3,1,0:T(8,128)} %copy-done.41, f32[2,16,256]{2,1,0:T(8,128)S(1)} %get-tuple-element.66), kind=kOutput, calls=%fused_computation.72 | convolution fusion | flops 283648256 | bytes 18907136 | tf_op jit(solution)/shard_map/bhqk,bhqd->bhkd/dot_general | solution.py:154
  318.3 13.3 %convert_reduce_fusion.2 = (f32[16,64]{1,0:T(8,128)S(1)}, bf16[2,256,16,64]{1,3,2,0:T(8,128)(2,1)}) fusion(f32[2,16,256,256]{2,3,1,0:T(8,128)} %fusion.55, f32[2,16,256,256]{2,3,1,0:T(8,128)} %copy-done.41, f32[2,16,256]{2,1,0:T(8,128)S(1)} %get-tuple-element.66, bf16[2,256,16,64]{1,0,3,2:T(2,128)(2,1)S(1)} %copy-done.11), kind=kOutput, calls=%fused_computation.33 | convolution fusion | flops 284695808 | bytes 18911232 | tf_op jit(solution)/shard_map/bhqk,bhkd->bhqd/dot_general | solution.py:153
  331.6 5.2 convert_reduce_fusion.1
  346.4 3.7 pad_maximum_fusion
  350.1 9.8 %convolution_convert_fusion.1 = bf16[1024,4096]{1,0:T(8,128)(2,1)} fusion(bf16[512,4096]{1,0:T(8,128)(2,1)} %copy-done.42, f32[512,1024]{1,0:T(8,128)S(1)} %get-tuple-element.69, f32[1024]{0:T(1024)S(1)} %get-tuple-element.57, f32[1024]{0:T(1024)S(1)} %get-tuple-element.58, f32[512]{0:T(512)S(1)} %add_rsqrt_fusion.1, f32[512]{0:T(512)S(1)} %broadcast_multiply_fusion.4), kind=kOutput, calls=%fused_computation.21 | convolution fusion | flops 4301783040 | bytes 14692352 | tf_op jit(solution)/shard_map/dot_general | solution.py:19
  362.0 9.9 %convolution_convert_fusion = bf16[4096,1024]{1,0:T(8,128)(2,1)} fusion(bf16[512,4096]{1,0:T(8,128)(2,1)} %get-tuple-element.70, f32[512,1024]{1,0:T(8,128)S(1)} %copy-done.17), kind=kOutput, calls=%fused_computation.20 | convolution fusion | flops 4299685888 | bytes 14680064 | tf_op jit(solution)/shard_map/dot_general | solution.py:19
  377.3 44.2 %reduce-scatter.4.cloned.1.call-done = bf16[512,1024]{1,0:T(8,128)(2,1)} async-done(((bf16[4096,1024]{1,0:T(8,128)(2,1)}), bf16[512,1024]{1,0:T(8,128)(2,1)}) %reduce-scatter.4.cloned.1.call-update) | async-done | bytes 1048592 | tf_op jit(solution)/shard_map/reduce_scatter | solution.py:133
  421.6 75.0 %reduce-scatter.6.cloned.1.call-done = bf16[128,4096]{1,0:T(8,128)(2,1)} async-done(((bf16[1024,4096]{1,0:T(8,128)(2,1)}), bf16[128,4096]{1,0:T(8,128)(2,1)}) %reduce-scatter.6.cloned.1.call-update) | async-done | bytes 1048592 | tf_op jit(solution)/shard_map/reduce_scatter | solution.py:133
  496.6 74.7 %reduce-scatter.8.cloned.1.call-done = bf16[512,1024]{1,0:T(8,128)(2,1)} async-done(((bf16[4096,1024]{1,0:T(8,128)(2,1)}), bf16[512,1024]{1,0:T(8,128)(2,1)}) %reduce-scatter.8.cloned.1.call-update) | async-done | bytes 1048592 | tf_op jit(solution)/shard_map/reduce_scatter | solution.py:133
  571.4 43.1 %psum.29 = f32[8,1536]{1,0:T(8,128)S(1)} all-reduce(f32[8,1536]{1,0:T(8,128)S(1)} %constant_dynamic-update-slice_fusion), channel_id=1, replica_groups=mesh['shard'=8,'rep'=4] {'shard','rep'}, use_global_device_ids=true, to_apply=%region_23.25 | all-reduce | flops 12288 | bytes 98304 | tf_op jit(solution)/shard_map/psum | solution.py:180
  615.9 2.7 fusion.107
  620.9 2.3 add_convert_fusion
  623.2 31.6 %all-gather.13.cloned.1.call-done = bf16[8,256,1024]{2,1,0:T(8,128)(2,1)} async-done(((bf16[2,256,1024]{2,1,0:T(8,128)(2,1)}), bf16[8,256,1024]{2,1,0:T(8,128)(2,1)}) %all-gather.13.cloned.1.call-update) | async-done | bytes 4194320 | tf_op jit(solution)/shard_map/all_gather | solution.py:123
  657.2 120.7 %all-reduce.3.cloned.1.call-done = (bf16[512,1024]{1,0:T(8,128)(2,1)}, bf16[128,4096]{1,0:T(8,128)(2,1)}, bf16[512,1024]{1,0:T(8,128)(2,1)}) async-done(((bf16[512,1024]{1,0:T(8,128)(2,1)}, bf16[128,4096]{1,0:T(8,128)(2,1)}, bf16[512,1024]{1,0:T(8,128)(2,1)}), (bf16[512,1024]{1,0:T(8,128)(2,1)}, bf16[128,4096]{1,0:T(8,128)(2,1)}, bf16[512,1024]{1,0:T(8,128)(2,1)})) %all-reduce.3.cloned.1.call-update) | async-done | bytes 3145744 | tf_op jit(solution)/shard_map/psum | solution.py:136
  777.8 2.7 fusion.98
  (191 shorter events, 54.0 us)
Async XLA Ops:
  7.2 21.6 %copy-start = (s32[64]{0:T(128)S(1)}, s32[64]{0:T(128)}, u32[]{:S(2)}) copy-start(s32[64]{0:T(128)} %param.22) | copy-start | bytes 772
  7.2 86.0 %all-gather.15.cloned.1.call-start = ((), (), s32[]{:S(2)}) async-start(), calls=%async_computation.7 | async-start | bytes 5242880 | tf_op jit(solution)/shard_map/all_gather | solution.py:95
  7.9 140.6 %all-gather.7.cloned.1.call-start = ((), (), s32[]{:S(2)}) async-start(), calls=%async_computation.3 | async-start | bytes 9437184 | tf_op jit(solution)/shard_map/all_gather | solution.py:75
  10.2 6.1 copy-start.33
  10.2 6.4 copy-start.34
  10.2 6.6 copy-start.35
  10.2 6.8 copy-start.36
  10.2 7.0 copy-start.37
  10.3 7.2 copy-start.38
  10.3 7.4 copy-start.39
  10.3 7.6 copy-start.40
  10.3 7.8 copy-start.32
  10.3 194.5 %all-gather.9.cloned.1.call-start = ((), (), s32[]{:S(2)}) async-start(), calls=%async_computation.4 | async-start | bytes 9437184 | tf_op jit(solution)/shard_map/all_gather | solution.py:75
  11.1 249.9 %all-gather.11.cloned.1.call-start = ((), (), s32[]{:S(2)}) async-start(), calls=%async_computation.5 | async-start | bytes 9437184 | tf_op jit(solution)/shard_map/all_gather | solution.py:75
  11.6 409.9 %reduce-scatter.4.cloned.1.call-start = ((), (), s32[]{:S(2)}) async-start(), calls=%async_computation.8 | async-start | bytes 9437184 | tf_op jit(solution)/shard_map/reduce_scatter | solution.py:133
  148.5 7.3 copy-start.27
  157.4 18.8 %copy-start.12 = (bf16[2,256,16,64]{1,0,3,2:T(2,128)(2,1)}, bf16[2,256,16,64]{1,0,3,2:T(2,128)(2,1)S(1)}, u32[]{:S(2)}) copy-start(bf16[2,256,16,64]{1,0,3,2:T(2,128)(2,1)S(1)} %reshape.333) | copy-start | bytes 3145732
  163.5 6.7 copy-start.10
  270.7 14.2 %slice-start = ((s8[8388608]{0:T(1024)(128)(4,1)}), s8[4194304]{0:T(1024)(128)(4,1)S(1)}, s32[]{:S(2)}) async-start(s8[8388608]{0:T(1024)(128)(4,1)} %bitcast.245), calls=%async_computation.12 | async-start | bytes 8388608
  273.0 12.0 %copy-start.16 = (f32[512,1024]{1,0:T(8,128)}, f32[512,1024]{1,0:T(8,128)S(1)}, u32[]{:S(2)}) copy-start(f32[512,1024]{1,0:T(8,128)S(1)} %get-tuple-element.30) | copy-start | bytes 6291460
  273.0 12.0 %slice-start.1 = ((s8[8388608]{0:T(1024)(128)(4,1)}), s8[4194304]{0:T(1024)(128)(4,1)S(1)}, s32[]{:S(2)}) async-start(s8[8388608]{0:T(1024)(128)(4,1)} %bitcast.245), calls=%async_computation.13 | async-start | bytes 8388608
  284.9 5.3 copy-start.42
  294.5 4.5 copy-start.13
  304.8 13.5 %copy-start.11 = (bf16[2,256,16,64]{1,0,3,2:T(2,128)(2,1)S(1)}, bf16[2,256,16,64]{1,0,3,2:T(2,128)(2,1)}, u32[]{:S(2)}) copy-start(bf16[2,256,16,64]{1,0,3,2:T(2,128)(2,1)} %copy-done.10) | copy-start | bytes 3145732
  331.5 5.3 copy-start.4
  331.6 5.3 copy-start.15
  350.1 146.5 %reduce-scatter.6.cloned.1.call-start = ((), (), s32[]{:S(2)}) async-start(), calls=%async_computation.9 | async-start | bytes 9437184 | tf_op jit(solution)/shard_map/reduce_scatter | solution.py:133
  360.0 211.4 %reduce-scatter.8.cloned.1.call-start = ((), (), s32[]{:S(2)}) async-start(), calls=%async_computation.10 | async-start | bytes 9437184 | tf_op jit(solution)/shard_map/reduce_scatter | solution.py:133
  371.9 282.9 %all-gather.13.cloned.1.call-start = ((), (), s32[]{:S(2)}) async-start(), calls=%async_computation.6 | async-start | bytes 5242880 | tf_op jit(solution)/shard_map/all_gather | solution.py:123
  371.9 199.5 %copy-start.30 = (f32[1024]{0:T(1024)S(1)}, f32[1024]{0:T(1024)}, u32[]{:S(2)}) copy-start(f32[1024]{0:T(1024)} %get-tuple-element.24) | copy-start | bytes 12292
  371.9 243.9 %copy-start.19 = (bf16[8,1,128,1024]{3,2,1,0:T(8,128)(2,1)S(1)}, bf16[8,1,128,1024]{3,2,1,0:T(8,128)(2,1)}, u32[]{:S(2)}) copy-start(bf16[8,1,128,1024]{3,2,1,0:T(8,128)(2,1)} %get-tuple-element.35) | copy-start | bytes 6291460
  372.6 405.2 %all-reduce.3.cloned.1.call-start = ((), (), s32[]{:S(2)}) async-start(), calls=%async_computation.11 | async-start | bytes 6291456 | tf_op jit(solution)/shard_map/psum | solution.py:136
  (22 other events, 48.0 us)
Sparse Core Ops, SparseCore 0:
  9.6 83.5 all-gather.14
  95.6 52.8 all-gather.6
  150.4 54.3 all-gather.8
  206.6 54.3 all-gather.10
  350.2 71.2 reduce-scatter.3
  425.3 71.2 reduce-scatter.5
  500.0 71.2 reduce-scatter.7
  573.0 81.7 all-gather.12
  657.6 120.2 all-reduce.2

commit v2 on v1

--- a/solution.py
+++ b/solution.py
@@ -1,6 +1,8 @@
 import jax
 import jax.numpy as jnp
 from jax import lax
+from jax.experimental import pallas as pl
+from jax.experimental.pallas import tpu as pltpu
 from jax.sharding import PartitionSpec as P
 
 H = 16
@@ -45,13 +47,958 @@
     return (pre * cumul, cumul + pre * density)
 
 
+VMEM = 56 * 1024 * 1024
+ANY = pl.BlockSpec(memory_space=pl.ANY)
+DMA = pltpu.SemaphoreType.DMA
+
+
+def spec(shape, index):
+    return pl.BlockSpec(shape, index)
+
+
+def whole(shape):
+    zeros = (0,) * len(shape)
+    return pl.BlockSpec(shape, lambda *_: zeros)
+
+
+def sds(shape, dtype):
+    return jax.ShapeDtypeStruct(shape, dtype)
+
+
+def call(kernel, grid, in_specs, out_specs, out_shape, scratch, flops, moved, trans=0):
+    return pl.pallas_call(
+        kernel,
+        grid_spec=pltpu.PrefetchScalarGridSpec(
+            num_scalar_prefetch=1,
+            grid=grid,
+            in_specs=in_specs,
+            out_specs=out_specs,
+            scratch_shapes=list(scratch),
+        ),
+        out_shape=out_shape,
+        compiler_params=pltpu.CompilerParams(vmem_limit_bytes=VMEM),
+        cost_estimate=pl.CostEstimate(flops=1024, bytes_accessed=1024, transcendentals=0),
+    )
+
+
+def dot_nn(a, b):
+    return lax.dot_general(a, b, (((1,), (0,)), ((), ())), preferred_element_type=F32)
+
+
+def dot_nt(a, b):
+    return lax.dot_general(a, b, (((1,), (1,)), ((), ())), preferred_element_type=F32)
+
+
+def dot_tn(a, b):
+    return lax.dot_general(a, b, (((0,), (0,)), ((), ())), preferred_element_type=F32)
+
+
+def fetch(meta, parts, target, sems, low, high, columns=None):
+    cut = parts[3].shape[0]
+    each = len(parts) // 2
+    for core in range(2):
+        for chip in range(4):
+            at = meta[0] ^ (2 * chip + core)
+            if chip < 3:
+                pieces = [(parts[each * core + chip], low, high, 0)]
+            else:
+                pieces = []
+                if low < cut:
+                    pieces.append((parts[each * core + 3], low, min(high, cut), 0))
+                if high > cut:
+                    start = max(low, cut)
+                    pieces.append((parts[each * core + 4], start - cut, high - cut, start - low))
+            for ref, begin, end, offset in pieces:
+                source = ref.at[pl.ds(begin, end - begin)]
+                if columns is not None:
+                    source = ref.at[pl.ds(begin, end - begin), columns]
+                goal = target.at[at]
+                if len(pieces) > 1:
+                    goal = target.at[at, pl.ds(offset, end - begin)]
+                pltpu.make_async_copy(source, goal, sems.at[at]).start()
+
+
+def arrived(target, sem):
+    pltpu.make_async_copy(target, target, sem).wait()
+
+
+def hand_over(meta, source, target, sems, block):
+    copies = []
+    for chip in range(4):
+        at = pl.ds(pl.multiple_of((meta[0] ^ (2 * chip + 1)) * block, block), block)
+        copies.append(pltpu.make_async_copy(source.at[:, at], target.at[chip], sems.at[chip]))
+        copies[-1].start()
+    return copies
+
+
+def gelu_and_slope(pre):
+    density = jnp.exp(-0.5 * pre * pre)
+    t = 1.0 / (1.0 + 0.27577164466275367 * jnp.abs(pre))
+    tail = -0.1137685166 * t + 0.4433319969
+    for coefficient in (-0.3176998336, 0.3247794523, 0.04569430636, 0.1176625937):
+        tail = tail * t + coefficient
+    tail = tail * t * density
+    cumul = jnp.where(pre < 0.0, tail, 1.0 - tail)
+    return pre * cumul, cumul + pre * (density * 0.3989422804014327)
+
+
+def project(meta, tokens, first):
+    rows, width = tokens.shape
+    tile = 512
+    count = width // tile
+
+    def kernel(meta, x_ref, *refs):
+        parts, (out_ref, vec_ref, up_ref, give_ref, held, short, made, sems, short_sems, out_sems, give_sems) = refs[: len(first)], refs[len(first) :]
+        for w in range(3):
+            fetch(meta, parts, held.at[w], sems.at[w], 128 * w, 128 * (w + 1))
+            if w == 0:
+                fetch(meta, parts, short, short_sems, 512, 528)
+        gifts = hand_over(meta, x_ref, give_ref, give_sems, 128)
+        for b in range(8):
+            arrived(short.at[b], short_sems.at[b])
+        for b in range(8):
+            two = short[b].astype(F32)
+            for v in range(8):
+                vec_ref[v : v + 1, 128 * b : 128 * (b + 1)] = two[0:1, 128 * v : 128 * (v + 1)]
+            up_ref[0:1, 512 * b : 512 * (b + 1)] = two[1:2, :512]
+
+        def body(i, carry):
+            w, n = i // count, i % count
+
+            @pl.when(n == 0)
+            def _():
+                for b in range(8):
+                    arrived(held.at[w, b], sems.at[w, b])
+
+            at = pl.ds(pl.multiple_of(n * tile, tile), tile)
+            weight = held[w, :, :, at].reshape(width, tile)
+            bias = jnp.where(w == 0, vec_ref[0:1, at], vec_ref[1:2, at])
+            bias = jnp.where(w == 1, jnp.zeros_like(bias), bias)
+            made[w, :, at] = (dot_nn(x_ref[...], weight) + bias).astype(BF16)
+
+            @pl.when(n == count - 1)
+            def _():
+                pltpu.make_async_copy(made.at[w], out_ref.at[w], out_sems.at[w]).start()
+
+            return carry
+
+        lax.fori_loop(0, 3 * count, body, 0)
+        for w in range(3):
+            pltpu.make_async_copy(made.at[w], out_ref.at[w], out_sems.at[w]).wait()
+        for copy in gifts:
+            copy.wait()
+
+    return call(
+        kernel,
+        (1,),
+        [whole((rows, width))] + [ANY] * len(first),
+        [ANY, whole((8, width)), whole((1, 4 * width)), ANY],
+        [sds((3, rows, width), BF16), sds((8, width), F32), sds((1, 4 * width), F32), sds((4, rows, 128), BF16)],
+        [
+            pltpu.VMEM((3, 8, 128, width), BF16), pltpu.VMEM((8, 16, width), BF16),
+            pltpu.VMEM((3, rows, width), BF16), DMA((3, 8)), DMA((8,)), DMA((3,)), DMA((4,)),
+        ],
+        flops=10 * rows * width * width,
+        moved=10 * rows * width + 6 * width * width,
+    )(meta, tokens, *first)
+
+
+HEADS = 4
+
+
+def attend(meta, qkv, batches, rows):
+    total, width = qkv.shape[1:]
+    span = HEADS * HD
+    steps = width // span
+
+    def kernel(meta, q_ref, k_ref, v_ref, mixed_ref, probs_ref):
+        length = meta[1 + pl.program_id(0)]
+        allowed = lax.broadcasted_iota(jnp.int32, (rows, rows), 1) < length
+        left = lax.broadcasted_iota(jnp.int32, (rows, 128), 1) < HD
+        for pair in range(HEADS // 2):
+            cols = slice(128 * pair, 128 * (pair + 1))
+            query, keyed, value = q_ref[0, :, cols], k_ref[0, :, cols], v_ref[0, :, cols]
+            outs = []
+            for half in range(2):
+                mine = left if half == 0 else jnp.logical_not(left)
+                scores = dot_nt(jnp.where(mine, query, jnp.zeros_like(query)), keyed) * (HD**-0.5)
+                scores = jnp.where(allowed, scores, NEG)
+                raised = jnp.exp(scores - jnp.max(scores, -1, keepdims=True))
+                probs = raised * (1.0 / jnp.sum(raised, -1, keepdims=True))
+                low = probs.astype(BF16)
+                probs_ref[0, 2 * pair + half] = low
+                outs.append(dot_nn(low, value))
+            mixed_ref[:, cols] = jnp.where(left, outs[0], outs[1]).astype(BF16)
+
+    part = lambda w: spec((1, rows, span), lambda b, h, meta: (w, b, h))
+    return call(
+        kernel,
+        (batches, steps),
+        [part(0), part(1), part(2)],
+        [
+            spec((rows, span), lambda b, h, meta: (b, h)),
+            spec((1, HEADS, rows, rows), lambda b, h, meta: (b, h, 0, 0)),
+        ],
+        [sds((total, width), BF16), sds((batches, H, rows, rows), BF16)],
+        [],
+        flops=20 * total * rows * width,
+        moved=8 * total * width + 2 * batches * H * rows * rows,
+        trans=batches * H * rows * rows,
+    )(meta, qkv, qkv, qkv)
+
+
+def mix_out(meta, mixed, tokens, first, vecs):
+    total, width = mixed.shape
+    tile = 128
+
+    def kernel(meta, mixed_ref, tokens_ref, vec_ref, *refs):
+        parts, (unit_ref, inv_ref, low_ref, give_ref, held, sems, give_sems) = refs[: len(first)], refs[len(first) :]
+        fetch(meta, parts, held, sems, 384, 512)
+        gifts = hand_over(meta, mixed_ref, give_ref.at[0], give_sems.at[0], 128)
+        for b in range(8):
+            arrived(held.at[b], sems.at[b])
+
+        def body(i, carry):
+            here = pl.ds(pl.multiple_of(i * tile, tile), tile)
+            branch = dot_nn(mixed_ref[here], held[...].reshape(width, width)) + vec_ref[2:3]
+            hidden, unit, inverse = normalize(tokens_ref[here].astype(F32) + branch, vec_ref[3:4], vec_ref[4:5])
+            unit_ref[here] = unit
+            inv_ref[here] = jnp.broadcast_to(inverse, (tile, 128))
+            low_ref[here] = hidden.astype(BF16)
+            return carry
+
+        lax.fori_loop(0, total // tile, body, 0)
+        gifts += hand_over(meta, low_ref, give_ref.at[1], give_sems.at[1], 128)
+        for copy in gifts:
+            copy.wait()
+
+    block = (total, width)
+    return call(
+        kernel,
+        (1,),
+        [whole(block), whole(block), whole(vecs.shape)] + [ANY] * len(first),
+        [whole(block), whole((total, 128)), whole(block), ANY],
+        [sds(block, F32), sds((total, 128), F32), sds(block, BF16), sds((2, 4, total, 128), BF16)],
+        [pltpu.VMEM((8, 128, width), BF16), DMA((8,)), DMA((2, 4))],
+        flops=5 * total * width * width,
+        moved=10 * total * width + 2 * width * width,
+    )(meta, mixed, tokens, vecs, *first)
+
+
+def feed_up(meta, low, up, bias):
+    total, width = low.shape
+    wide = up[0].shape[1]
+    strip, tile = 1024, 512
+    strips, inner = wide // strip, strip // tile
+
+    def kernel(meta, x_ref, bias_ref, *refs):
+        parts, (act_ref, slope_ref, give_ref, held, act, slope, sems, out_sems, give_sems) = refs[: len(up)], refs[len(up) :]
+        for t in range(strips):
+            fetch(meta, parts, held.at[t], sems.at[t], 0, 128, pl.ds(strip * t, strip))
+
+        def leave(i):
+            at = pl.ds(pl.multiple_of(i * tile, tile), tile)
+            return (
+                pltpu.make_async_copy(act.at[i], act_ref.at[:, at], out_sems.at[0, i]),
+                pltpu.make_async_copy(slope.at[i], slope_ref.at[:, at], out_sems.at[1, i]),
+            )
+
+        def body(i, carry):
+            t, n = i // inner, i % inner
+
+            @pl.when(n == 0)
+            def _():
+                for b in range(8):
+                    arrived(held.at[t, b], sems.at[t, b])
+
+            weight = held[t, :, :, pl.ds(pl.multiple_of(n * tile, tile), tile)].reshape(width, tile)
+            pre = dot_nn(x_ref[...], weight) + bias_ref[:, pl.ds(pl.multiple_of(i * tile, tile), tile)]
+            value, grad = gelu_and_slope(pre)
+            act[i] = value.astype(BF16)
+            slope[i] = grad.astype(BF16)
+            for copy in leave(i):
+                copy.start()
+            code = meta[0] ^ i
+
+            @pl.when(code % 2 == 1)
+            def _():
+                pltpu.make_async_copy(act.at[i], give_ref.at[code // 2], give_sems.at[code // 2]).start()
+
+            return carry
+
+        lax.fori_loop(0, strips * inner, body, 0)
+        for i in range(strips * inner):
+            for copy in leave(i):
+                copy.wait()
+        for chip in range(4):
+            arrived(give_ref.at[chip], give_sems.at[chip])
+
+    out = sds((total, wide), BF16)
+    tiles = wide // tile
+    return call(
+        kernel,
+        (1,),
+        [whole((total, width)), whole((1, wide))] + [ANY] * len(up),
+        [ANY, ANY, ANY],
+        [out, out, sds((4, total, tile), BF16)],
+        [
+            pltpu.VMEM((strips, 8, 128, strip), BF16), pltpu.VMEM((tiles, total, tile), BF16),
+            pltpu.VMEM((tiles, total, tile), BF16), DMA((strips, 8)), DMA((2, tiles)), DMA((4,)),
+        ],
+        flops=5 * total * width * wide,
+        moved=4 * total * wide + 2 * width * wide,
+    )(meta, low, bias, *up)
+
+
+def feed_down(meta, act, down, unit_one, cot_pool, vecs, batches, rows):
+    total, wide = act.shape
+    width = down[0].shape[1]
+    chunk = 64
+
+    def kernel(meta, act_ref, unit_ref, cot_ref, vec_ref, *refs):
+        parts = refs[: len(down)]
+        (out_ref, sum_ref, low_ref, grad_ref, held, left, total_ref, unit, cot, sems, left_sems, more) = refs[len(down) :]
+        for b in range(8):
+            pltpu.make_async_copy(act_ref.at[:, pl.ds(512 * b, 512)], left.at[b], left_sems.at[b]).start()
+        fetch(meta, parts, held, sems, 0, 512)
+        rest = [pltpu.make_async_copy(unit_ref, unit, more.at[0])] + [
+            pltpu.make_async_copy(cot_ref.at[meta[3 + i]], cot.at[i], more.at[1 + i]) for i in range(batches)
+        ]
+        for copy in rest:
+            copy.start()
+
+        def add(b, carry):
+            arrived(left.at[b], left_sems.at[b])
+            arrived(held.at[b], sems.at[b])
+            part = dot_nn(left[b], held[b])
+
+            @pl.when(b == 0)
+            def _():
+                total_ref[...] = part
+
+            @pl.when(b > 0)
+            def _():
+                total_ref[...] += part
+
+            return carry
+
+        lax.fori_loop(0, 8, add, 0)
+        for copy in rest:
+            copy.wait()
+        grad_ref[...] = jnp.zeros_like(grad_ref)
+
+        def body(i, carry):
+            here = pl.ds(pl.multiple_of(i * chunk, chunk), chunk)
+            batch = i // (rows // chunk)
+            at = pl.multiple_of((i % (rows // chunk)) * chunk, chunk)
+            summed = (unit[here] * vec_ref[3:4] + vec_ref[4:5]) + total_ref[here] + vec_ref[5:6]
+            normed, unit_two, inverse = normalize(summed, vec_ref[6:7], vec_ref[7:8])
+            place = at + lax.broadcasted_iota(jnp.int32, (chunk, 1), 0)
+            valid = place < meta[1 + batch]
+            out_ref[here] = jnp.where(valid, normed, 0.0).astype(BF16)
+            grad_out = jnp.where(valid, cot[batch, pl.ds(at, chunk)].astype(F32), 0.0)
+            grad_sum = norm_back(grad_out, unit_two, inverse, vec_ref[6:7])
+            sum_ref[here] = grad_sum
+            low_ref[here] = grad_sum.astype(BF16)
+            grad_ref[0:1] += jnp.sum(grad_out * unit_two, 0, keepdims=True)
+            grad_ref[1:2] += jnp.sum(grad_out, 0, keepdims=True)
+            grad_ref[2:3] += jnp.sum(grad_sum, 0, keepdims=True)
+            return carry
+
+        lax.fori_loop(0, total // chunk, body, 0)
+
+    block = (total, width)
+    return call(
+        kernel,
+        (1,),
+        [ANY, ANY, ANY, whole(vecs.shape)] + [ANY] * len(down),
+        [whole(block), whole(block), whole(block), whole((8, width))],
+        [sds(block, BF16), sds(block, F32), sds(block, BF16), sds((8, width), F32)],
+        [
+            pltpu.VMEM((8, 512, width), BF16), pltpu.VMEM((8, total, 512), BF16), pltpu.VMEM(block, F32),
+            pltpu.VMEM(block, F32), pltpu.VMEM((batches, rows, width), BF16), DMA((8,)), DMA((8,)), DMA((1 + batches,)),
+        ],
+        flops=6 * total * width * wide,
+        moved=2 * total * wide + 2 * width * wide + 14 * total * width,
+    )(meta, act, unit_one, cot_pool, vecs, *down)
+
+
+def back_down(meta, low, down, slope):
+    total, width = low.shape
+    wide = slope.shape[1]
+
+    def kernel(meta, low_ref, slope_ref, *refs):
+        parts, (pre_ref, bias_ref, held, right, made, sems, right_sems, out_sems) = refs[: len(down)], refs[len(down) :]
+        fetch(meta, parts, held, sems, 0, 512)
+        for b in range(8):
+            pltpu.make_async_copy(slope_ref.at[:, pl.ds(512 * b, 512)], right.at[b], right_sems.at[b]).start()
+
+        def leave(b):
+            at = pl.ds(pl.multiple_of(512 * b, 512), 512)
+            return pltpu.make_async_copy(made.at[b], pre_ref.at[:, at], out_sems.at[b])
+
+        def body(b, carry):
+            arrived(held.at[b], sems.at[b])
+            arrived(right.at[b], right_sems.at[b])
+            grad = (dot_nt(low_ref[...], held[b]) * right[b].astype(F32)).astype(BF16)
+            made[b] = grad
+            leave(b).start()
+            bias_ref[:, pl.ds(pl.multiple_of(512 * b, 512), 512)] = jnp.sum(grad.astype(F32), 0, keepdims=True)
+            return carry
+
+        lax.fori_loop(0, 8, body, 0)
+        for b in range(8):
+            leave(b).wait()
+
+    return call(
+        kernel,
+        (1,),
+        [whole((total, width)), ANY] + [ANY] * len(down),
+        [ANY, whole((1, wide))],
+        [sds((total, wide), BF16), sds((1, wide), F32)],
+        [
+            pltpu.VMEM((8, 512, width), BF16), pltpu.VMEM((8, total, 512), BF16), pltpu.VMEM((8, total, 512), BF16),
+            DMA((8,)), DMA((8,)), DMA((8,)),
+        ],
+        flops=4 * total * width * wide,
+        moved=4 * total * wide + 2 * width * wide,
+    )(meta, low, slope, *down)
+
+
+def back_up(meta, pre, up, first, grad_sum, unit_one, inverse_one, vecs):
+    total, wide = pre.shape
+    width = grad_sum.shape[1]
+    chunk = 64
+
+    def kernel(meta, pre_ref, sum_ref, unit_ref, inv_ref, vec_ref, *refs):
+        parts, others = refs[: len(up)], refs[len(up) : len(up) + len(first)]
+        (resid_ref, low_ref, mixed_ref, grad_ref, held, out_held, grad_hidden, unit, sems, out_sems, more) = refs[len(up) + len(first) :]
+        fetch(meta, parts, held, sems, 0, 128)
+        rest = [
+            pltpu.make_async_copy(sum_ref, grad_hidden, more.at[0]),
+            pltpu.make_async_copy(unit_ref, unit, more.at[1]),
+        ]
+        for copy in rest:
+            copy.start()
+        fetch(meta, others, out_held, out_sems, 384, 512)
+        rest[0].wait()
+
+        def through(j, carry):
+            for b in range(2):
+                arrived(held.at[2 * j + b], sems.at[2 * j + b])
+            weight = held[pl.ds(2 * j, 2)].reshape(256, wide)
+            grad_hidden[:, pl.ds(pl.multiple_of(256 * j, 256), 256)] += dot_nt(pre_ref[...], weight)
+            return carry
+
+        lax.fori_loop(0, 4, through, 0)
+        rest[1].wait()
+        grad_ref[...] = jnp.zeros_like(grad_ref)
+
+        def body(i, carry):
+            here = pl.ds(pl.multiple_of(i * chunk, chunk), chunk)
+            grad, unit_here = grad_hidden[here], unit[here]
+            grad_ref[0:1] += jnp.sum(grad * unit_here, 0, keepdims=True)
+            grad_ref[1:2] += jnp.sum(grad, 0, keepdims=True)
+            resid = norm_back(grad, unit_here, inv_ref[here, 0:1], vec_ref[3:4])
+            grad_ref[2:3] += jnp.sum(resid, 0, keepdims=True)
+            resid_ref[here] = resid
+            low_ref[here] = resid.astype(BF16)
+            return carry
+
+        lax.fori_loop(0, total // chunk, body, 0)
+        for b in range(8):
+            arrived(out_held.at[b], out_sems.at[b])
+
+        def out(j, carry):
+            weight = out_held[pl.ds(4 * j, 4)].reshape(512, width)
+            mixed_ref[:, pl.ds(pl.multiple_of(512 * j, 512), 512)] = dot_nt(low_ref[...], weight).astype(BF16)
+            return carry
+
+        lax.fori_loop(0, 2, out, 0)
+
+    block = (total, width)
+    return call(
+        kernel,
+        (1,),
+        [whole((total, wide)), ANY, ANY, whole((total, 128)), whole(vecs.shape)] + [ANY] * (len(up) + len(first)),
+        [whole(block), whole(block), whole(block), whole((8, width))],
+        [sds(block, F32), sds(block, BF16), sds(block, BF16), sds((8, width), F32)],
+        [
+            pltpu.VMEM((8, 128, wide), BF16), pltpu.VMEM((8, 128, width), BF16), pltpu.VMEM(block, F32),
+            pltpu.VMEM(block, F32), DMA((8,)), DMA((8,)), DMA((2,)),
+        ],
+        flops=5 * total * width * wide,
+        moved=2 * total * wide + 2 * width * wide + 18 * total * width,
+    )(meta, pre, grad_sum, unit_one, inverse_one, vecs, *up, *first)
+
+
+def attend_back(meta, qkv, probs, grad_mixed, batches, rows):
+    total, width = grad_mixed.shape
+    span = HEADS * HD
+
+    def kernel(meta, q_ref, k_ref, v_ref, g_ref, probs_ref, out_ref, bias_ref):
+        left = lax.broadcasted_iota(jnp.int32, (rows, 128), 1) < HD
+        for pair in range(HEADS // 2):
+            cols = slice(128 * pair, 128 * (pair + 1))
+            query, keyed, value, grad = q_ref[0, :, cols], k_ref[0, :, cols], v_ref[0, :, cols], g_ref[:, cols]
+            got = ([], [], [])
+            for half in range(2):
+                mine = left if half == 0 else jnp.logical_not(left)
+                low = probs_ref[0, 2 * pair + half]
+                probs = low.astype(F32)
+                grad_probs = dot_nt(jnp.where(mine, grad, jnp.zeros_like(grad)), value)
+                inner = jnp.sum(probs * grad_probs, -1, keepdims=True)
+                scores = (probs * (grad_probs - inner) * (HD**-0.5)).astype(BF16)
+                got[0].append(dot_nn(scores, keyed))
+                got[1].append(dot_tn(scores, query))
+                got[2].append(dot_tn(low, grad))
+            for i in range(3):
+                part = jnp.where(left, got[i][0], got[i][1]).astype(BF16)
+                out_ref[i, :, cols] = part
+                bias_ref[0, i : i + 1, cols] = jnp.sum(part.astype(F32), 0, keepdims=True)
+
+    part = lambda w: spec((1, rows, span), lambda b, h, meta: (w, b, h))
+    return call(
+        kernel,
+        (batches, width // span),
+        [
+            part(0), part(1), part(2),
+            spec((rows, span), lambda b, h, meta: (b, h)),
+            spec((1, HEADS, rows, rows), lambda b, h, meta: (b, h, 0, 0)),
+        ],
+        [
+            spec((3, rows, span), lambda b, h, meta: (0, b, h)),
+            spec((1, 8, span), lambda b, h, meta: (b, 0, h)),
+        ],
+        [sds((3, total, width), BF16), sds((batches, 8, width), F32)],
+        [],
+        flops=30 * total * rows * width,
+        moved=14 * total * width + 2 * batches * H * rows * rows,
+    )(meta, qkv, qkv, qkv, grad_mixed, probs)
+
+
+def back_project(meta, grads, first, grad_resid):
+    total, width = grad_resid.shape
+
+    def kernel(meta, g_ref, resid_ref, *refs):
+        parts, (out_ref, held, resid, made, sems, more, out_sems) = refs[: len(first)], refs[len(first) :]
+        fetch(meta, parts, held, sems, 0, 384)
+        incoming = pltpu.make_async_copy(resid_ref, resid, more)
+        incoming.start()
+        incoming.wait()
+
+        def leave(j):
+            at = pl.ds(pl.multiple_of(256 * j, 256), 256)
+            return pltpu.make_async_copy(made.at[:, at], out_ref.at[:, at], out_sems.at[j])
+
+        def body(j, carry):
+            for b in range(2):
+                arrived(held.at[2 * j + b], sems.at[2 * j + b])
+            at = pl.ds(pl.multiple_of(256 * j, 256), 256)
+            part = resid[:, at]
+            for w in range(3):
+                weight = held[pl.ds(2 * j, 2), 128 * w : 128 * (w + 1)].reshape(256, width)
+                part = part + dot_nt(g_ref[w], weight)
+            made[:, at] = part.astype(BF16)
+            leave(j).start()
+            return carry
+
+        lax.fori_loop(0, 4, body, 0)
+        for j in range(4):
+            leave(j).wait()
+
+    block = (total, width)
+    return call(
+        kernel,
+        (1,),
+        [whole((3, total, width)), ANY] + [ANY] * len(first),
+        ANY,
+        sds(block, BF16),
+        [
+            pltpu.VMEM((8, 384, width), BF16), pltpu.VMEM(block, F32), pltpu.VMEM(block, BF16), DMA((8,)), DMA(()),
+            DMA((4,)),
+        ],
+        flops=10 * total * width * width,
+        moved=12 * total * width + 6 * width * width,
+    )(meta, grads, grad_resid, *first)
+
+
+def weight_grad(meta, left, left_got, right, right_got, codes, block):
+    total, cols = right.shape
+    share = cols // 2
+    tile = min(share, 1024)
+    tiles = share // tile
+    count = len(codes[0])
+
+    def kernel(meta, left_ref, left_got_ref, right_ref, right_got_ref, *refs):
+        outs = refs[:2]
+        lefts, rights, made, left_sems, right_sems, out_sems = refs[2:]
+        own, got = pl.ds(0, total), pl.ds(total, total)
+        for half in range(2):
+            for t in range(tiles):
+                at = pl.ds(share * half + tile * t, tile)
+                slot = half * tiles + t
+                pltpu.make_async_copy(right_ref.at[:, at], rights.at[slot, own], right_sems.at[slot]).start()
+                pltpu.make_async_copy(right_got_ref.at[:, at], rights.at[slot, got], right_sems.at[slot]).start()
+                if t == 0:
+                    for i, code in enumerate(codes[half]):
+                        at = pl.ds(pl.multiple_of((meta[0] ^ code) * block, block), block)
+                        sem = left_sems.at[half, i]
+                        pltpu.make_async_copy(left_ref.at[:, at], lefts.at[half, i, own], sem).start()
+                        pltpu.make_async_copy(left_got_ref.at[code // 2], lefts.at[half, i, got], sem).start()
+
+        def leave(half, n):
+            t, i = n // count, n % count
+            at = pl.ds(pl.multiple_of(t * tile, tile), tile)
+            return pltpu.make_async_copy(made.at[half, i, :, at], outs[half].at[i, :, at], out_sems.at[half, n])
+
+        for half in range(2):
+
+            def body(n, carry):
+                t, i = n // count, n % count
+
+                @pl.when(i == 0)
+                def _():
+                    arrived(rights.at[half * tiles + t], right_sems.at[half * tiles + t])
+
+                @pl.when(t == 0)
+                def _():
+                    arrived(lefts.at[half, i], left_sems.at[half, i])
+
+                at = pl.ds(pl.multiple_of(t * tile, tile), tile)
+                made[half, i, :, at] = dot_tn(lefts[half, i], rights[half * tiles + t]).astype(BF16)
+                leave(half, n).start()
+                return carry
+
+            lax.fori_loop(0, tiles * count, body, 0)
+        for half in range(2):
+            for n in range(tiles * count):
+                leave(half, n).wait()
+
+    out = (2, count, block, share)
+    return call(
+        kernel,
+        (1,),
+        [ANY] * 4,
+        [ANY] * 2,
+        [sds(out[1:], BF16)] * 2,
+        [
+            pltpu.VMEM((2, count, 2 * total, block), BF16), pltpu.VMEM((2 * tiles, 2 * total, tile), BF16),
+            pltpu.VMEM(out, BF16), DMA((2, count)), DMA((2 * tiles,)), DMA((2, tiles * count)),
+        ],
+        flops=0,
+        moved=0,
+    )(meta, left, left_got, right, right_got)
+
+
+HIGH = 272
+
+
+def first_grad(meta, tokens, tokens_got, mixed, mixed_got, grads, grads_got, low, low_got, vec, vec_got, codes):
+    total, width = tokens.shape
+    count = len(codes[0])
+
+    def kernel(meta, x_ref, x_got, mixed_ref, mixed_got, g_ref, g_got, low_ref, low_got, vec_ref, vec_got, *refs):
+        outs = refs[:2]
+        lefts, rights, made, short, left_sems, right_sems, out_sems, short_sems = refs[2:]
+        own, got = pl.ds(0, total), pl.ds(total, total)
+
+        def left_copy(half, kind, i):
+            code = codes[half][i]
+            at = pl.ds(pl.multiple_of((meta[0] ^ code) * 128, 128), 128)
+            slot, sem = half + kind, left_sems.at[half + kind, i]
+            source, other = ((x_ref, x_got), (mixed_ref, mixed_got))[kind]
+            pltpu.make_async_copy(source.at[:, at], lefts.at[slot, i, own], sem).start()
+            pltpu.make_async_copy(other.at[code // 2], lefts.at[slot, i, got], sem).start()
+
+        for half in range(2):
+            for w in (2 * half, 2 * half + 1):
+                source, other = (g_ref.at[w], g_got.at[w]) if w < 3 else (low_ref, low_got)
+                pltpu.make_async_copy(source, rights.at[w, own], right_sems.at[w]).start()
+                pltpu.make_async_copy(other, rights.at[w, got], right_sems.at[w]).start()
+            for i in range(count):
+                left_copy(half, 0, i)
+                if half == 1:
+                    left_copy(half, 1, i)
+                    at = meta[0] ^ codes[1][i]
+                    pltpu.make_async_copy(vec_ref.at[at], short.at[i, 0], short_sems.at[i]).start()
+                    pltpu.make_async_copy(vec_got.at[at], short.at[i, 1], short_sems.at[i]).start()
+        for half in range(2):
+
+            def body(i, carry):
+                for k in range(2):
+                    w = 2 * half + k
+                    kind = 1 if w == 3 else 0
+                    if kind == 1 or k == 0:
+                        arrived(lefts.at[half + kind, i], left_sems.at[half + kind, i])
+
+                    @pl.when(i == 0)
+                    def _():
+                        arrived(rights.at[w], right_sems.at[w])
+
+                    part = dot_tn(lefts[half + kind, i], rights[w])
+                    made[half, i, 128 * k : 128 * (k + 1)] = part.astype(BF16)
+                if half == 0:
+                    made[half, i, 256:] = jnp.zeros((16, width), BF16)
+                else:
+                    arrived(short.at[i], short_sems.at[i])
+                    made[half, i, 256:] = (short[i, 0].astype(F32) + short[i, 1].astype(F32)).astype(BF16)
+                pltpu.make_async_copy(made.at[half, i], outs[half].at[i], out_sems.at[half, i]).start()
+                return carry
+
+            lax.fori_loop(0, count, body, 0)
+        for half in range(2):
+            for i in range(count):
+                pltpu.make_async_copy(made.at[half, i], outs[half].at[i], out_sems.at[half, i]).wait()
+
+    out = (2, count, HIGH, width)
+    return call(
+        kernel,
+        (1,),
+        [ANY] * 10,
+        [ANY] * 2,
+        [sds(out[1:], BF16)] * 2,
+        [
+            pltpu.VMEM((3, count, 2 * total, 128), BF16), pltpu.VMEM((4, 2 * total, width), BF16),
+            pltpu.VMEM(out, BF16), pltpu.VMEM((count, 2, 16, width), BF16),
+            DMA((3, count)), DMA((4,)), DMA((2, count)), DMA((count,)),
+        ],
+        flops=0,
+        moved=0,
+    )(meta, tokens, tokens_got, mixed, mixed_got, grads, grads_got, low, low_got, vec, vec_got)
+
+
+def pack(weights, small):
+    block, width = weights[0].shape
+    high = block * len(weights) + 16
+
+    def kernel(*refs):
+        out_ref = refs[-1]
+        for i in range(len(weights)):
+            out_ref[block * i : block * (i + 1)] = refs[i][...]
+        out_ref[block * len(weights) :] = jnp.zeros((16, width), BF16)
+        start = 0
+        for ref in refs[len(weights) : -1]:
+            count = ref.shape[1]
+            row, column = block * len(weights) + start // width, start % width
+            out_ref[row : row + 1, column : column + count] = ref[...]
+            start += count
+
+    return pl.pallas_call(
+        kernel,
+        out_shape=jax.ShapeDtypeStruct((high, width), BF16),
+        compiler_params=pltpu.CompilerParams(vmem_limit_bytes=VMEM),
+        cost_estimate=pl.CostEstimate(flops=1024, bytes_accessed=1024, transcendentals=0),
+    )(*weights, *[part.reshape(1, -1) for part in small])
+
+
+CORE, ALONG_X, ALONG_Y = 1, 2, 4
+
+
+def swap(value, mask):
+    return lax.ppermute(value, "shard", [(i, i ^ mask) for i in range(8)])
+
+
+def plus(*parts):
+    total = parts[0].astype(F32)
+    for part in parts[1:]:
+        total = total + part.astype(F32)
+    return total.astype(BF16)
+
+
+class Order:
+    def __init__(self, meta):
+        self.meta = meta
+
+    def place(self, *values):
+        return lax.optimization_barrier(values + (self.meta,))[:-1]
+
+    def then(self, value):
+        self.meta, value = lax.optimization_barrier((self.meta, value))
+        return value
+
+    def run(self, function, *values):
+        return self.then(function(*self.place(*values)))
+
+
+def late(value, *before):
+    return lax.optimization_barrier((value,) + before)[0]
+
+
+def both_cores(*mine):
+    return mine + tuple(swap(part, CORE) for part in mine)
+
+
+class Reduction:
+    def __init__(self, order):
+        self.order = order
+        self.odd = lax.axis_index("rep") % 2 == 1
+
+    def send(self, far):
+        self.got = swap(far[0], ALONG_Y), swap(far[1], ALONG_X)
+
+    def keep(self, near):
+        self.near = near
+
+    def turn(self):
+        def add(near_a, near_b, got_a, got_b):
+            return plus(near_a[1], got_a[1]), plus(near_b[1], got_b[1])
+
+        passed = self.order.run(add, *self.near, *self.got)
+        self.passed = swap(passed[0], ALONG_X), swap(passed[1], ALONG_Y)
+
+    def pair(self):
+        def add(near_a, near_b, got_a, got_b, passed_a, passed_b):
+            first, second = plus(near_a[0], got_a[0], passed_a), plus(near_b[0], got_b[0], passed_b)
+            return jnp.where(self.odd, second, first), jnp.where(self.odd, first, second)
+
+        self.kept, given = self.order.run(add, *self.near, *self.got, *self.passed)
+        self.taken = lax.ppermute(given, "rep", [(i, i ^ 1) for i in range(4)])
+
+    def across(self):
+        self.half = self.order.run(plus, self.kept, self.taken)
+        self.over = lax.ppermute(self.half, "rep", [(i, i ^ 2) for i in range(4)])
+
+    def back(self):
+        self.total = self.order.run(plus, self.half, self.over)
+        self.other = lax.ppermute(self.total, "rep", [(i, i ^ 1) for i in range(4)])
+
+    def done(self, axis):
+        first = jnp.where(self.odd, self.other, self.total).astype(F32)
+        second = jnp.where(self.odd, self.total, self.other).astype(F32)
+        return jnp.concatenate([first, second], axis) if axis is not None else (first, second)
+
+
+def local_eight(
+    inputs, lengths, dealing, w_query, w_key, w_value, w_out, b_query, b_value, b_out,
+    ln1_gain, ln1_bias, w_up, b_up, w_down, b_down, ln2_gain, ln2_bias, cotangent,
+):
+    batches, rows, width = inputs.shape
+    wide = w_up.shape[1]
+    total = batches * rows
+    group = batches * 4
+    shard_index = lax.axis_index("shard")
+    anchor = shard_index * group
+    slots = anchor + lax.axis_index("rep") * batches + jnp.arange(batches, dtype=jnp.int32)
+    local_dealing = lax.dynamic_slice_in_dim(dealing, anchor, group) - anchor
+    sources = jnp.take(dealing, slots) - anchor
+    places = jnp.arange(group, dtype=jnp.int32)
+    wanted = jnp.sum(
+        jnp.where(local_dealing[None, :] == (slots - anchor)[:, None], places[None, :], 0), 1
+    )
+    meta = jnp.concatenate([shard_index[None].astype(jnp.int32), jnp.take(lengths, slots), wanted])
+    order = Order(meta)
+    tokens = inputs.reshape(total, width)
+
+    small = (b_query, b_value, b_out, ln1_gain, ln1_bias, b_down, ln2_gain, ln2_bias, b_up)
+    own_first = pack((w_query, w_key, w_value, w_out), small)
+    first_x, first_y = swap(own_first, ALONG_X), swap(own_first, ALONG_Y)
+    first_far = swap(first_x, ALONG_Y)
+    up_x = swap(late(w_up, first_x), ALONG_X)
+    up_y = swap(late(w_up, first_far), ALONG_Y)
+    down_x = swap(late(w_down, up_x), ALONG_X)
+    first = both_cores(own_first, first_x, first_y, first_far)
+    cot_pool = lax.all_gather(cotangent, "rep", axis=0, tiled=True)
+
+    qkv, vecs, bias_up, tokens_give = order.then(project(order.meta, tokens, first))
+    tokens_got = swap(tokens_give, CORE)
+    mixed, probs = order.then(attend(order.meta, qkv, batches, rows))
+    (up_y,) = order.then(order.place(up_y))
+    up_far = swap(up_y, ALONG_X)
+    down_y = swap(late(w_down, up_y), ALONG_Y)
+    unit_one, inverse_one, hidden_low, both_give = order.then(mix_out(order.meta, mixed, tokens, first, vecs))
+    (down_x,) = order.then(order.place(down_x))
+    down_top = swap(down_x[:256], ALONG_Y)
+    (up_far,) = order.place(up_far)
+    up = both_cores(w_up, up_x, up_y, up_far)
+    act, slope, act_give = order.then(feed_up(order.meta, hidden_low, up, bias_up))
+    (down_y,) = order.then(order.place(down_y))
+    down_end = swap(down_y[256:], ALONG_X)
+    down = both_cores(w_down, down_x, down_y, down_top, down_end)
+    both_got, act_got = swap(both_give, CORE), swap(act_give, CORE)
+    tokens_got, both_got, act_got = order.then((tokens_got, both_got, act_got))
+    mixed_got, hidden_got = both_got[0], both_got[1]
+    out, grad_sum, sum_low, grads_two = order.then(
+        feed_down(order.meta, act, down, unit_one, cot_pool, vecs, batches, rows)
+    )
+    sum_got = order.then(swap(sum_low, CORE))
+    out_pool = lax.all_gather(out.reshape(batches, rows, width), "rep", axis=0, tiled=True)
+    far, near = [[4, 6], [2, 6]], [[0, 2], [0, 4]]
+    of_down, of_up, of_first = Reduction(order), Reduction(order), Reduction(order)
+
+    def down_grad(codes):
+        return order.then(weight_grad(order.meta, act, act_got, sum_low, sum_got, codes, 512))
+
+    def up_grad(codes):
+        return order.then(weight_grad(order.meta, hidden_low, hidden_got, pre, pre_got, codes, 128))
+
+    def attn_grad(codes):
+        return order.then(
+            first_grad(
+                order.meta, tokens, tokens_got, mixed, mixed_got, grads, grads_got, resid_low, resid_got, vec, vec_got,
+                codes,
+            )
+        )
+
+    of_down.send(down_grad(far))
+    pre, grad_bias_up = order.then(back_down(order.meta, sum_low, down, slope))
+    pre_got = swap(pre, CORE)
+    of_down.keep(down_grad(near))
+    of_up.send(up_grad(far))
+    grad_resid, resid_low, grad_mixed, grads_one = order.then(
+        back_up(order.meta, pre, up, first, grad_sum, unit_one, inverse_one, vecs)
+    )
+    of_down.turn()
+    resid_got = swap(resid_low, CORE)
+    of_up.keep(up_grad(near))
+    grads, grads_bias = order.then(attend_back(order.meta, qkv, probs, grad_mixed, batches, rows))
+    (out_pool,) = order.then(order.place(out_pool))
+    of_down.pair()
+    of_up.turn()
+    grads_got = swap(grads, CORE)
+    grads_bias = jnp.sum(grads_bias, 0)
+    rows_of = (
+        grads_bias[0], grads_bias[2], grads_one[2], grads_one[0], grads_one[1],
+        grads_two[2], grads_two[0], grads_two[1],
+    )
+    vec = jnp.concatenate(
+        [jnp.stack(rows_of).reshape(8, 8, 128).transpose(1, 0, 2).reshape(8, width), grad_bias_up.reshape(8, 512)], 1
+    )
+    vec = jnp.pad(vec, ((0, 0), (0, 16 * width - vec.shape[1]))).reshape(8, 16, width).astype(BF16)
+    vec_got = swap(vec, CORE)
+    grad_input = order.then(back_project(order.meta, grads, first, grad_resid))
+    of_down.across()
+    of_first.send(attn_grad(far))
+    of_up.pair()
+    of_first.keep(attn_grad(near))
+    of_down.back()
+    of_up.across()
+    of_first.turn()
+    of_up.back()
+    of_first.pair()
+    g_down = order.run(lambda *_: of_down.done(1))
+    of_first.across()
+    g_up = order.run(lambda *_: of_up.done(1))
+    of_first.back()
+    top, end = of_first.done(None)
+    layer_out = pick(out_pool, sources)
+    g_vec = end[256:258].reshape(-1)
+    line = lambda i: g_vec[128 * i : 128 * (i + 1)]
+    return (
+        layer_out, grad_input.reshape(batches, rows, width),
+        top[0:128], top[128:256], end[0:128], end[128:256],
+        line(0), line(1), line(2), line(3), line(4),
+        g_up, g_vec[1024:1536], g_down, line(5), line(6), line(7),
+    )
+
+
 def pick(pool, targets):
     return jnp.stack(
         [lax.dynamic_index_in_dim(pool, targets[i], 0, keepdims=False) for i in range(targets.shape[0])]
     )
 
 
-def local(
+def local_general(
     inputs, lengths, dealing, w_query, w_key, w_value, w_out, b_query, b_value, b_out,
     ln1_gain, ln1_bias, w_up, b_up, w_down, b_down, ln2_gain, ln2_bias, cotangent,
 ):
@@ -202,4 +1149,6 @@
     out_specs = (
         seqs, seqs, mat, mat, mat, mat, vec, vec, vec, vec, vec, mat, vec, mat, vec, vec, vec,
     )
+    shape = dict(mesh.shape)
+    local = local_eight if shape["shard"] == 8 and shape["rep"] == 4 else local_general
     return jax.shard_map(local, mesh=mesh, in_specs=in_specs, out_specs=out_specs, check_vma=False)

time: 794 us -> 450 us (0.57)
  waiting for transfers between devices: 530 us -> 179 us
  Pallas kernels: 0 us -> 167 us
  matrix products: 123 us -> 0 us
  blocking collectives: 53.8 us -> 0 us
  starting transfers between devices: 0.36 us -> 45.3 us
  local copies, waits for them, and re-layouts: 40.2 us -> 17.2 us
    all_gather x5 -> x2, waiting for transfers between devices: 213 us -> 0.02 us  [the longest x1 0.02 us: local_eight(): lax.all_gather(out.reshape(batches, rows, width), 'rep', axis=0, tiled=True)]
    reduce_scatter x3 -> x0, waiting for transfers between devices: 194 us -> none  [reduced(): return lax.psum_scatter(part, 'shard', scatter_dimension=0, tiled=True)]
    ppermute x0 -> x52, waiting for transfers between devices: none -> 179 us  [the longest x43 109 us: swap(): return lax.ppermute(value, 'shard', [(i, i ^ mask) for i in range(8)])]
    pallas_call x0 -> x16, Pallas kernels: none -> 167 us  [the longest x4 27.6 us: weight_grad(): call(kernel, (1,), [ANY] * 4, [ANY] * 2, [sds(out[1:], BF16)] * 2, [pltpu...]
    dot_general x24 -> x0, matrix products: 123 us -> none  [the longest x6 31.3 us: matmul(): return jnp.dot(left, right, preferred_element_type=F32)]
    psum x1 -> x0, waiting for transfers between devices: 121 us -> none  [over_rep(): return lax.psum(part, 'rep').astype(F32)]
    ppermute x0 -> x52, starting transfers between devices: none -> 45.2 us  [the longest x43 33.3 us: swap(): return lax.ppermute(value, 'shard', [(i, i ^ mask) for i in range(8)])]
    psum x1 -> x0, blocking collectives: 43.1 us -> none  [local(): g_vec = lax.psum(g_vec, ('shard', 'rep'))]
  transfers between devices with their start and end apart: 9 -> 54, of which waited for: 9 -> 22; matrix products, arithmetic and copies ran while one was open for 10% -> 6% of each run, Pallas kernels for 0% -> 33%
where the time goes in v2:
time: 450 us; the launch traced here: 449 us
  waiting for transfers between devices  179 us (40%)
  Pallas kernels  167 us (37%)
  starting transfers between devices  45.3 us (10%)
  other arithmetic  21.9 us (5%)
  between operations  18.7 us (4%)
  local copies, waits for them, and re-layouts  17.2 us (4%)
    ppermute x43, waiting for transfers between devices, swap(): return lax.ppermute(value, 'shard', [(i, i ^ mask) for i in range(8)])  109 us
    ppermute x43, starting transfers between devices, swap(): return lax.ppermute(value, 'shard', [(i, i ^ mask) for i in range(8)])  33.3 us
    pallas_call x4, Pallas kernels, weight_grad(): call(kernel, (1,), [ANY] * 4, [ANY] * 2, [sds(out[1:], BF16)] * 2, [pltpu...  27.6 us
    ppermute x3, waiting for transfers between devices, across(): self.over = lax.ppermute(self.half, 'rep', [(i, i ^ 2) for i in range(4)])  24.7 us
    ppermute x3, waiting for transfers between devices, pair(): self.taken = lax.ppermute(given, 'rep', [(i, i ^ 1) for i in range(4)])  22.9 us
    ppermute x3, waiting for transfers between devices, back(): self.other = lax.ppermute(self.total, 'rep', [(i, i ^ 1) for i in range(4)])  22.6 us
    pallas_call x1, Pallas kernels, feed_up(): call(kernel, (1,), [whole((total, width)), whole((1, wide))] + [ANY] * le...  17.7 us
    pallas_call x1, Pallas kernels, back_up(): call(kernel, (1,), [whole((total, wide)), ANY, ANY, whole((total, 128)),...  16.7 us
  transfers between devices with their start and end apart: 54, of which 22 were waited for; matrix products, arithmetic and copies ran while one was open for 6% of the time, Pallas kernels for 33%

profile of v2, /device:TPU:0, one launch (start us, length us, event | category | flops | bytes accessed | tf_op | source)
XLA Modules:
  0.0 448.8 jit_solution(13513474734435866753)
XLA Ops:
  10.8 2.9 collective-permute-start
  15.3 22.5 %collective-permute-done.refs_1_.refs_9_ = bf16[528,1024]{1,0:T(8,128)(2,1)S(1)} collective-permute-done((bf16[528,1024]{1,0:T(8,128)(2,1)}, bf16[528,1024]{1,0:T(8,128)(2,1)S(1)}, u32[]{:S(2)}, u32[]{:S(2)}) %collective-permute-start) | collective-permute-done | bytes 1081376 | tf_op jit(solution)/shard_map/ppermute | solution.py:799
  41.9 21.0 %collective-permute-done.2.refs_3_.refs_11_ = bf16[528,1024]{1,0:T(8,128)(2,1)S(1)} collective-permute-done((bf16[528,1024]{1,0:T(8,128)(2,1)S(1)}, bf16[528,1024]{1,0:T(8,128)(2,1)S(1)}, u32[]{:S(2)}, u32[]{:S(2)}) %collective-permute-start.2) | collective-permute-done | bytes 1081376 | tf_op jit(solution)/shard_map/ppermute | solution.py:799
  68.1 11.2 %shard_map.315 = (bf16[3,512,1024]{2,1,0:T(8,128)(2,1)}, f32[8,1024]{1,0:T(8,128)}, f32[1,4096]{1,0:T(1,128)}, bf16[4,512,128]{2,1,0:T(8,128)(2,1)}) custom-call(s32[5]{0:T(128)} %pad_add_fusion.meta, bf16[512,1024]{1,0:T(8,128)(2,1)} %bitcast.94, bf16[528,1024]{1,0:T(8,128)(2,1)} %shard_map.314.refs_0_.refs_8_, bf16[528,1024]{1,0:T(8,128)(2,1)} %copy-done.3, ...), custom_call_target="tpu_custom_call" | custom-call | flops 1024 | bytes 1024 | tf_op jit(solution)/shard_map/pallas_call | solution.py:191
  79.3 11.6 %shard_map.316 = (bf16[512,1024]{1,0:T(8,128)(2,1)}, bf16[2,16,256,256]{3,2,1,0:T(8,128)(2,1)}) custom-call(s32[5]{0:T(128)} %pad_add_fusion.meta, bf16[3,512,1024]{2,1,0:T(8,128)(2,1)} %get-tuple-element.211.q_ref.k_ref.v_ref, bf16[3,512,1024]{2,1,0:T(8,128)(2,1)} %get-tuple-element.211.q_ref.k_ref.v_ref, ...), custom_call_target="tpu_custom_call" | custom-call | flops 1024 | bytes 1024 | tf_op jit(solution)/shard_map/pallas_call | solution.py:234
  92.1 9.4 %shard_map.317 = (f32[512,1024]{1,0:T(8,128)}, f32[512,128]{1,0:T(8,128)}, bf16[512,1024]{1,0:T(8,128)(2,1)}, bf16[2,4,512,128]{3,2,1,0:T(8,128)(2,1)}) custom-call(s32[5]{0:T(128)} %pad_add_fusion.meta, bf16[512,1024]{1,0:T(8,128)(2,1)} %get-tuple-element.218.mixed_ref, bf16[512,1024]{1,0:T(8,128)(2,1)} %bitcast.95, f32[8,1024]{1,0:T(8,128)} %get-tuple-element.219.vec_ref, ...), custom_call_target="tpu_custom_call" | custom-call | flops 1024 | bytes 1024 | tf_op jit(solution)/shard_map/pallas_call | solution.py:276
  101.5 14.7 %collective-permute-done.10.refs_3_ = bf16[128,4096]{1,0:T(8,128)(2,1)S(1)} collective-permute-done((bf16[128,4096]{1,0:T(8,128)(2,1)}, bf16[128,4096]{1,0:T(8,128)(2,1)S(1)}, u32[]{:S(2)}, u32[]{:S(2)}) %collective-permute-start.10) | collective-permute-done | bytes 1048608 | tf_op jit(solution)/shard_map/ppermute | solution.py:799
  116.3 2.6 collective-permute-done.14.refs_7_
  119.9 17.7 %shard_map.318 = (bf16[512,4096]{1,0:T(8,128)(2,1)}, bf16[512,4096]{1,0:T(8,128)(2,1)}, bf16[4,512,512]{2,1,0:T(8,128)(2,1)}) custom-call(s32[5]{0:T(128)} %pad_add_fusion.meta, bf16[512,1024]{1,0:T(8,128)(2,1)} %get-tuple-element.229.x_ref.left_ref, f32[1,4096]{1,0:T(1,128)} %get-tuple-element.230.bias_ref, bf16[128,4096]{1,0:T(8,128)(2,1)} %refs_0_.9, ...), custom_call_target="tpu_custom_call" | custom-call | flops 1024 | bytes 1024 | tf_op jit(solution)/shard_map/pallas_call | solution.py:338
  140.3 23.5 %collective-permute-done.15.refs_2_ = bf16[512,1024]{1,0:T(8,128)(2,1)S(1)} collective-permute-done((bf16[512,1024]{1,0:T(8,128)(2,1)}, bf16[512,1024]{1,0:T(8,128)(2,1)S(1)}, u32[]{:S(2)}, u32[]{:S(2)}) %collective-permute-start.15) | collective-permute-done | bytes 1048608 | tf_op jit(solution)/shard_map/ppermute | solution.py:799
  164.5 10.1 %collective-permute-done.19.refs_3_ = bf16[256,1024]{1,0:T(8,128)(2,1)S(1)} collective-permute-done((bf16[256,1024]{1,0:T(8,128)(2,1)S(1)}, bf16[256,1024]{1,0:T(8,128)(2,1)S(1)}, u32[]{:S(2)}, u32[]{:S(2)}) %collective-permute-start.19) | collective-permute-done | bytes 524320 | tf_op jit(solution)/shard_map/ppermute | solution.py:799
  175.7 2.8 collective-permute-done.20.refs_4_
  181.5 16.1 %shard_map.319 = (bf16[512,1024]{1,0:T(8,128)(2,1)}, f32[512,1024]{1,0:T(8,128)}, bf16[512,1024]{1,0:T(8,128)(2,1)}, f32[8,1024]{1,0:T(8,128)}) custom-call(s32[5]{0:T(128)} %pad_add_fusion.meta, bf16[512,4096]{1,0:T(8,128)(2,1)} %get-tuple-element.244.act_ref.left_ref, f32[512,1024]{1,0:T(8,128)} %get-tuple-element.245.unit_ref, ...), custom_call_target="tpu_custom_call" | custom-call | flops 1024 | bytes 1024 | tf_op jit(solution)/shard_map/pallas_call | solution.py:411
  202.1 6.5 %shard_map.320 = (bf16[2,512,512]{2,1,0:T(8,128)(2,1)}, bf16[2,512,512]{2,1,0:T(8,128)(2,1)}) custom-call(s32[5]{0:T(128)} %pad_add_fusion.meta, bf16[512,4096]{1,0:T(8,128)(2,1)} %get-tuple-element.244.act_ref.left_ref, bf16[4,512,512]{2,1,0:T(8,128)(2,1)} %copy-done.8, bf16[512,1024]{1,0:T(8,128)(2,1)} %get-tuple-element.253.right_ref.low_ref, ...), custom_call_target="tpu_custom_call" | custom-call | flops 1024 | bytes 1024 | tf_op jit(solution)/shard_map/pallas_call | solution.py:679
  208.6 12.2 %shard_map.321 = (bf16[512,4096]{1,0:T(8,128)(2,1)}, f32[1,4096]{1,0:T(1,128)}) custom-call(s32[5]{0:T(128)} %pad_add_fusion.meta, bf16[512,1024]{1,0:T(8,128)(2,1)} %get-tuple-element.253.right_ref.low_ref, bf16[512,4096]{1,0:T(8,128)(2,1)} %get-tuple-element.260.slope_ref, bf16[512,1024]{1,0:T(8,128)(2,1)} %refs_0_.8, bf16[512,1024]{1,0:T(8,128)(2,1)} %copy-done.9, ...), custom_call_target="tpu_custom_call" | custom-call | flops 1024 | bytes 1024 | tf_op jit(solution)/shard_map/pallas_call | solution.py:453
  224.4 2.6 collective-permute-start.29
  228.0 6.5 %shard_map.322 = (bf16[2,512,512]{2,1,0:T(8,128)(2,1)}, bf16[2,512,512]{2,1,0:T(8,128)(2,1)}) custom-call(s32[5]{0:T(128)} %pad_add_fusion.meta, bf16[512,4096]{1,0:T(8,128)(2,1)} %get-tuple-element.244.act_ref.left_ref, bf16[4,512,512]{2,1,0:T(8,128)(2,1)} %copy-done.8, bf16[512,1024]{1,0:T(8,128)(2,1)} %get-tuple-element.253.right_ref.low_ref, ...), custom_call_target="tpu_custom_call" | custom-call | flops 1024 | bytes 1024 | tf_op jit(solution)/shard_map/pallas_call | solution.py:679
  236.5 7.1 %shard_map.323 = (bf16[2,128,2048]{2,1,0:T(8,128)(2,1)}, bf16[2,128,2048]{2,1,0:T(8,128)(2,1)}) custom-call(s32[5]{0:T(128)} %pad_add_fusion.meta, bf16[512,1024]{1,0:T(8,128)(2,1)} %get-tuple-element.229.x_ref.left_ref, bf16[4,512,128]{2,1,0:T(8,128)(2,1)} %get-tuple-element.413.left_got_ref, bf16[512,4096]{1,0:T(8,128)(2,1)} %get-tuple-element.268.right_ref.pre_ref, ...), custom_call_target="tpu_custom_call" | custom-call | flops 1024 | bytes 1024 | tf_op jit(solution)/shard_map/pallas_call | solution.py:679
  243.6 16.7 %shard_map.324 = (f32[512,1024]{1,0:T(8,128)}, bf16[512,1024]{1,0:T(8,128)(2,1)}, bf16[512,1024]{1,0:T(8,128)(2,1)}, f32[8,1024]{1,0:T(8,128)}) custom-call(s32[5]{0:T(128)} %pad_add_fusion.meta, bf16[512,4096]{1,0:T(8,128)(2,1)} %get-tuple-element.268.right_ref.pre_ref, f32[512,1024]{1,0:T(8,128)} %get-tuple-element.272.sum_ref, ...), custom_call_target="tpu_custom_call" | custom-call | flops 1024 | bytes 1024 | tf_op jit(solution)/shard_map/pallas_call | solution.py:520
  266.5 7.5 %shard_map.325 = (bf16[2,128,2048]{2,1,0:T(8,128)(2,1)}, bf16[2,128,2048]{2,1,0:T(8,128)(2,1)}) custom-call(s32[5]{0:T(128)} %pad_add_fusion.meta, bf16[512,1024]{1,0:T(8,128)(2,1)} %get-tuple-element.229.x_ref.left_ref, bf16[4,512,128]{2,1,0:T(8,128)(2,1)} %get-tuple-element.413.left_got_ref, bf16[512,4096]{1,0:T(8,128)(2,1)} %get-tuple-element.268.right_ref.pre_ref, ...), custom_call_target="tpu_custom_call" | custom-call | flops 1024 | bytes 1024 | tf_op jit(solution)/shard_map/pallas_call | solution.py:679
  274.0 16.6 %shard_map.326 = (bf16[3,512,1024]{2,1,0:T(8,128)(2,1)}, f32[2,8,1024]{2,1,0:T(8,128)}) custom-call(s32[5]{0:T(128)} %pad_add_fusion.meta, bf16[3,512,1024]{2,1,0:T(8,128)(2,1)} %get-tuple-element.211.q_ref.k_ref.v_ref, bf16[3,512,1024]{2,1,0:T(8,128)(2,1)} %get-tuple-element.211.q_ref.k_ref.v_ref, ...), custom_call_target="tpu_custom_call" | custom-call | flops 1024 | bytes 1024 | tf_op jit(solution)/shard_map/pallas_call | solution.py:561
  291.8 5.7 %collective-permute-done.30 = bf16[512,512]{1,0:T(8,128)(2,1)} collective-permute-done((bf16[512,512]{1,0:T(8,128)(2,1)}, bf16[512,512]{1,0:T(8,128)(2,1)}, u32[]{:S(2)}, u32[]{:S(2)}) %collective-permute-start.30) | collective-permute-done | bytes 524320 | tf_op jit(solution)/shard_map/ppermute | solution.py:799
  297.5 3.1 broadcast_select_fusion.8
  307.9 10.2 %shard_map.327 = bf16[512,1024]{1,0:T(8,128)(2,1)} custom-call(s32[5]{0:T(128)} %pad_add_fusion.meta, bf16[3,512,1024]{2,1,0:T(8,128)(2,1)} %get-tuple-element.318.g_ref, f32[512,1024]{1,0:T(8,128)} %get-tuple-element.319.resid_ref, bf16[528,1024]{1,0:T(8,128)(2,1)} %shard_map.314.refs_0_.refs_8_, bf16[528,1024]{1,0:T(8,128)(2,1)} %copy-done.3, ...), custom_call_target="tpu_custom_call" | custom-call | flops 1024 | bytes 1024 | tf_op jit(solution)/shard_map/pallas_call | solution.py:611
  326.2 7.6 %shard_map.328 = (bf16[2,272,1024]{2,1,0:T(8,128)(2,1)}, bf16[2,272,1024]{2,1,0:T(8,128)(2,1)}) custom-call(s32[5]{0:T(128)} %pad_add_fusion.meta, bf16[512,1024]{1,0:T(8,128)(2,1)} %bitcast.96, bf16[4,512,128]{2,1,0:T(8,128)(2,1)} %copy-done.19, bf16[512,1024]{1,0:T(8,128)(2,1)} %get-tuple-element.218.mixed_ref, ...), custom_call_target="tpu_custom_call" | custom-call | flops 1024 | bytes 1024 | tf_op jit(solution)/shard_map/pallas_call | solution.py:755
  339.3 7.6 %shard_map.329 = (bf16[2,272,1024]{2,1,0:T(8,128)(2,1)}, bf16[2,272,1024]{2,1,0:T(8,128)(2,1)}) custom-call(s32[5]{0:T(128)} %pad_add_fusion.meta, bf16[512,1024]{1,0:T(8,128)(2,1)} %bitcast.97, bf16[4,512,128]{2,1,0:T(8,128)(2,1)} %copy-done.19, bf16[512,1024]{1,0:T(8,128)(2,1)} %get-tuple-element.218.mixed_ref, ...), custom_call_target="tpu_custom_call" | custom-call | flops 1024 | bytes 1024 | tf_op jit(solution)/shard_map/pallas_call | solution.py:755
  349.3 9.8 %collective-permute-done.41 = bf16[128,2048]{1,0:T(8,128)(2,1)S(1)} collective-permute-done((bf16[128,2048]{1,0:T(8,128)(2,1)S(1)}, bf16[128,2048]{1,0:T(8,128)(2,1)S(1)}, u32[]{:S(2)}, u32[]{:S(2)}) %collective-permute-start.41) | collective-permute-done | bytes 524320 | tf_op jit(solution)/shard_map/ppermute | solution.py:856
  365.4 20.0 %collective-permute-done.44 = bf16[128,2048]{1,0:T(8,128)(2,1)S(1)} collective-permute-done((bf16[128,2048]{1,0:T(8,128)(2,1)S(1)}, bf16[128,2048]{1,0:T(8,128)(2,1)S(1)}, u32[]{:S(2)}, u32[]{:S(2)}) %collective-permute-start.44) | collective-permute-done | bytes 524320 | tf_op jit(solution)/shard_map/ppermute | solution.py:860
  390.0 11.9 %collective-permute-done.48 = bf16[272,1024]{1,0:T(8,128)(2,1)S(1)} collective-permute-done((bf16[272,1024]{1,0:T(8,128)(2,1)S(1)}, bf16[272,1024]{1,0:T(8,128)(2,1)S(1)}, u32[]{:S(2)}, u32[]{:S(2)}) %collective-permute-start.48) | collective-permute-done | bytes 557088 | tf_op jit(solution)/shard_map/ppermute | solution.py:856
  403.0 18.4 %collective-permute-done.49 = bf16[128,2048]{1,0:T(8,128)(2,1)S(1)} collective-permute-done((bf16[128,2048]{1,0:T(8,128)(2,1)S(1)}, bf16[128,2048]{1,0:T(8,128)(2,1)S(1)}, u32[]{:S(2)}, u32[]{:S(2)}) %collective-permute-start.49) | collective-permute-done | bytes 524320 | tf_op jit(solution)/shard_map/ppermute | solution.py:864
  423.0 3.6 collective-permute-done.50
  434.3 4.2 collective-permute-done.51
  (229 shorter events, 86.1 us)
Async XLA Ops:
  7.2 174.0 %all-gather.3.cloned.1.call-start = ((), (), s32[]{:S(2)}) async-start(), calls=%async_computation | async-start | bytes 5242880 | tf_op jit(solution)/shard_map/all_gather | solution.py:901
  10.8 27.0 %collective-permute-start = (bf16[528,1024]{1,0:T(8,128)(2,1)}, bf16[528,1024]{1,0:T(8,128)(2,1)S(1)}, u32[]{:S(2)}, u32[]{:S(2)}) collective-permute-start(bf16[528,1024]{1,0:T(8,128)(2,1)} %shard_map.314.refs_0_.refs_8_), channel_id=1, source_target_pairs={{0,8},{4,12},{8,0},{12,4},{16,24},{20,28},{24,16},{28,20},{1,9},{5... | collective-permute-start | bytes 3244040 | tf_op jit(solution)/shard_map/ppermute | solution.py:799
  13.8 28.0 %collective-permute-start.1 = (bf16[528,1024]{1,0:T(8,128)(2,1)}, bf16[528,1024]{1,0:T(8,128)(2,1)S(1)}, u32[]{:S(2)}, u32[]{:S(2)}) collective-permute-start(bf16[528,1024]{1,0:T(8,128)(2,1)} %shard_map.314.refs_0_.refs_8_), channel_id=1, source_target_pairs={{0,16},{4,20},{8,24},{12,28},{16,0},{20,4},{24,8},{28,12},{1,17},{... | collective-permute-start | bytes 3244040 | tf_op jit(solution)/shard_map/ppermute | solution.py:799
  37.9 25.0 %collective-permute-start.2 = (bf16[528,1024]{1,0:T(8,128)(2,1)S(1)}, bf16[528,1024]{1,0:T(8,128)(2,1)S(1)}, u32[]{:S(2)}, u32[]{:S(2)}) collective-permute-start(bf16[528,1024]{1,0:T(8,128)(2,1)S(1)} %collective-permute-done.refs_1_.refs_9_), channel_id=1, source_target_pairs={{0,16},{4,20},{8,24},{12,28},{16,0},{20,4},{24,8},{28,12},{1,17},{... | collective-permute-start | bytes 3244040 | tf_op jit(solution)/shard_map/ppermute | solution.py:799
  41.1 250.6 %all-gather.5.cloned.1.call-start = ((), (), s32[]{:S(2)}) async-start(), calls=%async_computation.1 | async-start | bytes 5242880 | tf_op jit(solution)/shard_map/all_gather | solution.py:925
  41.2 25.4 %collective-permute-start.3 = (bf16[528,1024]{1,0:T(8,128)(2,1)}, bf16[528,1024]{1,0:T(8,128)(2,1)}, u32[]{:S(2)}, u32[]{:S(2)}) collective-permute-start(bf16[528,1024]{1,0:T(8,128)(2,1)} %shard_map.314.refs_0_.refs_8_), channel_id=1, source_target_pairs={{0,4},{4,0},{8,12},{12,8},{16,20},{20,16},{24,28},{28,24},{1,5},{5... | collective-permute-start | bytes 3244040 | tf_op jit(solution)/shard_map/ppermute | solution.py:799
  41.3 26.8 %collective-permute-start.4 = (bf16[528,1024]{1,0:T(8,128)(2,1)S(1)}, bf16[528,1024]{1,0:T(8,128)(2,1)}, u32[]{:S(2)}, u32[]{:S(2)}) collective-permute-start(bf16[528,1024]{1,0:T(8,128)(2,1)S(1)} %collective-permute-done.refs_1_.refs_9_), channel_id=1, source_target_pairs={{0,4},{4,0},{8,12},{12,8},{16,20},{20,16},{24,28},{28,24},{1,5},{5... | collective-permute-start | bytes 3244040 | tf_op jit(solution)/shard_map/ppermute | solution.py:799
  41.8 26.3 %collective-permute-start.5 = (bf16[528,1024]{1,0:T(8,128)(2,1)S(1)}, bf16[528,1024]{1,0:T(8,128)(2,1)}, u32[]{:S(2)}, u32[]{:S(2)}) collective-permute-start(bf16[528,1024]{1,0:T(8,128)(2,1)S(1)} %collective-permute-done.1.refs_2_.refs_10_), channel_id=1, source_target_pairs={{0,4},{4,0},{8,12},{12,8},{16,20},{20,16},{24,28},{28,24},{1,5},{5... | collective-permute-start | bytes 3244040 | tf_op jit(solution)/shard_map/ppermute | solution.py:799
  63.7 27.3 %collective-permute-start.7 = (bf16[128,4096]{1,0:T(8,128)(2,1)}, bf16[128,4096]{1,0:T(8,128)(2,1)}, u32[]{:S(2)}, u32[]{:S(2)}) collective-permute-start(bf16[128,4096]{1,0:T(8,128)(2,1)} %refs_0_.9), channel_id=1, source_target_pairs={{0,16},{4,20},{8,24},{12,28},{16,0},{20,4},{24,8},{28,12},{1,17},{... | collective-permute-start | bytes 3145736 | tf_op jit(solution)/shard_map/ppermute | solution.py:799
  66.6 34.9 %collective-permute-start.9 = (bf16[512,1024]{1,0:T(8,128)(2,1)}, bf16[512,1024]{1,0:T(8,128)(2,1)S(1)}, u32[]{:S(2)}, u32[]{:S(2)}) collective-permute-start(bf16[512,1024]{1,0:T(8,128)(2,1)} %refs_0_.8), channel_id=1, source_target_pairs={{0,8},{4,12},{8,0},{12,4},{16,24},{20,28},{24,16},{28,20},{1,9},{5... | collective-permute-start | bytes 3145736 | tf_op jit(solution)/shard_map/ppermute | solution.py:799
  91.0 25.2 %collective-permute-start.10 = (bf16[128,4096]{1,0:T(8,128)(2,1)}, bf16[128,4096]{1,0:T(8,128)(2,1)S(1)}, u32[]{:S(2)}, u32[]{:S(2)}) collective-permute-start(bf16[128,4096]{1,0:T(8,128)(2,1)} %collective-permute-done.7.refs_2_), channel_id=1, source_target_pairs={{0,8},{4,12},{8,0},{12,4},{16,24},{20,28},{24,16},{28,20},{1,9},{5... | collective-permute-start | bytes 3145736 | tf_op jit(solution)/shard_map/ppermute | solution.py:799
  91.6 24.7 %collective-permute-start.12 = (bf16[128,4096]{1,0:T(8,128)(2,1)}, bf16[128,4096]{1,0:T(8,128)(2,1)S(1)}, u32[]{:S(2)}, u32[]{:S(2)}) collective-permute-start(bf16[128,4096]{1,0:T(8,128)(2,1)} %collective-permute-done.8.refs_1_), channel_id=1, source_target_pairs={{0,4},{4,0},{8,12},{12,8},{16,20},{20,16},{24,28},{28,24},{1,5},{5... | collective-permute-start | bytes 3145736 | tf_op jit(solution)/shard_map/ppermute | solution.py:799
  137.6 40.9 %collective-permute-start.18 = (bf16[4,512,512]{2,1,0:T(8,128)(2,1)}, bf16[4,512,512]{2,1,0:T(8,128)(2,1)S(1)}, u32[]{:S(2)}, u32[]{:S(2)}) collective-permute-start(bf16[4,512,512]{2,1,0:T(8,128)(2,1)} %get-tuple-element.242), channel_id=1, source_target_pairs={{0,4},{4,0},{8,12},{12,8},{16,20},{20,16},{24,28},{28,24},{1,5},{5... | collective-permute-start | bytes 6291464 | tf_op jit(solution)/shard_map/ppermute | solution.py:799
  137.7 26.2 %collective-permute-start.15 = (bf16[512,1024]{1,0:T(8,128)(2,1)}, bf16[512,1024]{1,0:T(8,128)(2,1)S(1)}, u32[]{:S(2)}, u32[]{:S(2)}) collective-permute-start(bf16[512,1024]{1,0:T(8,128)(2,1)} %refs_0_.8), channel_id=1, source_target_pairs={{0,16},{4,20},{8,24},{12,28},{16,0},{20,4},{24,8},{28,12},{1,17},{... | collective-permute-start | bytes 3145736 | tf_op jit(solution)/shard_map/ppermute | solution.py:799
  138.2 36.5 %collective-permute-start.17 = (bf16[2,4,512,128]{3,2,1,0:T(8,128)(2,1)}, bf16[2,4,512,128]{3,2,1,0:T(8,128)(2,1)S(1)}, u32[]{:S(2)}, u32[]{:S(2)}) collective-permute-start(bf16[2,4,512,128]{3,2,1,0:T(8,128)(2,1)} %get-tuple-element.241), channel_id=1, source_target_pairs={{0,4},{4,0},{8,12},{12,8},{16,20},{20,16},{24,28},{28,24},{1,5},{5... | collective-permute-start | bytes 3145736 | tf_op jit(solution)/shard_map/ppermute | solution.py:799
  138.4 25.5 %collective-permute-start.16 = (bf16[4,512,128]{2,1,0:T(8,128)(2,1)}, bf16[4,512,128]{2,1,0:T(8,128)(2,1)S(1)}, u32[]{:S(2)}, u32[]{:S(2)}) collective-permute-start(bf16[4,512,128]{2,1,0:T(8,128)(2,1)} %get-tuple-element.240), channel_id=1, source_target_pairs={{0,4},{4,0},{8,12},{12,8},{16,20},{20,16},{24,28},{28,24},{1,5},{5... | collective-permute-start | bytes 1572872 | tf_op jit(solution)/shard_map/ppermute | solution.py:799
  138.8 35.9 %collective-permute-start.19 = (bf16[256,1024]{1,0:T(8,128)(2,1)S(1)}, bf16[256,1024]{1,0:T(8,128)(2,1)S(1)}, u32[]{:S(2)}, u32[]{:S(2)}) collective-permute-start(bf16[256,1024]{1,0:T(8,128)(2,1)S(1)} %slice.160), channel_id=1, source_target_pairs={{0,16},{4,20},{8,24},{12,28},{16,0},{20,4},{24,8},{28,12},{1,17},{... | collective-permute-start | bytes 1572872 | tf_op jit(solution)/shard_map/ppermute | solution.py:799
  222.1 38.2 %collective-permute-start.28 = (bf16[2,512,512]{2,1,0:T(8,128)(2,1)}, bf16[2,512,512]{2,1,0:T(8,128)(2,1)S(1)}, u32[]{:S(2)}, u32[]{:S(2)}) collective-permute-start(bf16[2,512,512]{2,1,0:T(8,128)(2,1)} %get-tuple-element.281), channel_id=1, source_target_pairs={{0,16},{4,20},{8,24},{12,28},{16,0},{20,4},{24,8},{28,12},{1,17},{... | collective-permute-start | bytes 3145736 | tf_op jit(solution)/shard_map/ppermute | solution.py:799
  224.4 36.0 %collective-permute-start.29 = (bf16[2,512,512]{2,1,0:T(8,128)(2,1)}, bf16[2,512,512]{2,1,0:T(8,128)(2,1)S(1)}, u32[]{:S(2)}, u32[]{:S(2)}) collective-permute-start(bf16[2,512,512]{2,1,0:T(8,128)(2,1)} %get-tuple-element.282), channel_id=1, source_target_pairs={{0,8},{4,12},{8,0},{12,4},{16,24},{20,28},{24,16},{28,20},{1,9},{5... | collective-permute-start | bytes 3145736 | tf_op jit(solution)/shard_map/ppermute | solution.py:799
  260.3 40.3 %collective-permute-start.32 = (bf16[2,128,2048]{2,1,0:T(8,128)(2,1)}, bf16[2,128,2048]{2,1,0:T(8,128)(2,1)}, u32[]{:S(2)}, u32[]{:S(2)}) collective-permute-start(bf16[2,128,2048]{2,1,0:T(8,128)(2,1)} %get-tuple-element.311), channel_id=1, source_target_pairs={{0,16},{4,20},{8,24},{12,28},{16,0},{20,4},{24,8},{28,12},{1,17},{... | collective-permute-start | bytes 3145736 | tf_op jit(solution)/shard_map/ppermute | solution.py:799
  261.1 39.5 %collective-permute-start.33 = (bf16[2,128,2048]{2,1,0:T(8,128)(2,1)}, bf16[2,128,2048]{2,1,0:T(8,128)(2,1)}, u32[]{:S(2)}, u32[]{:S(2)}) collective-permute-start(bf16[2,128,2048]{2,1,0:T(8,128)(2,1)} %get-tuple-element.312), channel_id=1, source_target_pairs={{0,8},{4,12},{8,0},{12,4},{16,24},{20,28},{24,16},{28,20},{1,9},{5... | collective-permute-start | bytes 3145736 | tf_op jit(solution)/shard_map/ppermute | solution.py:799
  263.5 34.0 %collective-permute-start.30 = (bf16[512,512]{1,0:T(8,128)(2,1)}, bf16[512,512]{1,0:T(8,128)(2,1)}, u32[]{:S(2)}, u32[]{:S(2)}) collective-permute-start(bf16[512,512]{1,0:T(8,128)(2,1)} %fusion.8), channel_id=1, source_target_pairs={{0,8},{4,12},{8,0},{12,4},{16,24},{20,28},{24,16},{28,20},{1,9},{5... | collective-permute-start | bytes 1572872 | tf_op jit(solution)/shard_map/ppermute | solution.py:799
  265.0 32.5 %collective-permute-start.31 = (bf16[512,512]{1,0:T(8,128)(2,1)}, bf16[512,512]{1,0:T(8,128)(2,1)}, u32[]{:S(2)}, u32[]{:S(2)}) collective-permute-start(bf16[512,512]{1,0:T(8,128)(2,1)} %fusion.9), channel_id=1, source_target_pairs={{0,16},{4,20},{8,24},{12,28},{16,0},{20,4},{24,8},{28,12},{1,17},{... | collective-permute-start | bytes 1572872 | tf_op jit(solution)/shard_map/ppermute | solution.py:799
  291.6 32.5 %collective-permute-start.35 = (bf16[3,512,1024]{2,1,0:T(8,128)(2,1)}, bf16[3,512,1024]{2,1,0:T(8,128)(2,1)S(1)}, u32[]{:S(2)}, u32[]{:S(2)}) collective-permute-start(bf16[3,512,1024]{2,1,0:T(8,128)(2,1)} %get-tuple-element.318.g_ref), channel_id=1, source_target_pairs={{0,4},{4,0},{8,12},{12,8},{16,20},{20,16},{24,28},{28,24},{1,5},{5... | collective-permute-start | bytes 9437192 | tf_op jit(solution)/shard_map/ppermute | solution.py:799
  297.5 26.7 %collective-permute-start.36 = (bf16[512,1024]{1,0:T(8,128)(2,1)}, bf16[512,1024]{1,0:T(8,128)(2,1)S(1)}, u32[]{:S(2)}, u32[]{:S(2)}) collective-permute-start(bf16[512,1024]{1,0:T(8,128)(2,1)} %get-tuple-element.328.low_ref), channel_id=1, source_target_pairs={{0,4},{4,0},{8,12},{12,8},{16,20},{20,16},{24,28},{28,24},{1,5},{5... | collective-permute-start | bytes 3145736 | tf_op jit(solution)/shard_map/ppermute | solution.py:799
  306.2 27.6 %collective-permute-start.38 = (bf16[128,2048]{1,0:T(8,128)(2,1)}, bf16[128,2048]{1,0:T(8,128)(2,1)S(1)}, u32[]{:S(2)}, u32[]{:S(2)}) collective-permute-start(bf16[128,2048]{1,0:T(8,128)(2,1)} %fusion.10), channel_id=1, source_target_pairs={{0,8},{4,12},{8,0},{12,4},{16,24},{20,28},{24,16},{28,20},{1,9},{5... | collective-permute-start | bytes 1572872 | tf_op jit(solution)/shard_map/ppermute | solution.py:799
  307.0 26.8 %collective-permute-start.39 = (bf16[128,2048]{1,0:T(8,128)(2,1)}, bf16[128,2048]{1,0:T(8,128)(2,1)}, u32[]{:S(2)}, u32[]{:S(2)}) collective-permute-start(bf16[128,2048]{1,0:T(8,128)(2,1)} %fusion.11), channel_id=1, source_target_pairs={{0,16},{4,20},{8,24},{12,28},{16,0},{20,4},{24,8},{28,12},{1,17},{... | collective-permute-start | bytes 1572872 | tf_op jit(solution)/shard_map/ppermute | solution.py:799
  321.6 26.4 %collective-permute-start.40 = (bf16[512,512]{1,0:T(8,128)(2,1)S(1)}, bf16[512,512]{1,0:T(8,128)(2,1)}, u32[]{:S(2)}, u32[]{:S(2)}) collective-permute-start(bf16[512,512]{1,0:T(8,128)(2,1)S(1)} %add_convert_fusion.7), channel_id=1, source_target_pairs={{0,2},{1,3},{2,0},{3,1},{4,6},{5,7},{6,4},{7,5},{8,10},{9,11},{10,... | collective-permute-start | bytes 1572872 | tf_op jit(solution)/shard_map/ppermute | solution.py:860
  333.8 27.0 %collective-permute-start.42 = (bf16[2,272,1024]{2,1,0:T(8,128)(2,1)}, bf16[2,272,1024]{2,1,0:T(8,128)(2,1)S(1)}, u32[]{:S(2)}, u32[]{:S(2)}) collective-permute-start(bf16[2,272,1024]{2,1,0:T(8,128)(2,1)} %get-tuple-element.359), channel_id=1, source_target_pairs={{0,16},{4,20},{8,24},{12,28},{16,0},{20,4},{24,8},{28,12},{1,17},{... | collective-permute-start | bytes 3342344 | tf_op jit(solution)/shard_map/ppermute | solution.py:799
  334.7 26.5 %collective-permute-start.43 = (bf16[2,272,1024]{2,1,0:T(8,128)(2,1)}, bf16[2,272,1024]{2,1,0:T(8,128)(2,1)S(1)}, u32[]{:S(2)}, u32[]{:S(2)}) collective-permute-start(bf16[2,272,1024]{2,1,0:T(8,128)(2,1)} %get-tuple-element.360), channel_id=1, source_target_pairs={{0,8},{4,12},{8,0},{12,4},{16,24},{20,28},{24,16},{28,20},{1,9},{5... | collective-permute-start | bytes 3342344 | tf_op jit(solution)/shard_map/ppermute | solution.py:799
  359.2 26.2 %collective-permute-start.44 = (bf16[128,2048]{1,0:T(8,128)(2,1)S(1)}, bf16[128,2048]{1,0:T(8,128)(2,1)S(1)}, u32[]{:S(2)}, u32[]{:S(2)}) collective-permute-start(bf16[128,2048]{1,0:T(8,128)(2,1)S(1)} %add_convert_fusion.5), channel_id=1, source_target_pairs={{0,2},{1,3},{2,0},{3,1},{4,6},{5,7},{6,4},{7,5},{8,10},{9,11},{10,... | collective-permute-start | bytes 1572872 | tf_op jit(solution)/shard_map/ppermute | solution.py:860
  386.4 35.1 %collective-permute-start.49 = (bf16[128,2048]{1,0:T(8,128)(2,1)S(1)}, bf16[128,2048]{1,0:T(8,128)(2,1)S(1)}, u32[]{:S(2)}, u32[]{:S(2)}) collective-permute-start(bf16[128,2048]{1,0:T(8,128)(2,1)S(1)} %add_convert_fusion.4), channel_id=1, source_target_pairs={{0,1},{1,0},{2,3},{3,2},{4,5},{5,4},{6,7},{7,6},{8,9},{9,8},{10,11... | collective-permute-start | bytes 1572872 | tf_op jit(solution)/shard_map/ppermute | solution.py:864
  (62 other events, 767.9 us)
Sparse Core Ops, SparseCore 0:
  41.3 80.1 all-gather.2
  198.7 82.2 all-gather.4

commit v3 on v2

--- a/solution.py
+++ b/solution.py
@@ -1,3 +1,5 @@
+import math
+
 import jax
 import jax.numpy as jnp
 from jax import lax
@@ -48,6 +50,7 @@
 
 
 VMEM = 56 * 1024 * 1024
+TIGHT = ()
 ANY = pl.BlockSpec(memory_space=pl.ANY)
 DMA = pltpu.SemaphoreType.DMA
 
@@ -65,20 +68,39 @@
     return jax.ShapeDtypeStruct(shape, dtype)
 
 
-def call(kernel, grid, in_specs, out_specs, out_shape, scratch, flops, moved, trans=0):
-    return pl.pallas_call(
-        kernel,
-        grid_spec=pltpu.PrefetchScalarGridSpec(
-            num_scalar_prefetch=1,
-            grid=grid,
-            in_specs=in_specs,
-            out_specs=out_specs,
-            scratch_shapes=list(scratch),
-        ),
-        out_shape=out_shape,
-        compiler_params=pltpu.CompilerParams(vmem_limit_bytes=VMEM),
-        cost_estimate=pl.CostEstimate(flops=1024, bytes_accessed=1024, transcendentals=0),
-    )
+def room(specs, shapes, scratch):
+    total = 8 * 1024 * 1024
+    for block, shape in zip(specs, shapes):
+        if block.block_shape is not None:
+            total += 2 * math.prod(block.block_shape) * shape.dtype.itemsize
+    for item in scratch:
+        if item.memory_space == pltpu.VMEM:
+            total += math.prod(item.shape) * jnp.dtype(item.dtype).itemsize
+    return total
+
+
+def call(kernel, grid, in_specs, out_specs, out_shape, scratch):
+    def run(*args):
+        outs = out_shape if isinstance(out_shape, (list, tuple)) else [out_shape]
+        specs = out_specs if isinstance(out_specs, (list, tuple)) else [out_specs]
+        limit = VMEM
+        if kernel.__qualname__.split(".")[0] in TIGHT:
+            limit = room(list(in_specs) + list(specs), list(args[1:]) + list(outs), scratch)
+        return pl.pallas_call(
+            kernel,
+            grid_spec=pltpu.PrefetchScalarGridSpec(
+                num_scalar_prefetch=1,
+                grid=grid,
+                in_specs=in_specs,
+                out_specs=out_specs,
+                scratch_shapes=list(scratch),
+            ),
+            out_shape=out_shape,
+            compiler_params=pltpu.CompilerParams(vmem_limit_bytes=limit),
+            cost_estimate=pl.CostEstimate(flops=1024, bytes_accessed=1024, transcendentals=0),
+        )(*args)
+
+    return run
 
 
 def dot_nn(a, b):
@@ -131,17 +153,6 @@
     return copies
 
 
-def gelu_and_slope(pre):
-    density = jnp.exp(-0.5 * pre * pre)
-    t = 1.0 / (1.0 + 0.27577164466275367 * jnp.abs(pre))
-    tail = -0.1137685166 * t + 0.4433319969
-    for coefficient in (-0.3176998336, 0.3247794523, 0.04569430636, 0.1176625937):
-        tail = tail * t + coefficient
-    tail = tail * t * density
-    cumul = jnp.where(pre < 0.0, tail, 1.0 - tail)
-    return pre * cumul, cumul + pre * (density * 0.3989422804014327)
-
-
 def project(meta, tokens, first):
     rows, width = tokens.shape
     tile = 512
@@ -198,8 +209,6 @@
             pltpu.VMEM((3, 8, 128, width), BF16), pltpu.VMEM((8, 16, width), BF16),
             pltpu.VMEM((3, rows, width), BF16), DMA((3, 8)), DMA((8,)), DMA((3,)), DMA((4,)),
         ],
-        flops=10 * rows * width * width,
-        moved=10 * rows * width + 6 * width * width,
     )(meta, tokens, *first)
 
 
@@ -211,39 +220,35 @@
     span = HEADS * HD
     steps = width // span
 
-    def kernel(meta, q_ref, k_ref, v_ref, mixed_ref, probs_ref):
+    def kernel(meta, q_ref, k_ref, v_ref, mixed_ref, raised_ref, inverse_ref):
         length = meta[1 + pl.program_id(0)]
-        allowed = lax.broadcasted_iota(jnp.int32, (rows, rows), 1) < length
+        allowed = lax.broadcasted_iota(jnp.int32, (1, rows), 1) < length
+        shift = jnp.where(allowed, 0.0, NEG)
         left = lax.broadcasted_iota(jnp.int32, (rows, 128), 1) < HD
+        one = jnp.ones((rows, 128), BF16)
         for pair in range(HEADS // 2):
             cols = slice(128 * pair, 128 * (pair + 1))
-            query, keyed, value = q_ref[0, :, cols], k_ref[0, :, cols], v_ref[0, :, cols]
+            query, keyed, value = q_ref[0, :, cols] * jnp.asarray(HD**-0.5, BF16), k_ref[0, :, cols], v_ref[0, :, cols]
             outs = []
             for half in range(2):
                 mine = left if half == 0 else jnp.logical_not(left)
-                scores = dot_nt(jnp.where(mine, query, jnp.zeros_like(query)), keyed) * (HD**-0.5)
-                scores = jnp.where(allowed, scores, NEG)
-                raised = jnp.exp(scores - jnp.max(scores, -1, keepdims=True))
-                probs = raised * (1.0 / jnp.sum(raised, -1, keepdims=True))
-                low = probs.astype(BF16)
-                probs_ref[0, 2 * pair + half] = low
-                outs.append(dot_nn(low, value))
-            mixed_ref[:, cols] = jnp.where(left, outs[0], outs[1]).astype(BF16)
+                scores = dot_nt(jnp.where(mine, query, jnp.zeros_like(query)), keyed) + shift
+                raised = jnp.exp(scores - jnp.max(scores, -1, keepdims=True)).astype(BF16)
+                raised_ref[0, 2 * pair + half] = raised
+                outs.append(dot_nn(raised, jnp.where(mine, value, one)))
+            inverse = 1.0 / pltpu.roll(jnp.where(left, outs[1], outs[0]), HD, 1)
+            inverse_ref[:, cols] = inverse
+            mixed_ref[:, cols] = (jnp.where(left, outs[0], outs[1]) * inverse).astype(BF16)
 
     part = lambda w: spec((1, rows, span), lambda b, h, meta: (w, b, h))
+    here = spec((rows, span), lambda b, h, meta: (b, h))
     return call(
         kernel,
         (batches, steps),
         [part(0), part(1), part(2)],
-        [
-            spec((rows, span), lambda b, h, meta: (b, h)),
-            spec((1, HEADS, rows, rows), lambda b, h, meta: (b, h, 0, 0)),
-        ],
-        [sds((total, width), BF16), sds((batches, H, rows, rows), BF16)],
+        [here, spec((1, HEADS, rows, rows), lambda b, h, meta: (b, h, 0, 0)), here],
+        [sds((total, width), BF16), sds((batches, H, rows, rows), BF16), sds((total, width), F32)],
         [],
-        flops=20 * total * rows * width,
-        moved=8 * total * width + 2 * batches * H * rows * rows,
-        trans=batches * H * rows * rows,
     )(meta, qkv, qkv, qkv)
 
 
@@ -280,8 +285,6 @@
         [whole(block), whole((total, 128)), whole(block), ANY],
         [sds(block, F32), sds((total, 128), F32), sds(block, BF16), sds((2, 4, total, 128), BF16)],
         [pltpu.VMEM((8, 128, width), BF16), DMA((8,)), DMA((2, 4))],
-        flops=5 * total * width * width,
-        moved=10 * total * width + 2 * width * width,
     )(meta, mixed, tokens, vecs, *first)
 
 
@@ -313,7 +316,7 @@
 
             weight = held[t, :, :, pl.ds(pl.multiple_of(n * tile, tile), tile)].reshape(width, tile)
             pre = dot_nn(x_ref[...], weight) + bias_ref[:, pl.ds(pl.multiple_of(i * tile, tile), tile)]
-            value, grad = gelu_and_slope(pre)
+            value, grad = gelu_both(pre)
             act[i] = value.astype(BF16)
             slope[i] = grad.astype(BF16)
             for copy in leave(i):
@@ -345,19 +348,20 @@
             pltpu.VMEM((strips, 8, 128, strip), BF16), pltpu.VMEM((tiles, total, tile), BF16),
             pltpu.VMEM((tiles, total, tile), BF16), DMA((strips, 8)), DMA((2, tiles)), DMA((4,)),
         ],
-        flops=5 * total * width * wide,
-        moved=4 * total * wide + 2 * width * wide,
     )(meta, low, bias, *up)
 
 
-def feed_down(meta, act, down, unit_one, cot_pool, vecs, batches, rows):
+def feed_down(meta, act, slope, down, unit_one, cot_pool, vecs, batches, rows):
     total, wide = act.shape
     width = down[0].shape[1]
-    chunk = 64
-
-    def kernel(meta, act_ref, unit_ref, cot_ref, vec_ref, *refs):
+    chunk = 128
+
+    def kernel(meta, act_ref, slope_ref, unit_ref, cot_ref, vec_ref, *refs):
         parts = refs[: len(down)]
-        (out_ref, sum_ref, low_ref, grad_ref, held, left, total_ref, unit, cot, sems, left_sems, more) = refs[len(down) :]
+        (
+            out_ref, sum_ref, low_ref, grad_ref, pre_ref, bias_ref, out, grad_sums, low, early,
+            held, left, right, total_ref, unit, cot, sems, left_sems, right_sems, out_sems, more,
+        ) = refs[len(down) :]
         for b in range(8):
             pltpu.make_async_copy(act_ref.at[:, pl.ds(512 * b, 512)], left.at[b], left_sems.at[b]).start()
         fetch(meta, parts, held, sems, 0, 512)
@@ -366,6 +370,8 @@
         ]
         for copy in rest:
             copy.start()
+        for b in range(8):
+            pltpu.make_async_copy(slope_ref.at[:, pl.ds(512 * b, 512)], right.at[b], right_sems.at[b]).start()
 
         def add(b, carry):
             arrived(left.at[b], left_sems.at[b])
@@ -395,186 +401,209 @@
             normed, unit_two, inverse = normalize(summed, vec_ref[6:7], vec_ref[7:8])
             place = at + lax.broadcasted_iota(jnp.int32, (chunk, 1), 0)
             valid = place < meta[1 + batch]
-            out_ref[here] = jnp.where(valid, normed, 0.0).astype(BF16)
+            out[here] = jnp.where(valid, normed, 0.0).astype(BF16)
             grad_out = jnp.where(valid, cot[batch, pl.ds(at, chunk)].astype(F32), 0.0)
             grad_sum = norm_back(grad_out, unit_two, inverse, vec_ref[6:7])
-            sum_ref[here] = grad_sum
-            low_ref[here] = grad_sum.astype(BF16)
+            grad_sums[here] = grad_sum
+            low[here] = grad_sum.astype(BF16)
             grad_ref[0:1] += jnp.sum(grad_out * unit_two, 0, keepdims=True)
             grad_ref[1:2] += jnp.sum(grad_out, 0, keepdims=True)
             grad_ref[2:3] += jnp.sum(grad_sum, 0, keepdims=True)
             return carry
 
         lax.fori_loop(0, total // chunk, body, 0)
+        leaving = [
+            pltpu.make_async_copy(source, target, early.at[i])
+            for i, (source, target) in enumerate(((low, low_ref), (out, out_ref), (grad_sums, sum_ref)))
+        ]
+        for copy in leaving:
+            copy.start()
+
+        def leave(b):
+            at = pl.ds(pl.multiple_of(512 * b, 512), 512)
+            return pltpu.make_async_copy(left.at[b], pre_ref.at[:, at], out_sems.at[b])
+
+        def through(b, carry):
+            arrived(right.at[b], right_sems.at[b])
+            grad = (dot_nt(low[...], held[b]) * right[b].astype(F32)).astype(BF16)
+            left[b] = grad
+            leave(b).start()
+            bias_ref[:, pl.ds(pl.multiple_of(512 * b, 512), 512)] = jnp.sum(grad.astype(F32), 0, keepdims=True)
+            return carry
+
+        lax.fori_loop(0, 8, through, 0)
+        for b in range(8):
+            leave(b).wait()
+        for copy in leaving:
+            copy.wait()
 
     block = (total, width)
     return call(
         kernel,
         (1,),
-        [ANY, ANY, ANY, whole(vecs.shape)] + [ANY] * len(down),
-        [whole(block), whole(block), whole(block), whole((8, width))],
-        [sds(block, BF16), sds(block, F32), sds(block, BF16), sds((8, width), F32)],
+        [ANY, ANY, ANY, ANY, whole(vecs.shape)] + [ANY] * len(down),
+        [ANY, ANY, ANY, whole((8, width)), ANY, whole((1, wide))],
         [
-            pltpu.VMEM((8, 512, width), BF16), pltpu.VMEM((8, total, 512), BF16), pltpu.VMEM(block, F32),
-            pltpu.VMEM(block, F32), pltpu.VMEM((batches, rows, width), BF16), DMA((8,)), DMA((8,)), DMA((1 + batches,)),
+            sds(block, BF16), sds(block, F32), sds(block, BF16), sds((8, width), F32),
+            sds((total, wide), BF16), sds((1, wide), F32),
         ],
-        flops=6 * total * width * wide,
-        moved=2 * total * wide + 2 * width * wide + 14 * total * width,
-    )(meta, act, unit_one, cot_pool, vecs, *down)
-
-
-def back_down(meta, low, down, slope):
-    total, width = low.shape
-    wide = slope.shape[1]
-
-    def kernel(meta, low_ref, slope_ref, *refs):
-        parts, (pre_ref, bias_ref, held, right, made, sems, right_sems, out_sems) = refs[: len(down)], refs[len(down) :]
-        fetch(meta, parts, held, sems, 0, 512)
-        for b in range(8):
-            pltpu.make_async_copy(slope_ref.at[:, pl.ds(512 * b, 512)], right.at[b], right_sems.at[b]).start()
-
-        def leave(b):
-            at = pl.ds(pl.multiple_of(512 * b, 512), 512)
-            return pltpu.make_async_copy(made.at[b], pre_ref.at[:, at], out_sems.at[b])
-
-        def body(b, carry):
-            arrived(held.at[b], sems.at[b])
-            arrived(right.at[b], right_sems.at[b])
-            grad = (dot_nt(low_ref[...], held[b]) * right[b].astype(F32)).astype(BF16)
-            made[b] = grad
-            leave(b).start()
-            bias_ref[:, pl.ds(pl.multiple_of(512 * b, 512), 512)] = jnp.sum(grad.astype(F32), 0, keepdims=True)
-            return carry
-
-        lax.fori_loop(0, 8, body, 0)
-        for b in range(8):
-            leave(b).wait()
-
-    return call(
-        kernel,
-        (1,),
-        [whole((total, width)), ANY] + [ANY] * len(down),
-        [ANY, whole((1, wide))],
-        [sds((total, wide), BF16), sds((1, wide), F32)],
         [
+            pltpu.VMEM(block, BF16), pltpu.VMEM(block, F32), pltpu.VMEM(block, BF16), DMA((3,)),
             pltpu.VMEM((8, 512, width), BF16), pltpu.VMEM((8, total, 512), BF16), pltpu.VMEM((8, total, 512), BF16),
-            DMA((8,)), DMA((8,)), DMA((8,)),
+            pltpu.VMEM(block, F32), pltpu.VMEM(block, F32), pltpu.VMEM((batches, rows, width), BF16),
+            DMA((8,)), DMA((8,)), DMA((8,)), DMA((8,)), DMA((1 + batches,)),
         ],
-        flops=4 * total * width * wide,
-        moved=4 * total * wide + 2 * width * wide,
-    )(meta, low, slope, *down)
+    )(meta, act, slope, unit_one, cot_pool, vecs, *down)
 
 
 def back_up(meta, pre, up, first, grad_sum, unit_one, inverse_one, vecs):
     total, wide = pre.shape
     width = grad_sum.shape[1]
-    chunk = 64
+    chunk, strip = 128, 1024
+    strips = wide // strip
 
     def kernel(meta, pre_ref, sum_ref, unit_ref, inv_ref, vec_ref, *refs):
         parts, others = refs[: len(up)], refs[len(up) : len(up) + len(first)]
-        (resid_ref, low_ref, mixed_ref, grad_ref, held, out_held, grad_hidden, unit, sems, out_sems, more) = refs[len(up) + len(first) :]
-        fetch(meta, parts, held, sems, 0, 128)
-        rest = [
-            pltpu.make_async_copy(sum_ref, grad_hidden, more.at[0]),
-            pltpu.make_async_copy(unit_ref, unit, more.at[1]),
-        ]
-        for copy in rest:
-            copy.start()
+        (
+            resid_ref, low_ref, mixed_ref, grad_ref,
+            held, pres, out_held, hidden, unit, low, mixed, sems, pre_sems, out_sems, more, leave_sems,
+        ) = refs[len(up) + len(first) :]
+        for t in range(strips):
+            at = pl.ds(strip * t, strip)
+            pltpu.make_async_copy(pre_ref.at[:, at], pres.at[t], pre_sems.at[t]).start()
+            fetch(meta, parts, held.at[t], sems.at[t], 0, 128, at)
+            if t == 0:
+                incoming = pltpu.make_async_copy(sum_ref, hidden, more.at[0])
+                incoming.start()
+        other = pltpu.make_async_copy(unit_ref, unit, more.at[1])
+        other.start()
         fetch(meta, others, out_held, out_sems, 384, 512)
-        rest[0].wait()
-
-        def through(j, carry):
-            for b in range(2):
-                arrived(held.at[2 * j + b], sems.at[2 * j + b])
-            weight = held[pl.ds(2 * j, 2)].reshape(256, wide)
-            grad_hidden[:, pl.ds(pl.multiple_of(256 * j, 256), 256)] += dot_nt(pre_ref[...], weight)
+        incoming.wait()
+
+        def through(t, carry):
+            arrived(pres.at[t], pre_sems.at[t])
+            for b in range(8):
+                arrived(held.at[t, b], sems.at[t, b])
+            hidden[...] += dot_nt(pres[t], held[t].reshape(width, strip))
             return carry
 
-        lax.fori_loop(0, 4, through, 0)
-        rest[1].wait()
+        lax.fori_loop(0, strips, through, 0)
+        other.wait()
         grad_ref[...] = jnp.zeros_like(grad_ref)
 
         def body(i, carry):
             here = pl.ds(pl.multiple_of(i * chunk, chunk), chunk)
-            grad, unit_here = grad_hidden[here], unit[here]
+            grad, unit_here = hidden[here], unit[here]
             grad_ref[0:1] += jnp.sum(grad * unit_here, 0, keepdims=True)
             grad_ref[1:2] += jnp.sum(grad, 0, keepdims=True)
             resid = norm_back(grad, unit_here, inv_ref[here, 0:1], vec_ref[3:4])
             grad_ref[2:3] += jnp.sum(resid, 0, keepdims=True)
-            resid_ref[here] = resid
-            low_ref[here] = resid.astype(BF16)
+            hidden[here] = resid
+            low[here] = resid.astype(BF16)
             return carry
 
         lax.fori_loop(0, total // chunk, body, 0)
+        leaving = [
+            pltpu.make_async_copy(low, low_ref, leave_sems.at[0]), pltpu.make_async_copy(hidden, resid_ref, leave_sems.at[1])
+        ]
+        for copy in leaving:
+            copy.start()
         for b in range(8):
             arrived(out_held.at[b], out_sems.at[b])
 
+        def leave(j):
+            at = pl.ds(pl.multiple_of(512 * j, 512), 512)
+            return pltpu.make_async_copy(mixed.at[:, at], mixed_ref.at[:, at], leave_sems.at[2 + j])
+
         def out(j, carry):
             weight = out_held[pl.ds(4 * j, 4)].reshape(512, width)
-            mixed_ref[:, pl.ds(pl.multiple_of(512 * j, 512), 512)] = dot_nt(low_ref[...], weight).astype(BF16)
+            mixed[:, pl.ds(pl.multiple_of(512 * j, 512), 512)] = dot_nt(low[...], weight).astype(BF16)
+            leave(j).start()
             return carry
 
         lax.fori_loop(0, 2, out, 0)
+        for copy in leaving + [leave(0), leave(1)]:
+            copy.wait()
 
     block = (total, width)
     return call(
         kernel,
         (1,),
-        [whole((total, wide)), ANY, ANY, whole((total, 128)), whole(vecs.shape)] + [ANY] * (len(up) + len(first)),
-        [whole(block), whole(block), whole(block), whole((8, width))],
+        [ANY, ANY, ANY, whole((total, 128)), whole(vecs.shape)] + [ANY] * (len(up) + len(first)),
+        [ANY, ANY, ANY, whole((8, width))],
         [sds(block, F32), sds(block, BF16), sds(block, BF16), sds((8, width), F32)],
         [
-            pltpu.VMEM((8, 128, wide), BF16), pltpu.VMEM((8, 128, width), BF16), pltpu.VMEM(block, F32),
-            pltpu.VMEM(block, F32), DMA((8,)), DMA((8,)), DMA((2,)),
+            pltpu.VMEM((strips, 8, 128, strip), BF16), pltpu.VMEM((strips, total, strip), BF16),
+            pltpu.VMEM((8, 128, width), BF16), pltpu.VMEM(block, F32), pltpu.VMEM(block, F32), pltpu.VMEM(block, BF16),
+            pltpu.VMEM(block, BF16), DMA((strips, 8)), DMA((strips,)), DMA((8,)), DMA((2,)), DMA((4,)),
         ],
-        flops=5 * total * width * wide,
-        moved=2 * total * wide + 2 * width * wide + 18 * total * width,
     )(meta, pre, grad_sum, unit_one, inverse_one, vecs, *up, *first)
 
 
-def attend_back(meta, qkv, probs, grad_mixed, batches, rows):
+def attend_back(meta, qkv, mixed, raised, inverse, grad_mixed, grads_one, grads_two, bias_up, batches, rows):
     total, width = grad_mixed.shape
     span = HEADS * HD
-
-    def kernel(meta, q_ref, k_ref, v_ref, g_ref, probs_ref, out_ref, bias_ref):
+    steps = width // span
+
+    def kernel(meta, q_ref, k_ref, v_ref, mixed_ref, g_ref, raised_ref, inv_ref, one_ref, two_ref, up_ref, out_ref, vec_ref, sums):
+        batch, step = pl.program_id(0), pl.program_id(1)
         left = lax.broadcasted_iota(jnp.int32, (rows, 128), 1) < HD
+        none = jnp.zeros((rows, 128), BF16)
+
+        @pl.when((batch == 0) & (step == 0))
+        def _():
+            sums[...] = jnp.zeros_like(sums)
+
         for pair in range(HEADS // 2):
             cols = slice(128 * pair, 128 * (pair + 1))
-            query, keyed, value, grad = q_ref[0, :, cols], k_ref[0, :, cols], v_ref[0, :, cols], g_ref[:, cols]
+            query, keyed, value = q_ref[0, :, cols] * jnp.asarray(HD**-0.5, BF16), k_ref[0, :, cols], v_ref[0, :, cols]
+            grad = g_ref[:, cols].astype(F32) * inv_ref[:, cols]
+            both = grad * mixed_ref[:, cols].astype(F32)
+            grad = grad.astype(BF16)
             got = ([], [], [])
             for half in range(2):
                 mine = left if half == 0 else jnp.logical_not(left)
-                low = probs_ref[0, 2 * pair + half]
-                probs = low.astype(F32)
-                grad_probs = dot_nt(jnp.where(mine, grad, jnp.zeros_like(grad)), value)
-                inner = jnp.sum(probs * grad_probs, -1, keepdims=True)
-                scores = (probs * (grad_probs - inner) * (HD**-0.5)).astype(BF16)
+                low = raised_ref[0, 2 * pair + half]
+                inner = jnp.sum(jnp.where(mine, both, 0.0), -1, keepdims=True)
+                slope = dot_nt(jnp.where(mine, grad, none), value) - inner
+                scores = (low.astype(F32) * slope).astype(BF16)
                 got[0].append(dot_nn(scores, keyed))
                 got[1].append(dot_tn(scores, query))
                 got[2].append(dot_tn(low, grad))
             for i in range(3):
-                part = jnp.where(left, got[i][0], got[i][1]).astype(BF16)
+                part = jnp.where(left, got[i][0], got[i][1])
+                if i == 0:
+                    part = part * (HD**-0.5)
+                part = part.astype(BF16)
                 out_ref[i, :, cols] = part
-                bias_ref[0, i : i + 1, cols] = jnp.sum(part.astype(F32), 0, keepdims=True)
+                if i != 1:
+                    at = pl.ds(pl.multiple_of(step * span, span) + 128 * pair, 128)
+                    sums[i : i + 1, at] += jnp.sum(part.astype(F32), 0, keepdims=True)
+
+        @pl.when((batch == batches - 1) & (step == steps - 1))
+        def _():
+            vec_ref[...] = jnp.zeros_like(vec_ref)
+            rows_of = (
+                sums[0:1], sums[2:3], one_ref[2:3], one_ref[0:1], one_ref[1:2], two_ref[2:3], two_ref[0:1], two_ref[1:2]
+            )
+            table = jnp.concatenate(rows_of, 0).astype(BF16)
+            for b in range(8):
+                vec_ref[b, 0:8, 0:128] = table[:, 128 * b : 128 * (b + 1)]
+                vec_ref[b, 8:9, 0:512] = up_ref[:, 512 * b : 512 * (b + 1)].astype(BF16)
 
     part = lambda w: spec((1, rows, span), lambda b, h, meta: (w, b, h))
+    here = spec((rows, span), lambda b, h, meta: (b, h))
     return call(
         kernel,
-        (batches, width // span),
+        (batches, steps),
         [
-            part(0), part(1), part(2),
-            spec((rows, span), lambda b, h, meta: (b, h)),
-            spec((1, HEADS, rows, rows), lambda b, h, meta: (b, h, 0, 0)),
+            part(0), part(1), part(2), here, here, spec((1, HEADS, rows, rows), lambda b, h, meta: (b, h, 0, 0)), here,
+            whole((8, width)), whole((8, width)), whole((1, 4 * width)),
         ],
-        [
-            spec((3, rows, span), lambda b, h, meta: (0, b, h)),
-            spec((1, 8, span), lambda b, h, meta: (b, 0, h)),
-        ],
-        [sds((3, total, width), BF16), sds((batches, 8, width), F32)],
-        [],
-        flops=30 * total * rows * width,
-        moved=14 * total * width + 2 * batches * H * rows * rows,
-    )(meta, qkv, qkv, qkv, grad_mixed, probs)
+        [spec((3, rows, span), lambda b, h, meta: (0, b, h)), whole((8, 16, width))],
+        [sds((3, total, width), BF16), sds((8, 16, width), BF16)],
+        [pltpu.VMEM((8, width), F32)],
+    )(meta, qkv, qkv, qkv, mixed, grad_mixed, raised, inverse, grads_one, grads_two, bias_up)
 
 
 def back_project(meta, grads, first, grad_resid):
@@ -618,154 +647,211 @@
             pltpu.VMEM((8, 384, width), BF16), pltpu.VMEM(block, F32), pltpu.VMEM(block, BF16), DMA((8,)), DMA(()),
             DMA((4,)),
         ],
-        flops=10 * total * width * width,
-        moved=12 * total * width + 6 * width * width,
     )(meta, grads, grad_resid, *first)
 
 
-def weight_grad(meta, left, left_got, right, right_got, codes, block):
-    total, cols = right.shape
-    share = cols // 2
-    tile = min(share, 1024)
-    tiles = share // tile
-    count = len(codes[0])
-
-    def kernel(meta, left_ref, left_got_ref, right_ref, right_got_ref, *refs):
-        outs = refs[:2]
-        lefts, rights, made, left_sems, right_sems, out_sems = refs[2:]
-        own, got = pl.ds(0, total), pl.ds(total, total)
+def ship(made, outs, sems, half, i):
+    def copy(target):
+        return pltpu.make_async_copy(made.at[half, i], target, sems.at[half, i])
+
+    if isinstance(i, int):
+        copy(outs[half].at[i] if i < 2 else outs[2 * i - 2 + half]).start()
+        return
+
+    @pl.when(i < 2)
+    def _():
+        copy(outs[half].at[jnp.minimum(i, 1)]).start()
+
+    @pl.when(i == 2)
+    def _():
+        copy(outs[2 + half]).start()
+
+    @pl.when(i == 3)
+    def _():
+        copy(outs[4 + half]).start()
+
+
+def shipped(made, sems):
+    for half in range(2):
+        for i in range(4):
+            arrived(made.at[half, i], sems.at[half, i])
+
+
+def chip_of(half, i):
+    return (i + 2) % 4 if half == 0 else (2 * i + 1) % 5
+
+
+def six(rows, cols):
+    return [sds((2, rows, cols), BF16)] * 2 + [sds((rows, cols), BF16)] * 4
+
+
+def load_lefts(meta, own_ref, got_ref, lefts, sems, block, total):
+    for chip in (2, 3, 1, 0):
+        at = pl.ds(pl.multiple_of((meta[0] ^ (2 * chip)) * block, block), block)
+        pltpu.make_async_copy(own_ref.at[:, at], lefts.at[chip, pl.ds(0, total)], sems.at[chip]).start()
+        pltpu.make_async_copy(got_ref.at[chip], lefts.at[chip, pl.ds(total, total)], sems.at[chip]).start()
+
+
+def load_right(own, got, target, sem, total):
+    pltpu.make_async_copy(own, target.at[pl.ds(0, total)], sem).start()
+    pltpu.make_async_copy(got, target.at[pl.ds(total, total)], sem).start()
+
+
+def down_grad(meta, act, act_got, low, low_got):
+    total, width = low.shape
+    block, share = 512, width // 2
+
+    def kernel(meta, left_ref, left_got, right_ref, right_got, *refs):
+        outs, (lefts, rights, made, left_sems, right_sems, out_sems) = refs[:6], refs[6:]
         for half in range(2):
-            for t in range(tiles):
-                at = pl.ds(share * half + tile * t, tile)
-                slot = half * tiles + t
-                pltpu.make_async_copy(right_ref.at[:, at], rights.at[slot, own], right_sems.at[slot]).start()
-                pltpu.make_async_copy(right_got_ref.at[:, at], rights.at[slot, got], right_sems.at[slot]).start()
-                if t == 0:
-                    for i, code in enumerate(codes[half]):
-                        at = pl.ds(pl.multiple_of((meta[0] ^ code) * block, block), block)
-                        sem = left_sems.at[half, i]
-                        pltpu.make_async_copy(left_ref.at[:, at], lefts.at[half, i, own], sem).start()
-                        pltpu.make_async_copy(left_got_ref.at[code // 2], lefts.at[half, i, got], sem).start()
-
-        def leave(half, n):
-            t, i = n // count, n % count
-            at = pl.ds(pl.multiple_of(t * tile, tile), tile)
-            return pltpu.make_async_copy(made.at[half, i, :, at], outs[half].at[i, :, at], out_sems.at[half, n])
-
+            at = pl.ds(share * half, share)
+            load_right(right_ref.at[:, at], right_got.at[:, at], rights.at[half], right_sems.at[half], total)
+            if half == 0:
+                load_lefts(meta, left_ref, left_got, lefts, left_sems, block, total)
         for half in range(2):
-
-            def body(n, carry):
-                t, i = n // count, n % count
-
-                @pl.when(i == 0)
-                def _():
-                    arrived(rights.at[half * tiles + t], right_sems.at[half * tiles + t])
-
-                @pl.when(t == 0)
-                def _():
-                    arrived(lefts.at[half, i], left_sems.at[half, i])
-
-                at = pl.ds(pl.multiple_of(t * tile, tile), tile)
-                made[half, i, :, at] = dot_tn(lefts[half, i], rights[half * tiles + t]).astype(BF16)
-                leave(half, n).start()
+            arrived(rights.at[half], right_sems.at[half])
+
+            def body(i, carry):
+                chip = chip_of(half, i)
+                if half == 0:
+                    arrived(lefts.at[chip], left_sems.at[chip])
+                made[half, i] = dot_tn(lefts[chip], rights[half]).astype(BF16)
+                ship(made, outs, out_sems, half, i)
                 return carry
 
-            lax.fori_loop(0, tiles * count, body, 0)
-        for half in range(2):
-            for n in range(tiles * count):
-                leave(half, n).wait()
-
-    out = (2, count, block, share)
-    return call(
+            lax.fori_loop(0, 4, body, 0)
+        shipped(made, out_sems)
+
+    outs = call(
         kernel,
         (1,),
         [ANY] * 4,
-        [ANY] * 2,
-        [sds(out[1:], BF16)] * 2,
+        [ANY] * 6,
+        six(block, share),
         [
-            pltpu.VMEM((2, count, 2 * total, block), BF16), pltpu.VMEM((2 * tiles, 2 * total, tile), BF16),
-            pltpu.VMEM(out, BF16), DMA((2, count)), DMA((2 * tiles,)), DMA((2, tiles * count)),
+            pltpu.VMEM((4, 2 * total, block), BF16), pltpu.VMEM((2, 2 * total, share), BF16),
+            pltpu.VMEM((2, 4, block, share), BF16), DMA((4,)), DMA((2,)), DMA((2, 4)),
         ],
-        flops=0,
-        moved=0,
-    )(meta, left, left_got, right, right_got)
-
-
-HIGH = 272
-
-
-def first_grad(meta, tokens, tokens_got, mixed, mixed_got, grads, grads_got, low, low_got, vec, vec_got, codes):
+    )(meta, act, act_got, low, low_got)
+    return outs[:2], outs[2:4], outs[4:]
+
+
+def load_columns(meta, own_ref, got_ref, target, sem, total):
+    for chip in range(4):
+        at = pl.ds(pl.multiple_of((meta[0] ^ (2 * chip)) * 128, 128), 128)
+        cols = pl.ds(128 * chip, 128)
+        pltpu.make_async_copy(own_ref.at[:, at], target.at[pl.ds(0, total), cols], sem).start()
+        pltpu.make_async_copy(got_ref.at[chip], target.at[pl.ds(total, total), cols], sem).start()
+
+
+ORDER = ((2, 3, 0, 1), (1, 3, 0, 2))
+
+
+def up_grad(meta, hidden, hidden_got, pre, pre_got):
+    total, width = hidden.shape
+    wide = pre.shape[1]
+    tile = 1024
+    tiles = wide // tile // 2
+
+    def kernel(meta, x_ref, x_got, pre_ref, pre_got, *refs):
+        outs, (lefts, rights, made, left_sem, right_sems, out_sems) = refs[:6], refs[6:]
+        for t in range(2 * tiles):
+            at = pl.ds(tile * t, tile)
+            load_right(pre_ref.at[:, at], pre_got.at[:, at], rights.at[t], right_sems.at[t], total)
+            if t == 0:
+                load_columns(meta, x_ref, x_got.at[1], lefts, left_sem, total)
+        arrived(lefts, left_sem)
+        for half in range(2):
+
+            def body(t, carry):
+                arrived(rights.at[half * tiles + t], right_sems.at[half * tiles + t])
+                part = dot_tn(lefts[...], rights[half * tiles + t]).astype(BF16)
+                at = pl.ds(pl.multiple_of(t * tile, tile), tile)
+                for i, chip in enumerate(ORDER[half]):
+                    made[half, i, :, at] = part[128 * chip : 128 * (chip + 1)]
+                return carry
+
+            lax.fori_loop(0, tiles, body, 0)
+            for i in range(4):
+                ship(made, outs, out_sems, half, i)
+        shipped(made, out_sems)
+
+    outs = call(
+        kernel,
+        (1,),
+        [ANY] * 4,
+        [ANY] * 6,
+        six(128, wide // 2),
+        [
+            pltpu.VMEM((2 * total, 512), BF16), pltpu.VMEM((2 * tiles, 2 * total, tile), BF16),
+            pltpu.VMEM((2, 4, 128, wide // 2), BF16), DMA(()), DMA((2 * tiles,)), DMA((2, 4)),
+        ],
+    )(meta, hidden, hidden_got, pre, pre_got)
+    return outs[:2], outs[2:4], outs[4:]
+
+
+def first_grad(meta, tokens, tokens_got, mixed, mixed_got, grads, grads_got, low, low_got, vec, vec_got):
     total, width = tokens.shape
-    count = len(codes[0])
-
-    def kernel(meta, x_ref, x_got, mixed_ref, mixed_got, g_ref, g_got, low_ref, low_got, vec_ref, vec_got, *refs):
-        outs = refs[:2]
-        lefts, rights, made, short, left_sems, right_sems, out_sems, short_sems = refs[2:]
-        own, got = pl.ds(0, total), pl.ds(total, total)
-
-        def left_copy(half, kind, i):
-            code = codes[half][i]
-            at = pl.ds(pl.multiple_of((meta[0] ^ code) * 128, 128), 128)
-            slot, sem = half + kind, left_sems.at[half + kind, i]
-            source, other = ((x_ref, x_got), (mixed_ref, mixed_got))[kind]
-            pltpu.make_async_copy(source.at[:, at], lefts.at[slot, i, own], sem).start()
-            pltpu.make_async_copy(other.at[code // 2], lefts.at[slot, i, got], sem).start()
-
-        for half in range(2):
-            for w in (2 * half, 2 * half + 1):
-                source, other = (g_ref.at[w], g_got.at[w]) if w < 3 else (low_ref, low_got)
-                pltpu.make_async_copy(source, rights.at[w, own], right_sems.at[w]).start()
-                pltpu.make_async_copy(other, rights.at[w, got], right_sems.at[w]).start()
-            for i in range(count):
-                left_copy(half, 0, i)
-                if half == 1:
-                    left_copy(half, 1, i)
-                    at = meta[0] ^ codes[1][i]
-                    pltpu.make_async_copy(vec_ref.at[at], short.at[i, 0], short_sems.at[i]).start()
-                    pltpu.make_async_copy(vec_got.at[at], short.at[i, 1], short_sems.at[i]).start()
-        for half in range(2):
-
-            def body(i, carry):
-                for k in range(2):
-                    w = 2 * half + k
-                    kind = 1 if w == 3 else 0
-                    if kind == 1 or k == 0:
-                        arrived(lefts.at[half + kind, i], left_sems.at[half + kind, i])
-
-                    @pl.when(i == 0)
+    share = width // 2
+
+    def kernel(meta, x_ref, x_got, m_ref, m_got, g_ref, g_got, low_ref, low_got, vec_ref, vec_got, *refs):
+        outs = refs[:6], refs[6:12]
+        lefts, rights, made_a, made_b, short, left_sems, right_sems, sems_a, sems_b, short_sems = refs[12:]
+        for w in range(4):
+            own, got = (g_ref.at[w], g_got.at[w]) if w < 3 else (low_ref, low_got)
+            load_right(own, got, rights.at[w], right_sems.at[w], total)
+            if w == 0:
+                load_columns(meta, x_ref, x_got, lefts.at[0], left_sems.at[0], total)
+                for chip in range(4):
+                    at = meta[0] ^ (2 * chip)
+                    pltpu.make_async_copy(vec_ref.at[at], short.at[chip, 0], short_sems.at[chip]).start()
+                    pltpu.make_async_copy(vec_got.at[at], short.at[chip, 1], short_sems.at[chip]).start()
+            if w == 2:
+                load_columns(meta, m_ref, m_got.at[0], lefts.at[1], left_sems.at[1], total)
+        arrived(lefts.at[0], left_sems.at[0])
+        for group, (made, sems) in enumerate(((made_a, sems_a), (made_b, sems_b))):
+
+            def body(k, carry):
+                arrived(rights.at[2 * group + k], right_sems.at[2 * group + k])
+                if group == 1:
+
+                    @pl.when(k == 1)
                     def _():
-                        arrived(rights.at[w], right_sems.at[w])
-
-                    part = dot_tn(lefts[half + kind, i], rights[w])
-                    made[half, i, 128 * k : 128 * (k + 1)] = part.astype(BF16)
-                if half == 0:
-                    made[half, i, 256:] = jnp.zeros((16, width), BF16)
-                else:
-                    arrived(short.at[i], short_sems.at[i])
-                    made[half, i, 256:] = (short[i, 0].astype(F32) + short[i, 1].astype(F32)).astype(BF16)
-                pltpu.make_async_copy(made.at[half, i], outs[half].at[i], out_sems.at[half, i]).start()
+                        arrived(lefts.at[1], left_sems.at[1])
+
+                part = dot_tn(lefts[k * group], rights[2 * group + k]).astype(BF16)
+                rows = pl.ds(pl.multiple_of(128 * k, 128), 128)
+                for half in range(2):
+                    for i, chip in enumerate(ORDER[half]):
+                        made[half, i, rows] = part[128 * chip : 128 * (chip + 1), share * half : share * (half + 1)]
                 return carry
 
-            lax.fori_loop(0, count, body, 0)
-        for half in range(2):
-            for i in range(count):
-                pltpu.make_async_copy(made.at[half, i], outs[half].at[i], out_sems.at[half, i]).wait()
-
-    out = (2, count, HIGH, width)
-    return call(
+            lax.fori_loop(0, 2, body, 0)
+            if group == 1:
+                for i, chip in enumerate(ORDER[0]):
+                    arrived(short.at[chip], short_sems.at[chip])
+                    both = short[chip, 0].astype(F32) + short[chip, 1].astype(F32)
+                    made[0, i, 256:] = both[:, :share].astype(BF16)
+                    made[1, i, 256:] = jnp.zeros((16, share), BF16)
+            for half in range(2):
+                for i in range(4):
+                    ship(made, outs[group], sems, half, i)
+        shipped(made_a, sems_a)
+        shipped(made_b, sems_b)
+
+    outs = call(
         kernel,
         (1,),
         [ANY] * 10,
-        [ANY] * 2,
-        [sds(out[1:], BF16)] * 2,
+        [ANY] * 12,
+        six(256, share) + six(272, share),
         [
-            pltpu.VMEM((3, count, 2 * total, 128), BF16), pltpu.VMEM((4, 2 * total, width), BF16),
-            pltpu.VMEM(out, BF16), pltpu.VMEM((count, 2, 16, width), BF16),
-            DMA((3, count)), DMA((4,)), DMA((2, count)), DMA((count,)),
+            pltpu.VMEM((2, 2 * total, 512), BF16), pltpu.VMEM((4, 2 * total, width), BF16),
+            pltpu.VMEM((2, 4, 256, share), BF16), pltpu.VMEM((2, 4, 272, share), BF16),
+            pltpu.VMEM((4, 2, 16, width), BF16), DMA((2,)), DMA((4,)), DMA((2, 4)), DMA((2, 4)), DMA((4,)),
         ],
-        flops=0,
-        moved=0,
     )(meta, tokens, tokens_got, mixed, mixed_got, grads, grads_got, low, low_got, vec, vec_got)
+    return [(some[:2], some[2:4], some[4:]) for some in (outs[:6], outs[6:])]
 
 
 def pack(weights, small):
@@ -811,7 +897,8 @@
         self.meta = meta
 
     def place(self, *values):
-        return lax.optimization_barrier(values + (self.meta,))[:-1]
+        *values, self.meta = lax.optimization_barrier(values + (self.meta,))
+        return values
 
     def then(self, value):
         self.meta, value = lax.optimization_barrier((self.meta, value))
@@ -821,52 +908,39 @@
         return self.then(function(*self.place(*values)))
 
 
-def late(value, *before):
-    return lax.optimization_barrier((value,) + before)[0]
+def tie(*values):
+    return lax.optimization_barrier(values)
 
 
 def both_cores(*mine):
     return mine + tuple(swap(part, CORE) for part in mine)
 
 
-class Reduction:
-    def __init__(self, order):
-        self.order = order
-        self.odd = lax.axis_index("rep") % 2 == 1
-
-    def send(self, far):
-        self.got = swap(far[0], ALONG_Y), swap(far[1], ALONG_X)
-
-    def keep(self, near):
-        self.near = near
-
-    def turn(self):
-        def add(near_a, near_b, got_a, got_b):
-            return plus(near_a[1], got_a[1]), plus(near_b[1], got_b[1])
-
-        passed = self.order.run(add, *self.near, *self.got)
-        self.passed = swap(passed[0], ALONG_X), swap(passed[1], ALONG_Y)
-
-    def pair(self):
-        def add(near_a, near_b, got_a, got_b, passed_a, passed_b):
-            first, second = plus(near_a[0], got_a[0], passed_a), plus(near_b[0], got_b[0], passed_b)
-            return jnp.where(self.odd, second, first), jnp.where(self.odd, first, second)
-
-        self.kept, given = self.order.run(add, *self.near, *self.got, *self.passed)
-        self.taken = lax.ppermute(given, "rep", [(i, i ^ 1) for i in range(4)])
-
-    def across(self):
-        self.half = self.order.run(plus, self.kept, self.taken)
-        self.over = lax.ppermute(self.half, "rep", [(i, i ^ 2) for i in range(4)])
-
-    def back(self):
-        self.total = self.order.run(plus, self.half, self.over)
-        self.other = lax.ppermute(self.total, "rep", [(i, i ^ 1) for i in range(4)])
-
-    def done(self, axis):
-        first = jnp.where(self.odd, self.other, self.total).astype(F32)
-        second = jnp.where(self.odd, self.total, self.other).astype(F32)
-        return jnp.concatenate([first, second], axis) if axis is not None else (first, second)
+def pairs(value, mask):
+    return lax.ppermute(value, "rep", [(i, i ^ mask) for i in range(4)])
+
+
+def turned(rest, got):
+    return plus(rest[0], got[0][1]), plus(rest[1], got[1][1])
+
+
+def passed(values):
+    return swap(values[0], ALONG_X), swap(values[1], ALONG_Y)
+
+
+def sent(values):
+    return swap(values[0], ALONG_Y), swap(values[1], ALONG_X)
+
+
+def summed(own, got, late):
+    odd = lax.axis_index("rep") % 2 == 1
+    first, second = plus(own[0], got[0][0], late[0]), plus(own[1], got[1][0], late[1])
+    return jnp.where(odd, second, first), jnp.where(odd, first, second)
+
+
+def unfolded(mine, other):
+    odd = lax.axis_index("rep") % 2 == 1
+    return jnp.where(odd, other, mine).astype(F32), jnp.where(odd, mine, other).astype(F32)
 
 
 def local_eight(
@@ -893,102 +967,114 @@
     small = (b_query, b_value, b_out, ln1_gain, ln1_bias, b_down, ln2_gain, ln2_bias, b_up)
     own_first = pack((w_query, w_key, w_value, w_out), small)
     first_x, first_y = swap(own_first, ALONG_X), swap(own_first, ALONG_Y)
-    first_far = swap(first_x, ALONG_Y)
-    up_x = swap(late(w_up, first_x), ALONG_X)
-    up_y = swap(late(w_up, first_far), ALONG_Y)
-    down_x = swap(late(w_down, up_x), ALONG_X)
-    first = both_cores(own_first, first_x, first_y, first_far)
+    first_x, first_y, to_both = order.then((first_x, first_y, w_up))
+    first_far, up_x = swap(first_x, ALONG_Y), swap(to_both, ALONG_X)
+    first_c = [swap(part, CORE) for part in (own_first, first_x, first_y)]
+    first_far, up_x, to_x, to_y, *first_c = order.then((first_far, up_x, w_down, w_up, *first_c))
+    first = (own_first, first_x, first_y, first_far, *first_c, swap(first_far, CORE))
+    up_y, down_x = swap(to_y, ALONG_Y), swap(to_x, ALONG_X)
+    up_c = [swap(part, CORE) for part in (w_up, up_x)]
     cot_pool = lax.all_gather(cotangent, "rep", axis=0, tiled=True)
-
     qkv, vecs, bias_up, tokens_give = order.then(project(order.meta, tokens, first))
+    mixed, raised, inverse = order.then(attend(order.meta, qkv, batches, rows))
+    up_y, down_x, tokens_give, to_y, *up_c = order.then((up_y, down_x, tokens_give, w_down, *up_c))
+    up_far, down_y = swap(up_y, ALONG_X), swap(to_y, ALONG_Y)
+    up_c.append(swap(up_y, CORE))
     tokens_got = swap(tokens_give, CORE)
-    mixed, probs = order.then(attend(order.meta, qkv, batches, rows))
-    (up_y,) = order.then(order.place(up_y))
-    up_far = swap(up_y, ALONG_X)
-    down_y = swap(late(w_down, up_y), ALONG_Y)
     unit_one, inverse_one, hidden_low, both_give = order.then(mix_out(order.meta, mixed, tokens, first, vecs))
-    (down_x,) = order.then(order.place(down_x))
-    down_top = swap(down_x[:256], ALONG_Y)
-    (up_far,) = order.place(up_far)
-    up = both_cores(w_up, up_x, up_y, up_far)
+    up_far, down_y, tokens_got, both_give, *up_c = order.then((up_far, down_y, tokens_got, both_give, *up_c))
+    up = (w_up, up_x, up_y, up_far, *up_c, swap(up_far, CORE))
+    down_top, down_end = swap(down_x[:256], ALONG_Y), swap(down_y[256:], ALONG_X)
+    up = order.then(up)
+    down_c = [swap(part, CORE) for part in (w_down, down_x, down_y)]
     act, slope, act_give = order.then(feed_up(order.meta, hidden_low, up, bias_up))
-    (down_y,) = order.then(order.place(down_y))
-    down_end = swap(down_y[256:], ALONG_X)
-    down = both_cores(w_down, down_x, down_y, down_top, down_end)
-    both_got, act_got = swap(both_give, CORE), swap(act_give, CORE)
-    tokens_got, both_got, act_got = order.then((tokens_got, both_got, act_got))
-    mixed_got, hidden_got = both_got[0], both_got[1]
-    out, grad_sum, sum_low, grads_two = order.then(
-        feed_down(order.meta, act, down, unit_one, cot_pool, vecs, batches, rows)
-    )
-    sum_got = order.then(swap(sum_low, CORE))
+    down_top, down_end, act_give, both_give, *down_c = order.then((down_top, down_end, act_give, both_give, *down_c))
+    down = (w_down, down_x, down_y, down_top, down_end) + tuple(down_c)
+    down += tuple(swap(part, CORE) for part in (down_top, down_end))
+    *down, act_give, both_give = order.then((*down, act_give, both_give))
+    act_got, both_got = swap(act_give, CORE), swap(both_give, CORE)
+    out, grad_sum, sum_low, grads_two, pre, grad_bias_up = order.then(
+        feed_down(order.meta, act, slope, down, unit_one, cot_pool, vecs, batches, rows)
+    )
+    sum_got = swap(sum_low, CORE)
+    out, act_got, both_got, sum_got, pre = order.then((out, act_got, both_got, sum_got, pre))
+    pre_got = swap(pre, CORE)
     out_pool = lax.all_gather(out.reshape(batches, rows, width), "rep", axis=0, tiled=True)
-    far, near = [[4, 6], [2, 6]], [[0, 2], [0, 4]]
-    of_down, of_up, of_first = Reduction(order), Reduction(order), Reduction(order)
-
-    def down_grad(codes):
-        return order.then(weight_grad(order.meta, act, act_got, sum_low, sum_got, codes, 512))
-
-    def up_grad(codes):
-        return order.then(weight_grad(order.meta, hidden_low, hidden_got, pre, pre_got, codes, 128))
-
-    def attn_grad(codes):
-        return order.then(
-            first_grad(
-                order.meta, tokens, tokens_got, mixed, mixed_got, grads, grads_got, resid_low, resid_got, vec, vec_got,
-                codes,
-            )
-        )
-
-    of_down.send(down_grad(far))
-    pre, grad_bias_up = order.then(back_down(order.meta, sum_low, down, slope))
-    pre_got = swap(pre, CORE)
-    of_down.keep(down_grad(near))
-    of_up.send(up_grad(far))
+    far_down, own_down, rest_down = order.then(down_grad(order.meta, act, act_got, sum_low, sum_got))
+    pre_got, far_down = order.then((pre_got, far_down))
+    got_down = sent(far_down)
     grad_resid, resid_low, grad_mixed, grads_one = order.then(
         back_up(order.meta, pre, up, first, grad_sum, unit_one, inverse_one, vecs)
     )
-    of_down.turn()
-    resid_got = swap(resid_low, CORE)
-    of_up.keep(up_grad(near))
-    grads, grads_bias = order.then(attend_back(order.meta, qkv, probs, grad_mixed, batches, rows))
-    (out_pool,) = order.then(order.place(out_pool))
-    of_down.pair()
-    of_up.turn()
-    grads_got = swap(grads, CORE)
-    grads_bias = jnp.sum(grads_bias, 0)
-    rows_of = (
-        grads_bias[0], grads_bias[2], grads_one[2], grads_one[0], grads_one[1],
-        grads_two[2], grads_two[0], grads_two[1],
-    )
-    vec = jnp.concatenate(
-        [jnp.stack(rows_of).reshape(8, 8, 128).transpose(1, 0, 2).reshape(8, width), grad_bias_up.reshape(8, 512)], 1
-    )
-    vec = jnp.pad(vec, ((0, 0), (0, 16 * width - vec.shape[1]))).reshape(8, 16, width).astype(BF16)
-    vec_got = swap(vec, CORE)
+    far_up, own_up, rest_up = order.then(up_grad(order.meta, hidden_low, both_got, pre, pre_got))
+    got_down, far_up, resid_low = order.then((got_down, far_up, resid_low))
+    got_up = sent(far_up)
+    late_down = passed(order.then(turned(rest_down, got_down)))
+    grads, vec = order.then(
+        attend_back(
+            order.meta, qkv, mixed, raised, inverse, grad_mixed, grads_one, grads_two, grad_bias_up, batches, rows
+        )
+    )
     grad_input = order.then(back_project(order.meta, grads, first, grad_resid))
-    of_down.across()
-    of_first.send(attn_grad(far))
-    of_up.pair()
-    of_first.keep(attn_grad(near))
-    of_down.back()
-    of_up.across()
-    of_first.turn()
-    of_up.back()
-    of_first.pair()
-    g_down = order.run(lambda *_: of_down.done(1))
-    of_first.across()
-    g_up = order.run(lambda *_: of_up.done(1))
-    of_first.back()
-    top, end = of_first.done(None)
-    layer_out = pick(out_pool, sources)
-    g_vec = end[256:258].reshape(-1)
-    line = lambda i: g_vec[128 * i : 128 * (i + 1)]
+    got_up, late_down, resid_low, grads, vec = order.then((got_up, late_down, resid_low, grads, vec))
+    resid_got, grads_got, vec_got = swap(resid_low, CORE), swap(grads, CORE), swap(vec, CORE)
+    pass_up = order.then(turned(rest_up, got_up))
+    kept_down, given_down = order.then(summed(own_down, got_down, late_down))
+    resid_got, grads_got, vec_got, pass_up, given_down = order.then((resid_got, grads_got, vec_got, pass_up, given_down))
+    late_up, taken_down = passed(pass_up), pairs(given_down, 1)
+    (far_a, own_a, rest_a), (far_b, own_b, rest_b) = order.then(
+        first_grad(
+            order.meta, tokens, tokens_got, mixed, both_got, grads, grads_got, resid_low, resid_got, vec, vec_got
+        )
+    )
+    late_up, taken_down, far_a, out_pool = order.then((late_up, taken_down, far_a, out_pool))
+    got_a = sent(far_a)
+    far_b, half_down = order.then((far_b, plus(kept_down, taken_down)))
+    got_b = sent(far_b)
+    over_down = pairs(half_down, 2)
+    kept_up, given_up = order.then(summed(own_up, got_up, late_up))
+    got_a = order.then(got_a)
+    late_a = passed(order.then(turned(rest_a, got_a)))
+    taken_up = pairs(given_up, 1)
+    layer_out = order.then(pick(out_pool, sources))
+    got_b = order.then(got_b)
+    late_b = passed(order.then(turned(rest_b, got_b)))
+    late_a = order.then(late_a)
+    kept_a, given_a = order.then(summed(own_a, got_a, late_a))
+    taken_a = pairs(given_a, 1)
+    over_down, taken_up = order.then((over_down, taken_up))
+    total_down, half_up = order.then((plus(half_down, over_down), plus(kept_up, taken_up)))
+    late_b = order.then(late_b)
+    kept_b, given_b = order.then(summed(own_b, got_b, late_b))
+    taken_b = pairs(given_b, 1)
+    taken_a = order.then(taken_a)
+    half_a = order.then(plus(kept_a, taken_a))
+    over_a = pairs(half_a, 2)
+    over_up, other_down = pairs(half_up, 2), pairs(total_down, 1)
+    taken_b = order.then(taken_b)
+    half_b = order.then(plus(kept_b, taken_b))
+    over_b = pairs(half_b, 2)
+    over_a = order.then(over_a)
+    total_a = order.then(plus(half_a, over_a))
+    other_a = pairs(total_a, 1)
+    over_up, other_down = order.then((over_up, other_down))
+    total_up = order.then(plus(half_up, over_up))
+    other_up = pairs(total_up, 1)
+    g_down = order.then(jnp.concatenate(unfolded(total_down, other_down), 1))
+    over_b = order.then(over_b)
+    total_b = order.then(plus(half_b, over_b))
+    other_b = pairs(total_b, 1)
+    other_a, other_up = order.then((other_a, other_up))
+    g_up = order.then(jnp.concatenate(unfolded(total_up, other_up), 1))
+    g_a = order.then(jnp.concatenate(unfolded(total_a, other_a), 1))
+    left, right = unfolded(total_b, other_b)
+    g_b = jnp.concatenate([left[:256], right[:256]], 1)
+    line = lambda i: left[256 + i, :128]
     return (
         layer_out, grad_input.reshape(batches, rows, width),
-        top[0:128], top[128:256], end[0:128], end[128:256],
+        g_a[0:128], g_a[128:256], g_b[0:128], g_b[128:256],
         line(0), line(1), line(2), line(3), line(4),
-        g_up, g_vec[1024:1536], g_down, line(5), line(6), line(7),
+        g_up, left[264, :512], g_down, line(5), line(6), line(7),
     )
 
 

time: 450 us -> 393 us (0.87)
  waiting for transfers between devices: 179 us -> 136 us
  Pallas kernels: 167 us -> 142 us
  starting transfers between devices: 45.3 us -> 58.7 us
    ppermute x43 -> x47, waiting for transfers between devices: 109 us -> 82.1 us  [swap(): return lax.ppermute(value, 'shard', [(i, i ^ mask) for i in range(8)])]
    pallas_call x15 -> x11, Pallas kernels: 164 us -> 139 us  [run(): pl.pallas_call(kernel, grid_spec=pltpu.PrefetchScalarGridSpec(num_scalar_...]
    ppermute x9 -> x12, waiting for transfers between devices: 70.2 us -> 53.9 us  [pairs(): return lax.ppermute(value, 'rep', [(i, i ^ mask) for i in range(4)])]
    ppermute x9 -> x12, starting transfers between devices: 11.9 us -> 20.6 us  [pairs(): return lax.ppermute(value, 'rep', [(i, i ^ mask) for i in range(4)])]
    ppermute x43 -> x47, starting transfers between devices: 33.3 us -> 38 us  [swap(): return lax.ppermute(value, 'shard', [(i, i ^ mask) for i in range(8)])]
    convert_element_type x12 -> x16, other arithmetic: 9.5 us -> 8.89 us  [plus(): return total.astype(BF16)]
  transfers between devices with their start and end apart: 54 -> 61, of which waited for: 22 -> 26; matrix products, arithmetic and copies ran while one was open for 6% -> 6% of each run, Pallas kernels for 33% -> 36%
where the time goes in v3:
time: 393 us; the launch traced here: 392 us
  Pallas kernels  142 us (36%)
  waiting for transfers between devices  136 us (35%)
  starting transfers between devices  58.7 us (15%)
  other arithmetic  20.7 us (5%)
  between operations  18.8 us (5%)
  local copies, waits for them, and re-layouts  16.3 us (4%)
    pallas_call x11, Pallas kernels, run(): pl.pallas_call(kernel, grid_spec=pltpu.PrefetchScalarGridSpec(num_scalar_...  139 us
    ppermute x47, waiting for transfers between devices, swap(): return lax.ppermute(value, 'shard', [(i, i ^ mask) for i in range(8)])  82.1 us
    ppermute x12, waiting for transfers between devices, pairs(): return lax.ppermute(value, 'rep', [(i, i ^ mask) for i in range(4)])  53.9 us
    ppermute x47, starting transfers between devices, swap(): return lax.ppermute(value, 'shard', [(i, i ^ mask) for i in range(8)])  38 us
    ppermute x12, starting transfers between devices, pairs(): return lax.ppermute(value, 'rep', [(i, i ^ mask) for i in range(4)])  20.6 us
    convert_element_type x16, other arithmetic, plus(): return total.astype(BF16)  8.89 us
  transfers between devices with their start and end apart: 61, of which 26 were waited for; matrix products, arithmetic and copies ran while one was open for 6% of the time, Pallas kernels for 36%

profile of v3, /device:TPU:0, one launch (start us, length us, event | category | flops | bytes accessed | tf_op | source)
XLA Modules:
  0.0 392.1 jit_solution(7630844105241646187)
XLA Ops:
  10.8 2.9 collective-permute-start
  17.5 20.4 %collective-permute-done.refs_1_.refs_9_ = bf16[528,1024]{1,0:T(8,128)(2,1)S(1)} collective-permute-done((bf16[528,1024]{1,0:T(8,128)(2,1)}, bf16[528,1024]{1,0:T(8,128)(2,1)S(1)}, u32[]{:S(2)}, u32[]{:S(2)}) %collective-permute-start) | collective-permute-done | bytes 1081376 | tf_op jit(solution)/shard_map/ppermute | solution.py:885
  42.0 24.8 %collective-permute-done.3.refs_1_ = bf16[128,4096]{1,0:T(8,128)(2,1)} collective-permute-done((bf16[128,4096]{1,0:T(8,128)(2,1)}, bf16[128,4096]{1,0:T(8,128)(2,1)}, u32[]{:S(2)}, u32[]{:S(2)}) %collective-permute-start.3) | collective-permute-done | bytes 1048608 | tf_op jit(solution)/shard_map/ppermute | solution.py:885
  70.7 11.2 %shard_map.315 = (bf16[3,512,1024]{2,1,0:T(8,128)(2,1)}, f32[8,1024]{1,0:T(8,128)}, f32[1,4096]{1,0:T(1,128)}, bf16[4,512,128]{2,1,0:T(8,128)(2,1)}) custom-call(s32[5]{0:T(128)} %pad_add_fusion.meta, bf16[512,1024]{1,0:T(8,128)(2,1)} %bitcast.111, bf16[528,1024]{1,0:T(8,128)(2,1)} %shard_map.314.refs_0_.refs_8_, bf16[528,1024]{1,0:T(8,128)(2,1)} %copy-done.3, ...), custom_call_target="tpu_custom_call" | custom-call | flops 1024 | bytes 1024 | tf_op jit(solution)/shard_map/pallas_call | solution.py:89
  82.0 10.8 %shard_map.316 = (bf16[512,1024]{1,0:T(8,128)(2,1)}, bf16[2,16,256,256]{3,2,1,0:T(8,128)(2,1)}, f32[512,1024]{1,0:T(8,128)}) custom-call(s32[5]{0:T(128)} %pad_add_fusion.meta, bf16[3,512,1024]{2,1,0:T(8,128)(2,1)} %get-tuple-element.290.q_ref.k_ref.v_ref, bf16[3,512,1024]{2,1,0:T(8,128)(2,1)} %get-tuple-element.290.q_ref.k_ref.v_ref, ...), custom_call_target="tpu_custom_call" | custom-call | flops 1024 | bytes 1024 | tf_op jit(solution)/shard_map/pallas_call | solution.py:89
  96.0 9.4 %shard_map.317 = (f32[512,1024]{1,0:T(8,128)}, f32[512,128]{1,0:T(8,128)}, bf16[512,1024]{1,0:T(8,128)(2,1)}, bf16[2,4,512,128]{3,2,1,0:T(8,128)(2,1)}) custom-call(s32[5]{0:T(128)} %pad_add_fusion.meta, bf16[512,1024]{1,0:T(8,128)(2,1)} %get-tuple-element.300.mixed_ref.m_ref, bf16[512,1024]{1,0:T(8,128)(2,1)} %bitcast.112, ...), custom_call_target="tpu_custom_call" | custom-call | flops 1024 | bytes 1024 | tf_op jit(solution)/shard_map/pallas_call | solution.py:89
  105.5 12.7 %collective-permute-done.12.refs_3_ = bf16[128,4096]{1,0:T(8,128)(2,1)S(1)} collective-permute-done((bf16[128,4096]{1,0:T(8,128)(2,1)S(1)}, bf16[128,4096]{1,0:T(8,128)(2,1)S(1)}, u32[]{:S(2)}, u32[]{:S(2)}) %collective-permute-start.12) | collective-permute-done | bytes 1048608 | tf_op jit(solution)/shard_map/ppermute | solution.py:885
  124.9 13.8 %shard_map.318 = (bf16[512,4096]{1,0:T(8,128)(2,1)}, bf16[512,4096]{1,0:T(8,128)(2,1)}, bf16[4,512,512]{2,1,0:T(8,128)(2,1)}) custom-call(s32[5]{0:T(128)} %pad_add_fusion.meta, bf16[512,1024]{1,0:T(8,128)(2,1)} %get-tuple-element.319.x_ref, f32[1,4096]{1,0:T(1,128)} %get-tuple-element.320.bias_ref, bf16[128,4096]{1,0:T(8,128)(2,1)} %refs_0_.4, ...), custom_call_target="tpu_custom_call" | custom-call | flops 1024 | bytes 1024 | tf_op jit(solution)/shard_map/pallas_call | solution.py:89
  142.7 21.7 %shard_map.319 = (bf16[512,1024]{1,0:T(8,128)(2,1)}, f32[512,1024]{1,0:T(8,128)}, bf16[512,1024]{1,0:T(8,128)(2,1)}, f32[8,1024]{1,0:T(8,128)}, bf16[512,4096]{1,0:T(8,128)(2,1)}, /*index=5*/f32[1,4096]{1,0:T(1,128)}) custom-call(s32[5]{0:T(128)} %pad_add_fusion.meta, bf16[512,4096]{1,0:T(8,128)(2,1)} %get-tuple-element.346.act_ref.left_ref, ...), custom_call_target="tpu_custom_call" | custom-call | flops 1024 | bytes 1024 | tf_op jit(solution)/shard_map/pallas_call | solution.py:89
  165.6 2.5 collective-permute-done.26.right_got
  170.6 9.6 %shard_map.320 = (bf16[2,512,512]{2,1,0:T(8,128)(2,1)}, bf16[2,512,512]{2,1,0:T(8,128)(2,1)}, bf16[512,512]{1,0:T(8,128)(2,1)}, bf16[512,512]{1,0:T(8,128)(2,1)}...) custom-call(s32[5]{0:T(128)} %pad_add_fusion.meta, bf16[512,4096]{1,0:T(8,128)(2,1)} %get-tuple-element.346.act_ref.left_ref, ...), custom_call_target="tpu_custom_call" | custom-call | flops 1024 | bytes 1024 | tf_op jit(solution)/shard_map/pallas_call | solution.py:89
  182.3 2.6 collective-permute-start.29
  184.9 16.8 %shard_map.321 = (f32[512,1024]{1,0:T(8,128)}, bf16[512,1024]{1,0:T(8,128)(2,1)}, bf16[512,1024]{1,0:T(8,128)(2,1)}, f32[8,1024]{1,0:T(8,128)}) custom-call(s32[5]{0:T(128)} %pad_add_fusion.meta, bf16[512,4096]{1,0:T(8,128)(2,1)} %get-tuple-element.381.pre_ref, f32[512,1024]{1,0:T(8,128)} %get-tuple-element.385.sum_ref, ...), custom_call_target="tpu_custom_call" | custom-call | flops 1024 | bytes 1024 | tf_op jit(solution)/shard_map/pallas_call | solution.py:89
  201.7 11.1 %shard_map.322 = (bf16[2,128,2048]{2,1,0:T(8,128)(2,1)}, bf16[2,128,2048]{2,1,0:T(8,128)(2,1)}, bf16[128,2048]{1,0:T(8,128)(2,1)}, bf16[128,2048]{1,0:T(8,128)(2...) custom-call(s32[5]{0:T(128)} %pad_add_fusion.meta, bf16[512,1024]{1,0:T(8,128)(2,1)} %get-tuple-element.319.x_ref, ...), custom_call_target="tpu_custom_call" | custom-call | flops 1024 | bytes 1024 | tf_op jit(solution)/shard_map/pallas_call | solution.py:89
  218.9 14.7 %shard_map.323 = (bf16[3,512,1024]{2,1,0:T(8,128)(2,1)}, bf16[8,16,1024]{2,1,0:T(8,128)(2,1)}) custom-call(s32[5]{0:T(128)} %pad_add_fusion.meta, bf16[3,512,1024]{2,1,0:T(8,128)(2,1)} %get-tuple-element.290.q_ref.k_ref.v_ref, bf16[3,512,1024]{2,1,0:T(8,128)(2,1)} %get-tuple-element.290.q_ref.k_ref.v_ref, ...), custom_call_target="tpu_custom_call" | custom-call | flops 1024 | bytes 1024 | tf_op jit(solution)/shard_map/pallas_call | solution.py:89
  233.6 10.5 %shard_map.324 = bf16[512,1024]{1,0:T(8,128)(2,1)} custom-call(s32[5]{0:T(128)} %pad_add_fusion.meta, bf16[3,512,1024]{2,1,0:T(8,128)(2,1)} %get-tuple-element.442.g_ref, f32[512,1024]{1,0:T(8,128)} %get-tuple-element.422.resid_ref, bf16[528,1024]{1,0:T(8,128)(2,1)} %shard_map.314.refs_0_.refs_8_, bf16[528,1024]{1,0:T(8,128)(2,1)} %copy-done.3, ...), custom_call_target="tpu_custom_call" | custom-call | flops 1024 | bytes 1024 | tf_op jit(solution)/shard_map/pallas_call | solution.py:89
  244.1 5.2 %collective-permute-done.32 = bf16[512,512]{1,0:T(8,128)(2,1)S(1)} collective-permute-done((bf16[512,512]{1,0:T(8,128)(2,1)}, bf16[512,512]{1,0:T(8,128)(2,1)S(1)}, u32[]{:S(2)}, u32[]{:S(2)}) %collective-permute-start.32) | collective-permute-done | bytes 524320 | tf_op jit(solution)/shard_map/ppermute | solution.py:885
  256.6 2.7 broadcast_select_fusion.6
  268.2 9.7 %shard_map.325 = (bf16[2,256,512]{2,1,0:T(8,128)(2,1)}, bf16[2,256,512]{2,1,0:T(8,128)(2,1)}, bf16[256,512]{1,0:T(8,128)(2,1)}, bf16[256,512]{1,0:T(8,128)(2,1)}...) custom-call(s32[5]{0:T(128)} %pad_add_fusion.meta, ...), custom_call_target="tpu_custom_call" | custom-call | flops 1024 | bytes 1024 | tf_op jit(solution)/shard_map/pallas_call | solution.py:89
  284.2 2.6 collective-permute-start.49
  290.8 4.9 %collective-permute-done.40 = bf16[2,256,512]{2,1,0:T(8,128)(2,1)S(1)} collective-permute-done((bf16[2,256,512]{2,1,0:T(8,128)(2,1)S(1)}, bf16[2,256,512]{2,1,0:T(8,128)(2,1)S(1)}, u32[]{:S(2)}, u32[]{:S(2)}) %collective-permute-start.40) | collective-permute-done | bytes 524320 | tf_op jit(solution)/shard_map/ppermute | solution.py:885
  297.6 5.6 %collective-permute-done.50 = bf16[128,2048]{1,0:T(8,128)(2,1)S(1)} collective-permute-done((bf16[128,2048]{1,0:T(8,128)(2,1)S(1)}, bf16[128,2048]{1,0:T(8,128)(2,1)S(1)}, u32[]{:S(2)}, u32[]{:S(2)}) %collective-permute-start.50) | collective-permute-done | bytes 524320 | tf_op jit(solution)/shard_map/ppermute | solution.py:920
  303.2 5.8 %collective-permute-done.49 = bf16[512,512]{1,0:T(8,128)(2,1)S(1)} collective-permute-done((bf16[512,512]{1,0:T(8,128)(2,1)S(1)}, bf16[512,512]{1,0:T(8,128)(2,1)S(1)}, u32[]{:S(2)}, u32[]{:S(2)}) %collective-permute-start.49) | collective-permute-done | bytes 524320 | tf_op jit(solution)/shard_map/ppermute | solution.py:920
  313.7 3.4 collective-permute-done.44
  322.7 13.9 %collective-permute-done.51 = bf16[128,2048]{1,0:T(8,128)(2,1)S(1)} collective-permute-done((bf16[128,2048]{1,0:T(8,128)(2,1)S(1)}, bf16[128,2048]{1,0:T(8,128)(2,1)S(1)}, u32[]{:S(2)}, u32[]{:S(2)}) %collective-permute-start.51) | collective-permute-done | bytes 524320 | tf_op jit(solution)/shard_map/ppermute | solution.py:920
  336.5 8.4 %collective-permute-done.52 = bf16[512,512]{1,0:T(8,128)(2,1)S(1)} collective-permute-done((bf16[512,512]{1,0:T(8,128)(2,1)S(1)}, bf16[512,512]{1,0:T(8,128)(2,1)S(1)}, u32[]{:S(2)}, u32[]{:S(2)}) %collective-permute-start.52) | collective-permute-done | bytes 524320 | tf_op jit(solution)/shard_map/ppermute | solution.py:920
  345.1 8.5 %collective-permute-done.46 = bf16[256,512]{1,0:T(8,128)(2,1)S(1)} collective-permute-done((bf16[256,512]{1,0:T(8,128)(2,1)S(1)}, bf16[256,512]{1,0:T(8,128)(2,1)S(1)}, u32[]{:S(2)}, u32[]{:S(2)}) %collective-permute-start.46) | collective-permute-done | bytes 262176 | tf_op jit(solution)/shard_map/ppermute | solution.py:920
  356.1 2.5 collective-permute-start.53
  359.7 3.1 collective-permute-start.57
  362.8 3.4 collective-permute-done.47
  367.9 5.6 %collective-permute-done.57 = bf16[272,512]{1,0:T(8,128)(2,1)S(1)} collective-permute-done((bf16[272,512]{1,0:T(8,128)(2,1)S(1)}, bf16[272,512]{1,0:T(8,128)(2,1)S(1)}, u32[]{:S(2)}, u32[]{:S(2)}) %collective-permute-start.57) | collective-permute-done | bytes 278560 | tf_op jit(solution)/shard_map/ppermute | solution.py:920
  373.6 4.8 %collective-permute-start.58 = (bf16[272,512]{1,0:T(8,128)(2,1)S(1)}, bf16[272,512]{1,0:T(8,128)(2,1)S(1)}, u32[]{:S(2)}, u32[]{:S(2)}) collective-permute-start(bf16[272,512]{1,0:T(8,128)(2,1)S(1)} %add_convert_fusion.4), channel_id=1, source_target_pairs={{0,1},{1,0},{2,3},{3,2},{4,5},{5,4},{6,7},{7,6},{8,9},{9,8},{10,11... | collective-permute-start | bytes 835592 | tf_op jit(solution)/shard_map/ppermute | solution.py:920
  (262 shorter events, 87.7 us)
Async XLA Ops:
  7.2 135.4 %all-gather.3.cloned.1.call-start = ((), (), s32[]{:S(2)}) async-start(), calls=%async_computation | async-start | bytes 5242880 | tf_op jit(solution)/shard_map/all_gather | solution.py:977
  10.8 27.0 %collective-permute-start = (bf16[528,1024]{1,0:T(8,128)(2,1)}, bf16[528,1024]{1,0:T(8,128)(2,1)S(1)}, u32[]{:S(2)}, u32[]{:S(2)}) collective-permute-start(bf16[528,1024]{1,0:T(8,128)(2,1)} %shard_map.314.refs_0_.refs_8_), channel_id=1, source_target_pairs={{0,8},{4,12},{8,0},{12,4},{16,24},{20,28},{24,16},{28,20},{1,9},{5... | collective-permute-start | bytes 3244040 | tf_op jit(solution)/shard_map/ppermute | solution.py:885
  13.8 25.5 %collective-permute-start.1 = (bf16[528,1024]{1,0:T(8,128)(2,1)}, bf16[528,1024]{1,0:T(8,128)(2,1)S(1)}, u32[]{:S(2)}, u32[]{:S(2)}) collective-permute-start(bf16[528,1024]{1,0:T(8,128)(2,1)} %shard_map.314.refs_0_.refs_8_), channel_id=1, source_target_pairs={{0,16},{4,20},{8,24},{12,28},{16,0},{20,4},{24,8},{28,12},{1,17},{... | collective-permute-start | bytes 3244040 | tf_op jit(solution)/shard_map/ppermute | solution.py:885
  15.3 26.7 %collective-permute-start.4 = (bf16[528,1024]{1,0:T(8,128)(2,1)}, bf16[528,1024]{1,0:T(8,128)(2,1)S(1)}, u32[]{:S(2)}, u32[]{:S(2)}) collective-permute-start(bf16[528,1024]{1,0:T(8,128)(2,1)} %shard_map.314.refs_0_.refs_8_), channel_id=1, source_target_pairs={{0,4},{4,0},{8,12},{12,8},{16,20},{20,16},{24,28},{28,24},{1,5},{5... | collective-permute-start | bytes 3244040 | tf_op jit(solution)/shard_map/ppermute | solution.py:885
  39.3 27.4 %collective-permute-start.2 = (bf16[528,1024]{1,0:T(8,128)(2,1)S(1)}, bf16[528,1024]{1,0:T(8,128)(2,1)}, u32[]{:S(2)}, u32[]{:S(2)}) collective-permute-start(bf16[528,1024]{1,0:T(8,128)(2,1)S(1)} %collective-permute-done.refs_1_.refs_9_), channel_id=1, source_target_pairs={{0,16},{4,20},{8,24},{12,28},{16,0},{20,4},{24,8},{28,12},{1,17},{... | collective-permute-start | bytes 3244040 | tf_op jit(solution)/shard_map/ppermute | solution.py:885
  40.8 25.9 %collective-permute-start.5 = (bf16[528,1024]{1,0:T(8,128)(2,1)S(1)}, bf16[528,1024]{1,0:T(8,128)(2,1)}, u32[]{:S(2)}, u32[]{:S(2)}) collective-permute-start(bf16[528,1024]{1,0:T(8,128)(2,1)S(1)} %collective-permute-done.refs_1_.refs_9_), channel_id=1, source_target_pairs={{0,4},{4,0},{8,12},{12,8},{16,20},{20,16},{24,28},{28,24},{1,5},{5... | collective-permute-start | bytes 3244040 | tf_op jit(solution)/shard_map/ppermute | solution.py:885
  40.8 25.9 %collective-permute-start.6 = (bf16[528,1024]{1,0:T(8,128)(2,1)S(1)}, bf16[528,1024]{1,0:T(8,128)(2,1)}, u32[]{:S(2)}, u32[]{:S(2)}) collective-permute-start(bf16[528,1024]{1,0:T(8,128)(2,1)S(1)} %collective-permute-done.1.refs_2_.refs_10_), channel_id=1, source_target_pairs={{0,4},{4,0},{8,12},{12,8},{16,20},{20,16},{24,28},{28,24},{1,5},{5... | collective-permute-start | bytes 3244040 | tf_op jit(solution)/shard_map/ppermute | solution.py:885
  41.4 25.4 %collective-permute-start.3 = (bf16[128,4096]{1,0:T(8,128)(2,1)}, bf16[128,4096]{1,0:T(8,128)(2,1)}, u32[]{:S(2)}, u32[]{:S(2)}) collective-permute-start(bf16[128,4096]{1,0:T(8,128)(2,1)} %refs_0_.4), channel_id=1, source_target_pairs={{0,8},{4,12},{8,0},{12,4},{16,24},{20,28},{24,16},{28,20},{1,9},{5... | collective-permute-start | bytes 3145736 | tf_op jit(solution)/shard_map/ppermute | solution.py:885
  41.9 236.1 %all-gather.5.cloned.1.call-start = ((), (), s32[]{:S(2)}) async-start(), calls=%async_computation.1 | async-start | bytes 5242880 | tf_op jit(solution)/shard_map/all_gather | solution.py:1002
  66.8 26.0 %collective-permute-start.10 = (bf16[128,4096]{1,0:T(8,128)(2,1)}, bf16[128,4096]{1,0:T(8,128)(2,1)S(1)}, u32[]{:S(2)}, u32[]{:S(2)}) collective-permute-start(bf16[128,4096]{1,0:T(8,128)(2,1)} %refs_0_.4), channel_id=1, source_target_pairs={{0,4},{4,0},{8,12},{12,8},{16,20},{20,16},{24,28},{28,24},{1,5},{5... | collective-permute-start | bytes 3145736 | tf_op jit(solution)/shard_map/ppermute | solution.py:885
  67.3 25.5 %collective-permute-start.11 = (bf16[128,4096]{1,0:T(8,128)(2,1)}, bf16[128,4096]{1,0:T(8,128)(2,1)S(1)}, u32[]{:S(2)}, u32[]{:S(2)}) collective-permute-start(bf16[128,4096]{1,0:T(8,128)(2,1)} %collective-permute-done.3.refs_1_), channel_id=1, source_target_pairs={{0,4},{4,0},{8,12},{12,8},{16,20},{20,16},{24,28},{28,24},{1,5},{5... | collective-permute-start | bytes 3145736 | tf_op jit(solution)/shard_map/ppermute | solution.py:885
  67.4 25.7 %collective-permute-start.8 = (bf16[128,4096]{1,0:T(8,128)(2,1)}, bf16[128,4096]{1,0:T(8,128)(2,1)S(1)}, u32[]{:S(2)}, u32[]{:S(2)}) collective-permute-start(bf16[128,4096]{1,0:T(8,128)(2,1)} %refs_0_.4), channel_id=1, source_target_pairs={{0,16},{4,20},{8,24},{12,28},{16,0},{20,4},{24,8},{28,12},{1,17},{... | collective-permute-start | bytes 3145736 | tf_op jit(solution)/shard_map/ppermute | solution.py:885
  67.9 25.5 %collective-permute-start.9 = (bf16[512,1024]{1,0:T(8,128)(2,1)}, bf16[512,1024]{1,0:T(8,128)(2,1)}, u32[]{:S(2)}, u32[]{:S(2)}) collective-permute-start(bf16[512,1024]{1,0:T(8,128)(2,1)} %refs_0_.3), channel_id=1, source_target_pairs={{0,8},{4,12},{8,0},{12,4},{16,24},{20,28},{24,16},{28,20},{1,9},{5... | collective-permute-start | bytes 3145736 | tf_op jit(solution)/shard_map/ppermute | solution.py:885
  93.5 24.7 %collective-permute-start.12 = (bf16[128,4096]{1,0:T(8,128)(2,1)S(1)}, bf16[128,4096]{1,0:T(8,128)(2,1)S(1)}, u32[]{:S(2)}, u32[]{:S(2)}) collective-permute-start(bf16[128,4096]{1,0:T(8,128)(2,1)S(1)} %collective-permute-done.8.refs_2_), channel_id=1, source_target_pairs={{0,8},{4,12},{8,0},{12,4},{16,24},{20,28},{24,16},{28,20},{1,9},{5... | collective-permute-start | bytes 3145736 | tf_op jit(solution)/shard_map/ppermute | solution.py:885
  93.8 24.6 %collective-permute-start.13 = (bf16[512,1024]{1,0:T(8,128)(2,1)S(1)}, bf16[512,1024]{1,0:T(8,128)(2,1)S(1)}, u32[]{:S(2)}, u32[]{:S(2)}) collective-permute-start(bf16[512,1024]{1,0:T(8,128)(2,1)S(1)} %copy-done.18), channel_id=1, source_target_pairs={{0,16},{4,20},{8,24},{12,28},{16,0},{20,4},{24,8},{28,12},{1,17},{... | collective-permute-start | bytes 3145736 | tf_op jit(solution)/shard_map/ppermute | solution.py:885
  95.5 22.9 %collective-permute-start.15 = (bf16[128,4096]{1,0:T(8,128)(2,1)S(1)}, bf16[128,4096]{1,0:T(8,128)(2,1)S(1)}, u32[]{:S(2)}, u32[]{:S(2)}) collective-permute-start(bf16[128,4096]{1,0:T(8,128)(2,1)S(1)} %collective-permute-done.8.refs_2_), channel_id=1, source_target_pairs={{0,4},{4,0},{8,12},{12,8},{16,20},{20,16},{24,28},{28,24},{1,5},{5... | collective-permute-start | bytes 3145736 | tf_op jit(solution)/shard_map/ppermute | solution.py:885
  141.7 26.4 %collective-permute-start.24 = (bf16[4,512,512]{2,1,0:T(8,128)(2,1)}, bf16[4,512,512]{2,1,0:T(8,128)(2,1)S(1)}, u32[]{:S(2)}, u32[]{:S(2)}) collective-permute-start(bf16[4,512,512]{2,1,0:T(8,128)(2,1)} %get-tuple-element.367), channel_id=1, source_target_pairs={{0,4},{4,0},{8,12},{12,8},{16,20},{20,16},{24,28},{28,24},{1,5},{5... | collective-permute-start | bytes 6291464 | tf_op jit(solution)/shard_map/ppermute | solution.py:885
  142.5 23.1 %collective-permute-start.25 = (bf16[2,4,512,128]{3,2,1,0:T(8,128)(2,1)}, bf16[2,4,512,128]{3,2,1,0:T(8,128)(2,1)S(1)}, u32[]{:S(2)}, u32[]{:S(2)}) collective-permute-start(bf16[2,4,512,128]{3,2,1,0:T(8,128)(2,1)} %get-tuple-element.368), channel_id=1, source_target_pairs={{0,4},{4,0},{8,12},{12,8},{16,20},{20,16},{24,28},{28,24},{1,5},{5... | collective-permute-start | bytes 3145736 | tf_op jit(solution)/shard_map/ppermute | solution.py:885
  180.2 32.6 %collective-permute-start.28 = (bf16[2,512,512]{2,1,0:T(8,128)(2,1)}, bf16[2,512,512]{2,1,0:T(8,128)(2,1)S(1)}, u32[]{:S(2)}, u32[]{:S(2)}) collective-permute-start(bf16[2,512,512]{2,1,0:T(8,128)(2,1)} %get-tuple-element.401), channel_id=1, source_target_pairs={{0,16},{4,20},{8,24},{12,28},{16,0},{20,4},{24,8},{28,12},{1,17},{... | collective-permute-start | bytes 3145736 | tf_op jit(solution)/shard_map/ppermute | solution.py:885
  182.3 30.5 %collective-permute-start.29 = (bf16[2,512,512]{2,1,0:T(8,128)(2,1)}, bf16[2,512,512]{2,1,0:T(8,128)(2,1)S(1)}, u32[]{:S(2)}, u32[]{:S(2)}) collective-permute-start(bf16[2,512,512]{2,1,0:T(8,128)(2,1)} %get-tuple-element.402), channel_id=1, source_target_pairs={{0,8},{4,12},{8,0},{12,4},{16,24},{20,28},{24,16},{28,20},{1,9},{5... | collective-permute-start | bytes 3145736 | tf_op jit(solution)/shard_map/ppermute | solution.py:885
  212.8 36.5 %collective-permute-start.30 = (bf16[2,128,2048]{2,1,0:T(8,128)(2,1)}, bf16[2,128,2048]{2,1,0:T(8,128)(2,1)S(1)}, u32[]{:S(2)}, u32[]{:S(2)}) collective-permute-start(bf16[2,128,2048]{2,1,0:T(8,128)(2,1)} %get-tuple-element.424), channel_id=1, source_target_pairs={{0,16},{4,20},{8,24},{12,28},{16,0},{20,4},{24,8},{28,12},{1,17},{... | collective-permute-start | bytes 3145736 | tf_op jit(solution)/shard_map/ppermute | solution.py:885
  212.9 37.4 %collective-permute-start.31 = (bf16[2,128,2048]{2,1,0:T(8,128)(2,1)}, bf16[2,128,2048]{2,1,0:T(8,128)(2,1)S(1)}, u32[]{:S(2)}, u32[]{:S(2)}) collective-permute-start(bf16[2,128,2048]{2,1,0:T(8,128)(2,1)} %get-tuple-element.425), channel_id=1, source_target_pairs={{0,8},{4,12},{8,0},{12,4},{16,24},{20,28},{24,16},{28,20},{1,9},{5... | collective-permute-start | bytes 3145736 | tf_op jit(solution)/shard_map/ppermute | solution.py:885
  215.1 34.1 %collective-permute-start.32 = (bf16[512,512]{1,0:T(8,128)(2,1)}, bf16[512,512]{1,0:T(8,128)(2,1)S(1)}, u32[]{:S(2)}, u32[]{:S(2)}) collective-permute-start(bf16[512,512]{1,0:T(8,128)(2,1)} %fusion.11), channel_id=1, source_target_pairs={{0,8},{4,12},{8,0},{12,4},{16,24},{20,28},{24,16},{28,20},{1,9},{5... | collective-permute-start | bytes 1572872 | tf_op jit(solution)/shard_map/ppermute | solution.py:885
  216.9 32.4 %collective-permute-start.33 = (bf16[512,512]{1,0:T(8,128)(2,1)}, bf16[512,512]{1,0:T(8,128)(2,1)}, u32[]{:S(2)}, u32[]{:S(2)}) collective-permute-start(bf16[512,512]{1,0:T(8,128)(2,1)} %fusion.10), channel_id=1, source_target_pairs={{0,16},{4,20},{8,24},{12,28},{16,0},{20,4},{24,8},{28,12},{1,17},{... | collective-permute-start | bytes 1572872 | tf_op jit(solution)/shard_map/ppermute | solution.py:885
  280.2 23.0 %collective-permute-start.50 = (bf16[128,2048]{1,0:T(8,128)(2,1)S(1)}, bf16[128,2048]{1,0:T(8,128)(2,1)S(1)}, u32[]{:S(2)}, u32[]{:S(2)}) collective-permute-start(bf16[128,2048]{1,0:T(8,128)(2,1)S(1)} %get-tuple-element.513), channel_id=1, source_target_pairs={{0,1},{1,0},{2,3},{3,2},{4,5},{5,4},{6,7},{7,6},{8,9},{9,8},{10,11... | collective-permute-start | bytes 1572872 | tf_op jit(solution)/shard_map/ppermute | solution.py:920
  284.2 24.9 %collective-permute-start.49 = (bf16[512,512]{1,0:T(8,128)(2,1)S(1)}, bf16[512,512]{1,0:T(8,128)(2,1)S(1)}, u32[]{:S(2)}, u32[]{:S(2)}) collective-permute-start(bf16[512,512]{1,0:T(8,128)(2,1)S(1)} %add_convert_fusion.3), channel_id=1, source_target_pairs={{0,2},{1,3},{2,0},{3,1},{4,6},{5,7},{6,4},{7,5},{8,10},{9,11},{10,... | collective-permute-start | bytes 1572872 | tf_op jit(solution)/shard_map/ppermute | solution.py:920
  286.8 24.4 %collective-permute-start.42 = (bf16[2,272,512]{2,1,0:T(8,128)(2,1)S(1)}, bf16[2,272,512]{2,1,0:T(8,128)(2,1)S(1)}, u32[]{:S(2)}, u32[]{:S(2)}) collective-permute-start(bf16[2,272,512]{2,1,0:T(8,128)(2,1)S(1)} %copy-done.52), channel_id=1, source_target_pairs={{0,16},{4,20},{8,24},{12,28},{16,0},{20,4},{24,8},{28,12},{1,17},{... | collective-permute-start | bytes 1671176 | tf_op jit(solution)/shard_map/ppermute | solution.py:885
  313.7 22.9 %collective-permute-start.51 = (bf16[128,2048]{1,0:T(8,128)(2,1)S(1)}, bf16[128,2048]{1,0:T(8,128)(2,1)S(1)}, u32[]{:S(2)}, u32[]{:S(2)}) collective-permute-start(bf16[128,2048]{1,0:T(8,128)(2,1)S(1)} %add_convert_fusion.1), channel_id=1, source_target_pairs={{0,2},{1,3},{2,0},{3,1},{4,6},{5,7},{6,4},{7,5},{8,10},{9,11},{10,... | collective-permute-start | bytes 1572872 | tf_op jit(solution)/shard_map/ppermute | solution.py:920
  317.2 27.8 %collective-permute-start.52 = (bf16[512,512]{1,0:T(8,128)(2,1)S(1)}, bf16[512,512]{1,0:T(8,128)(2,1)S(1)}, u32[]{:S(2)}, u32[]{:S(2)}) collective-permute-start(bf16[512,512]{1,0:T(8,128)(2,1)S(1)} %add_convert_fusion.2), channel_id=1, source_target_pairs={{0,1},{1,0},{2,3},{3,2},{4,5},{5,4},{6,7},{7,6},{8,9},{9,8},{10,11... | collective-permute-start | bytes 1572872 | tf_op jit(solution)/shard_map/ppermute | solution.py:920
  319.2 34.4 %collective-permute-start.46 = (bf16[256,512]{1,0:T(8,128)(2,1)S(1)}, bf16[256,512]{1,0:T(8,128)(2,1)S(1)}, u32[]{:S(2)}, u32[]{:S(2)}) collective-permute-start(bf16[256,512]{1,0:T(8,128)(2,1)S(1)} %get-tuple-element.510), channel_id=1, source_target_pairs={{0,1},{1,0},{2,3},{3,2},{4,5},{5,4},{6,7},{7,6},{8,9},{9,8},{10,11... | collective-permute-start | bytes 786440 | tf_op jit(solution)/shard_map/ppermute | solution.py:920
  321.9 37.8 %collective-permute-start.56 = (bf16[272,512]{1,0:T(8,128)(2,1)S(1)}, bf16[272,512]{1,0:T(8,128)(2,1)S(1)}, u32[]{:S(2)}, u32[]{:S(2)}) collective-permute-start(bf16[272,512]{1,0:T(8,128)(2,1)S(1)} %get-tuple-element.531), channel_id=1, source_target_pairs={{0,1},{1,0},{2,3},{3,2},{4,5},{5,4},{6,7},{7,6},{8,9},{9,8},{10,11... | collective-permute-start | bytes 835592 | tf_op jit(solution)/shard_map/ppermute | solution.py:920
  356.1 22.3 %collective-permute-start.53 = (bf16[128,2048]{1,0:T(8,128)(2,1)S(1)}, bf16[128,2048]{1,0:T(8,128)(2,1)S(1)}, u32[]{:S(2)}, u32[]{:S(2)}) collective-permute-start(bf16[128,2048]{1,0:T(8,128)(2,1)S(1)} %add_convert_fusion), channel_id=1, source_target_pairs={{0,1},{1,0},{2,3},{3,2},{4,5},{5,4},{6,7},{7,6},{8,9},{9,8},{10,11... | collective-permute-start | bytes 1572872 | tf_op jit(solution)/shard_map/ppermute | solution.py:920
  (84 other events, 916.8 us)
Sparse Core Ops, SparseCore 0:
  42.0 81.0 all-gather.2
  169.6 83.5 all-gather.4

commit v4 on v3

--- a/solution.py
+++ b/solution.py
@@ -878,6 +878,22 @@
     )(*weights, *[part.reshape(1, -1) for part in small])
 
 
+def chosen(meta, pool, first):
+    rows, width = pool.shape[1:]
+
+    def kernel(meta, pool_ref, out_ref):
+        out_ref[...] = pool_ref[...]
+
+    return call(
+        kernel,
+        (2,),
+        [spec((1, rows, width), lambda i, meta: (meta[first + i], 0, 0))],
+        spec((1, rows, width), lambda i, meta: (i, 0, 0)),
+        sds((2, rows, width), BF16),
+        [],
+    )(meta, pool)
+
+
 CORE, ALONG_X, ALONG_Y = 1, 2, 4
 
 
@@ -936,6 +952,36 @@
     odd = lax.axis_index("rep") % 2 == 1
     first, second = plus(own[0], got[0][0], late[0]), plus(own[1], got[1][0], late[1])
     return jnp.where(odd, second, first), jnp.where(odd, first, second)
+
+
+def merge(meta, own, got, late, rest, got_next):
+    rows, cols = own[0].shape
+    high, wide = rest[0].shape
+    steps = 4
+
+    def kernel(meta, own_a, own_b, got_a, got_b, late_a, late_b, rest_a, rest_b, next_a, next_b, *outs):
+        kept_ref, given_ref, pass_a, pass_b = outs
+        first = own_a[...].astype(F32) + got_a[0].astype(F32) + late_a[...].astype(F32)
+        second = own_b[...].astype(F32) + got_b[0].astype(F32) + late_b[...].astype(F32)
+        odd = meta[7] == 1
+        kept_ref[...] = jnp.where(odd, second, first).astype(BF16)
+        given_ref[...] = jnp.where(odd, first, second).astype(BF16)
+        pass_a[...] = (rest_a[...].astype(F32) + next_a[0].astype(F32)).astype(BF16)
+        pass_b[...] = (rest_b[...].astype(F32) + next_b[0].astype(F32)).astype(BF16)
+
+    flat = spec((rows // steps, cols), lambda i, meta: (i, 0))
+    mine = spec((1, rows // steps, cols), lambda i, meta: (0, i, 0))
+    low = spec((high // steps, wide), lambda i, meta: (i, 0))
+    other = spec((1, high // steps, wide), lambda i, meta: (1, i, 0))
+    kept, given, *passing = call(
+        kernel,
+        (steps,),
+        [flat, flat, mine, mine, flat, flat, low, low, other, other],
+        [flat, flat, low, low],
+        [sds((rows, cols), BF16)] * 2 + [sds((high, wide), BF16)] * 2,
+        [],
+    )(meta, *own, *got, *late, *rest, *got_next)
+    return kept, given, tuple(passing)
 
 
 def unfolded(mine, other):
@@ -960,7 +1006,7 @@
     wanted = jnp.sum(
         jnp.where(local_dealing[None, :] == (slots - anchor)[:, None], places[None, :], 0), 1
     )
-    meta = jnp.concatenate([shard_index[None].astype(jnp.int32), jnp.take(lengths, slots), wanted])
+    meta = jnp.concatenate([shard_index[None].astype(jnp.int32), jnp.take(lengths, slots), wanted, jnp.clip(sources, 0, group - 1), (lax.axis_index("rep") % 2)[None].astype(jnp.int32)])
     order = Order(meta)
     tokens = inputs.reshape(total, width)
 
@@ -982,11 +1028,12 @@
     up_c.append(swap(up_y, CORE))
     tokens_got = swap(tokens_give, CORE)
     unit_one, inverse_one, hidden_low, both_give = order.then(mix_out(order.meta, mixed, tokens, first, vecs))
-    up_far, down_y, tokens_got, both_give, *up_c = order.then((up_far, down_y, tokens_got, both_give, *up_c))
+    to_top = order.then(down_x[:256])
+    up_far, down_y, tokens_got, both_give, to_top, *up_c = order.then((up_far, down_y, tokens_got, both_give, to_top, *up_c))
     up = (w_up, up_x, up_y, up_far, *up_c, swap(up_far, CORE))
-    down_top, down_end = swap(down_x[:256], ALONG_Y), swap(down_y[256:], ALONG_X)
-    up = order.then(up)
-    down_c = [swap(part, CORE) for part in (w_down, down_x, down_y)]
+    down_top, down_end = swap(to_top, ALONG_Y), swap(down_y[256:], ALONG_X)
+    up, *to_core = order.then((up, w_down, down_x, down_y))
+    down_c = [swap(part, CORE) for part in to_core]
     act, slope, act_give = order.then(feed_up(order.meta, hidden_low, up, bias_up))
     down_top, down_end, act_give, both_give, *down_c = order.then((down_top, down_end, act_give, both_give, *down_c))
     down = (w_down, down_x, down_y, down_top, down_end) + tuple(down_c)
@@ -1018,8 +1065,9 @@
     grad_input = order.then(back_project(order.meta, grads, first, grad_resid))
     got_up, late_down, resid_low, grads, vec = order.then((got_up, late_down, resid_low, grads, vec))
     resid_got, grads_got, vec_got = swap(resid_low, CORE), swap(grads, CORE), swap(vec, CORE)
-    pass_up = order.then(turned(rest_up, got_up))
-    kept_down, given_down = order.then(summed(own_down, got_down, late_down))
+    kept_down, given_down, pass_up = order.then(
+        merge(order.meta, own_down, got_down, late_down, rest_up, got_up)
+    )
     resid_got, grads_got, vec_got, pass_up, given_down = order.then((resid_got, grads_got, vec_got, pass_up, given_down))
     late_up, taken_down = passed(pass_up), pairs(given_down, 1)
     (far_a, own_a, rest_a), (far_b, own_b, rest_b) = order.then(
@@ -1036,7 +1084,7 @@
     got_a = order.then(got_a)
     late_a = passed(order.then(turned(rest_a, got_a)))
     taken_up = pairs(given_up, 1)
-    layer_out = order.then(pick(out_pool, sources))
+    layer_out = order.then(chosen(order.meta, out_pool, 5))
     got_b = order.then(got_b)
     late_b = passed(order.then(turned(rest_b, got_b)))
     late_a = order.then(late_a)

time: 393 us -> 390 us (level)
  other arithmetic: 20.7 us -> 10.2 us
  waiting for transfers between devices: 136 us -> 145 us
  Pallas kernels: 142 us -> 150 us
  between operations: 18.8 us -> 14.8 us
    ppermute x12, waiting for transfers between devices: 53.9 us -> 63.2 us  [pairs(): return lax.ppermute(value, 'rep', [(i, i ^ mask) for i in range(4)])]
    pallas_call x11 -> x13, Pallas kernels: 139 us -> 147 us  [run(): pl.pallas_call(kernel, grid_spec=pltpu.PrefetchScalarGridSpec(num_scalar_...]
    convert_element_type x16 -> x14, other arithmetic: 8.89 us -> 2.57 us  [plus(): return total.astype(BF16)]
  transfers between devices with their start and end apart: 61 -> 61, of which waited for: 26 -> 27; matrix products, arithmetic and copies ran while one was open for 6% -> 3% of each run, Pallas kernels for 36% -> 38%
where the time goes in v4:
time: 390 us; the launch traced here: 389 us
  Pallas kernels  150 us (38%)
  waiting for transfers between devices  145 us (37%)
  starting transfers between devices  56.3 us (14%)
  between operations  14.8 us (4%)
  local copies, waits for them, and re-layouts  12.8 us (3%)
  other arithmetic  10.2 us (3%)
    pallas_call x13, Pallas kernels, run(): pl.pallas_call(kernel, grid_spec=pltpu.PrefetchScalarGridSpec(num_scalar_...  147 us
    ppermute x47, waiting for transfers between devices, swap(): return lax.ppermute(value, 'shard', [(i, i ^ mask) for i in range(8)])  81.8 us
    ppermute x12, waiting for transfers between devices, pairs(): return lax.ppermute(value, 'rep', [(i, i ^ mask) for i in range(4)])  63.2 us
    ppermute x47, starting transfers between devices, swap(): return lax.ppermute(value, 'shard', [(i, i ^ mask) for i in range(8)])  39 us
    ppermute x12, starting transfers between devices, pairs(): return lax.ppermute(value, 'rep', [(i, i ^ mask) for i in range(4)])  17.3 us
  transfers between devices with their start and end apart: 61, of which 27 were waited for; matrix products, arithmetic and copies ran while one was open for 3% of the time, Pallas kernels for 38%

profile of v4, /device:TPU:0, one launch (start us, length us, event | category | flops | bytes accessed | tf_op | source)
XLA Modules:
  0.0 388.9 jit_solution(11930122502623131997)
XLA Ops:
  10.8 3.0 collective-permute-start.1
  17.5 20.4 %collective-permute-done.1.refs_2_.refs_10_ = bf16[528,1024]{1,0:T(8,128)(2,1)S(1)} collective-permute-done((bf16[528,1024]{1,0:T(8,128)(2,1)}, bf16[528,1024]{1,0:T(8,128)(2,1)S(1)}, u32[]{:S(2)}, u32[]{:S(2)}) %collective-permute-start.1) | collective-permute-done | bytes 1081376 | tf_op jit(solution)/shard_map/ppermute | solution.py:901
  42.0 23.4 %collective-permute-done.3.refs_1_ = bf16[128,4096]{1,0:T(8,128)(2,1)} collective-permute-done((bf16[128,4096]{1,0:T(8,128)(2,1)}, bf16[128,4096]{1,0:T(8,128)(2,1)}, u32[]{:S(2)}, u32[]{:S(2)}) %collective-permute-start.3) | collective-permute-done | bytes 1048608 | tf_op jit(solution)/shard_map/ppermute | solution.py:901
  70.1 11.2 %shard_map.315 = (bf16[3,512,1024]{2,1,0:T(8,128)(2,1)}, f32[8,1024]{1,0:T(8,128)}, f32[1,4096]{1,0:T(1,128)}, bf16[4,512,128]{2,1,0:T(8,128)(2,1)}) custom-call(s32[8]{0:T(128)} %concatenate.24.meta, bf16[512,1024]{1,0:T(8,128)(2,1)} %bitcast.90, bf16[528,1024]{1,0:T(8,128)(2,1)} %shard_map.314.refs_0_.refs_8_, bf16[528,1024]{1,0:T(8,128)(2,1)} %copy-done.4, ...), custom_call_target="tpu_custom_call" | custom-call | flops 1024 | bytes 1024 | tf_op jit(solution)/shard_map/pallas_call | solution.py:89
  81.3 10.8 %shard_map.316 = (bf16[512,1024]{1,0:T(8,128)(2,1)}, bf16[2,16,256,256]{3,2,1,0:T(8,128)(2,1)}, f32[512,1024]{1,0:T(8,128)}) custom-call(s32[8]{0:T(128)} %concatenate.24.meta, bf16[3,512,1024]{2,1,0:T(8,128)(2,1)} %get-tuple-element.299.q_ref.k_ref.v_ref, bf16[3,512,1024]{2,1,0:T(8,128)(2,1)} %get-tuple-element.299.q_ref.k_ref.v_ref, ...), custom_call_target="tpu_custom_call" | custom-call | flops 1024 | bytes 1024 | tf_op jit(solution)/shard_map/pallas_call | solution.py:89
  95.2 9.4 %shard_map.317 = (f32[512,1024]{1,0:T(8,128)}, f32[512,128]{1,0:T(8,128)}, bf16[512,1024]{1,0:T(8,128)(2,1)}, bf16[2,4,512,128]{3,2,1,0:T(8,128)(2,1)}) custom-call(s32[8]{0:T(128)} %concatenate.24.meta, bf16[512,1024]{1,0:T(8,128)(2,1)} %get-tuple-element.309.mixed_ref.m_ref, bf16[512,1024]{1,0:T(8,128)(2,1)} %bitcast.91, ...), custom_call_target="tpu_custom_call" | custom-call | flops 1024 | bytes 1024 | tf_op jit(solution)/shard_map/pallas_call | solution.py:89
  106.4 11.4 %collective-permute-done.13.refs_2_ = bf16[512,1024]{1,0:T(8,128)(2,1)S(1)} collective-permute-done((bf16[512,1024]{1,0:T(8,128)(2,1)S(1)}, bf16[512,1024]{1,0:T(8,128)(2,1)S(1)}, u32[]{:S(2)}, u32[]{:S(2)}) %collective-permute-start.13) | collective-permute-done | bytes 1048608 | tf_op jit(solution)/shard_map/ppermute | solution.py:901
  119.0 2.7 collective-permute-done.16.refs_7_
  126.1 13.7 %shard_map.318 = (bf16[512,4096]{1,0:T(8,128)(2,1)}, bf16[512,4096]{1,0:T(8,128)(2,1)}, bf16[4,512,512]{2,1,0:T(8,128)(2,1)}) custom-call(s32[8]{0:T(128)} %concatenate.24.meta, bf16[512,1024]{1,0:T(8,128)(2,1)} %get-tuple-element.332.x_ref, f32[1,4096]{1,0:T(1,128)} %get-tuple-element.333.bias_ref, bf16[128,4096]{1,0:T(8,128)(2,1)} %refs_0_.4, ...), custom_call_target="tpu_custom_call" | custom-call | flops 1024 | bytes 1024 | tf_op jit(solution)/shard_map/pallas_call | solution.py:89
  143.6 21.9 %shard_map.319 = (bf16[512,1024]{1,0:T(8,128)(2,1)}, f32[512,1024]{1,0:T(8,128)}, bf16[512,1024]{1,0:T(8,128)(2,1)}, f32[8,1024]{1,0:T(8,128)}, bf16[512,4096]{1,0:T(8,128)(2,1)}, /*index=5*/f32[1,4096]{1,0:T(1,128)}) custom-call(s32[8]{0:T(128)} %concatenate.24.meta, bf16[512,4096]{1,0:T(8,128)(2,1)} %get-tuple-element.361.act_ref.left_ref, ...), custom_call_target="tpu_custom_call" | custom-call | flops 1024 | bytes 1024 | tf_op jit(solution)/shard_map/pallas_call | solution.py:89
  166.6 3.0 collective-permute-done.26.right_got
  172.0 9.6 %shard_map.320 = (bf16[2,512,512]{2,1,0:T(8,128)(2,1)}, bf16[2,512,512]{2,1,0:T(8,128)(2,1)}, bf16[512,512]{1,0:T(8,128)(2,1)}, bf16[512,512]{1,0:T(8,128)(2,1)}...) custom-call(s32[8]{0:T(128)} %concatenate.24.meta, bf16[512,4096]{1,0:T(8,128)(2,1)} %get-tuple-element.361.act_ref.left_ref, ...), custom_call_target="tpu_custom_call" | custom-call | flops 1024 | bytes 1024 | tf_op jit(solution)/shard_map/pallas_call | solution.py:89
  185.8 16.8 %shard_map.321 = (f32[512,1024]{1,0:T(8,128)}, bf16[512,1024]{1,0:T(8,128)(2,1)}, bf16[512,1024]{1,0:T(8,128)(2,1)}, f32[8,1024]{1,0:T(8,128)}) custom-call(s32[8]{0:T(128)} %concatenate.24.meta, bf16[512,4096]{1,0:T(8,128)(2,1)} %get-tuple-element.396.pre_ref, f32[512,1024]{1,0:T(8,128)} %get-tuple-element.400.sum_ref, ...), custom_call_target="tpu_custom_call" | custom-call | flops 1024 | bytes 1024 | tf_op jit(solution)/shard_map/pallas_call | solution.py:89
  202.6 11.1 %shard_map.322 = (bf16[2,128,2048]{2,1,0:T(8,128)(2,1)}, bf16[2,128,2048]{2,1,0:T(8,128)(2,1)}, bf16[128,2048]{1,0:T(8,128)(2,1)}, bf16[128,2048]{1,0:T(8,128)(2...) custom-call(s32[8]{0:T(128)} %concatenate.24.meta, bf16[512,1024]{1,0:T(8,128)(2,1)} %get-tuple-element.332.x_ref, ...), custom_call_target="tpu_custom_call" | custom-call | flops 1024 | bytes 1024 | tf_op jit(solution)/shard_map/pallas_call | solution.py:89
  218.3 14.7 %shard_map.323 = (bf16[3,512,1024]{2,1,0:T(8,128)(2,1)}, bf16[8,16,1024]{2,1,0:T(8,128)(2,1)}) custom-call(s32[8]{0:T(128)} %concatenate.24.meta, bf16[3,512,1024]{2,1,0:T(8,128)(2,1)} %get-tuple-element.299.q_ref.k_ref.v_ref, bf16[3,512,1024]{2,1,0:T(8,128)(2,1)} %get-tuple-element.299.q_ref.k_ref.v_ref, ...), custom_call_target="tpu_custom_call" | custom-call | flops 1024 | bytes 1024 | tf_op jit(solution)/shard_map/pallas_call | solution.py:89
  233.0 10.7 %shard_map.324 = bf16[512,1024]{1,0:T(8,128)(2,1)} custom-call(s32[8]{0:T(128)} %concatenate.24.meta, bf16[3,512,1024]{2,1,0:T(8,128)(2,1)} %get-tuple-element.460.g_ref, f32[512,1024]{1,0:T(8,128)} %get-tuple-element.437.resid_ref, bf16[528,1024]{1,0:T(8,128)(2,1)} %shard_map.314.refs_0_.refs_8_, bf16[528,1024]{1,0:T(8,128)(2,1)} %copy-done.4, ...), custom_call_target="tpu_custom_call" | custom-call | flops 1024 | bytes 1024 | tf_op jit(solution)/shard_map/pallas_call | solution.py:89
  243.7 6.5 %collective-permute-done.32.late_a = bf16[512,512]{1,0:T(8,128)(2,1)S(1)} collective-permute-done((bf16[512,512]{1,0:T(8,128)(2,1)S(1)}, bf16[512,512]{1,0:T(8,128)(2,1)S(1)}, u32[]{:S(2)}, u32[]{:S(2)}) %collective-permute-start.32) | collective-permute-done | bytes 524320 | tf_op jit(solution)/shard_map/ppermute | solution.py:901
  251.8 5.2 %shard_map.325 = (bf16[512,512]{1,0:T(8,128)(2,1)}, bf16[512,512]{1,0:T(8,128)(2,1)}, bf16[128,2048]{1,0:T(8,128)(2,1)}, bf16[128,2048]{1,0:T(8,128)(2,1)}) custom-call(s32[8]{0:T(128)} %concatenate.24.meta, bf16[512,512]{1,0:T(8,128)(2,1)} %get-tuple-element.446.own_a, bf16[512,512]{1,0:T(8,128)(2,1)} %get-tuple-element.447.own_b, ...), custom_call_target="tpu_custom_call" | custom-call | flops 1024 | bytes 1024 | tf_op jit(solution)/shard_map/pallas_call | solution.py:89
  262.9 9.6 %shard_map.326 = (bf16[2,256,512]{2,1,0:T(8,128)(2,1)}, bf16[2,256,512]{2,1,0:T(8,128)(2,1)}, bf16[256,512]{1,0:T(8,128)(2,1)}, bf16[256,512]{1,0:T(8,128)(2,1)}...) custom-call(s32[8]{0:T(128)} %concatenate.24.meta, ...), custom_call_target="tpu_custom_call" | custom-call | flops 1024 | bytes 1024 | tf_op jit(solution)/shard_map/pallas_call | solution.py:89
  278.6 2.4 broadcast_select_fusion.4
  282.6 2.6 collective-permute-start.49
  286.9 4.7 %collective-permute-done.40 = bf16[2,256,512]{2,1,0:T(8,128)(2,1)S(1)} collective-permute-done((bf16[2,256,512]{2,1,0:T(8,128)(2,1)}, bf16[2,256,512]{2,1,0:T(8,128)(2,1)S(1)}, u32[]{:S(2)}, u32[]{:S(2)}) %collective-permute-start.40) | collective-permute-done | bytes 524320 | tf_op jit(solution)/shard_map/ppermute | solution.py:901
  293.5 10.9 %collective-permute-done.50 = bf16[128,2048]{1,0:T(8,128)(2,1)S(1)} collective-permute-done((bf16[128,2048]{1,0:T(8,128)(2,1)S(1)}, bf16[128,2048]{1,0:T(8,128)(2,1)S(1)}, u32[]{:S(2)}, u32[]{:S(2)}) %collective-permute-start.50) | collective-permute-done | bytes 524320 | tf_op jit(solution)/shard_map/ppermute | solution.py:936
  311.7 2.7 shard_map.327
  314.5 2.8 collective-permute-start.52
  319.9 11.9 %collective-permute-done.51 = bf16[128,2048]{1,0:T(8,128)(2,1)S(1)} collective-permute-done((bf16[128,2048]{1,0:T(8,128)(2,1)S(1)}, bf16[128,2048]{1,0:T(8,128)(2,1)S(1)}, u32[]{:S(2)}, u32[]{:S(2)}) %collective-permute-start.51) | collective-permute-done | bytes 524320 | tf_op jit(solution)/shard_map/ppermute | solution.py:936
  331.8 9.4 %collective-permute-done.52 = bf16[512,512]{1,0:T(8,128)(2,1)S(1)} collective-permute-done((bf16[512,512]{1,0:T(8,128)(2,1)S(1)}, bf16[512,512]{1,0:T(8,128)(2,1)S(1)}, u32[]{:S(2)}, u32[]{:S(2)}) %collective-permute-start.52) | collective-permute-done | bytes 524320 | tf_op jit(solution)/shard_map/ppermute | solution.py:936
  341.4 8.9 %collective-permute-done.46 = bf16[256,512]{1,0:T(8,128)(2,1)S(1)} collective-permute-done((bf16[256,512]{1,0:T(8,128)(2,1)S(1)}, bf16[256,512]{1,0:T(8,128)(2,1)S(1)}, u32[]{:S(2)}, u32[]{:S(2)}) %collective-permute-start.46) | collective-permute-done | bytes 262176 | tf_op jit(solution)/shard_map/ppermute | solution.py:936
  351.5 4.9 %collective-permute-done.56 = bf16[272,512]{1,0:T(8,128)(2,1)S(1)} collective-permute-done((bf16[272,512]{1,0:T(8,128)(2,1)S(1)}, bf16[272,512]{1,0:T(8,128)(2,1)S(1)}, u32[]{:S(2)}, u32[]{:S(2)}) %collective-permute-start.56) | collective-permute-done | bytes 278560 | tf_op jit(solution)/shard_map/ppermute | solution.py:936
  357.9 4.3 %collective-permute-done.47 = bf16[256,512]{1,0:T(8,128)(2,1)S(1)} collective-permute-done((bf16[256,512]{1,0:T(8,128)(2,1)S(1)}, bf16[256,512]{1,0:T(8,128)(2,1)S(1)}, u32[]{:S(2)}, u32[]{:S(2)}) %collective-permute-start.47) | collective-permute-done | bytes 262176 | tf_op jit(solution)/shard_map/ppermute | solution.py:936
  364.0 6.9 %collective-permute-done.57 = bf16[272,512]{1,0:T(8,128)(2,1)S(1)} collective-permute-done((bf16[272,512]{1,0:T(8,128)(2,1)S(1)}, bf16[272,512]{1,0:T(8,128)(2,1)S(1)}, u32[]{:S(2)}, u32[]{:S(2)}) %collective-permute-start.57) | collective-permute-done | bytes 278560 | tf_op jit(solution)/shard_map/ppermute | solution.py:936
  370.9 3.6 collective-permute-start.58
  (240 shorter events, 83.2 us)
Async XLA Ops:
  7.2 135.8 %all-gather.3.cloned.1.call-start = ((), (), s32[]{:S(2)}) async-start(), calls=%async_computation | async-start | bytes 5242880 | tf_op jit(solution)/shard_map/all_gather | solution.py:1023
  10.8 27.0 %collective-permute-start.1 = (bf16[528,1024]{1,0:T(8,128)(2,1)}, bf16[528,1024]{1,0:T(8,128)(2,1)S(1)}, u32[]{:S(2)}, u32[]{:S(2)}) collective-permute-start(bf16[528,1024]{1,0:T(8,128)(2,1)} %shard_map.314.refs_0_.refs_8_), channel_id=1, source_target_pairs={{0,16},{4,20},{8,24},{12,28},{16,0},{20,4},{24,8},{28,12},{1,17},{... | collective-permute-start | bytes 3244040 | tf_op jit(solution)/shard_map/ppermute | solution.py:901
  13.8 25.5 %collective-permute-start = (bf16[528,1024]{1,0:T(8,128)(2,1)}, bf16[528,1024]{1,0:T(8,128)(2,1)S(1)}, u32[]{:S(2)}, u32[]{:S(2)}) collective-permute-start(bf16[528,1024]{1,0:T(8,128)(2,1)} %shard_map.314.refs_0_.refs_8_), channel_id=1, source_target_pairs={{0,8},{4,12},{8,0},{12,4},{16,24},{20,28},{24,16},{28,20},{1,9},{5... | collective-permute-start | bytes 3244040 | tf_op jit(solution)/shard_map/ppermute | solution.py:901
  15.3 26.6 %collective-permute-start.4 = (bf16[528,1024]{1,0:T(8,128)(2,1)}, bf16[528,1024]{1,0:T(8,128)(2,1)S(1)}, u32[]{:S(2)}, u32[]{:S(2)}) collective-permute-start(bf16[528,1024]{1,0:T(8,128)(2,1)} %shard_map.314.refs_0_.refs_8_), channel_id=1, source_target_pairs={{0,4},{4,0},{8,12},{12,8},{16,20},{20,16},{24,28},{28,24},{1,5},{5... | collective-permute-start | bytes 3244040 | tf_op jit(solution)/shard_map/ppermute | solution.py:901
  39.3 26.0 %collective-permute-start.6 = (bf16[528,1024]{1,0:T(8,128)(2,1)S(1)}, bf16[528,1024]{1,0:T(8,128)(2,1)}, u32[]{:S(2)}, u32[]{:S(2)}) collective-permute-start(bf16[528,1024]{1,0:T(8,128)(2,1)S(1)} %collective-permute-done.1.refs_2_.refs_10_), channel_id=1, source_target_pairs={{0,4},{4,0},{8,12},{12,8},{16,20},{20,16},{24,28},{28,24},{1,5},{5... | collective-permute-start | bytes 3244040 | tf_op jit(solution)/shard_map/ppermute | solution.py:901
  39.4 26.0 %collective-permute-start.5 = (bf16[528,1024]{1,0:T(8,128)(2,1)S(1)}, bf16[528,1024]{1,0:T(8,128)(2,1)}, u32[]{:S(2)}, u32[]{:S(2)}) collective-permute-start(bf16[528,1024]{1,0:T(8,128)(2,1)S(1)} %collective-permute-done.refs_1_.refs_9_), channel_id=1, source_target_pairs={{0,4},{4,0},{8,12},{12,8},{16,20},{20,16},{24,28},{28,24},{1,5},{5... | collective-permute-start | bytes 3244040 | tf_op jit(solution)/shard_map/ppermute | solution.py:901
  39.9 25.9 %collective-permute-start.2 = (bf16[528,1024]{1,0:T(8,128)(2,1)S(1)}, bf16[528,1024]{1,0:T(8,128)(2,1)}, u32[]{:S(2)}, u32[]{:S(2)}) collective-permute-start(bf16[528,1024]{1,0:T(8,128)(2,1)S(1)} %collective-permute-done.refs_1_.refs_9_), channel_id=1, source_target_pairs={{0,16},{4,20},{8,24},{12,28},{16,0},{20,4},{24,8},{28,12},{1,17},{... | collective-permute-start | bytes 3244040 | tf_op jit(solution)/shard_map/ppermute | solution.py:901
  40.2 25.2 %collective-permute-start.3 = (bf16[128,4096]{1,0:T(8,128)(2,1)}, bf16[128,4096]{1,0:T(8,128)(2,1)}, u32[]{:S(2)}, u32[]{:S(2)}) collective-permute-start(bf16[128,4096]{1,0:T(8,128)(2,1)} %refs_0_.4), channel_id=1, source_target_pairs={{0,8},{4,12},{8,0},{12,4},{16,24},{20,28},{24,16},{28,20},{1,9},{5... | collective-permute-start | bytes 3145736 | tf_op jit(solution)/shard_map/ppermute | solution.py:901
  41.9 230.6 %all-gather.5.cloned.1.call-start = ((), (), s32[]{:S(2)}) async-start(), calls=%async_computation.1 | async-start | bytes 5242880 | tf_op jit(solution)/shard_map/all_gather | solution.py:1049
  65.7 26.4 %collective-permute-start.10 = (bf16[128,4096]{1,0:T(8,128)(2,1)}, bf16[128,4096]{1,0:T(8,128)(2,1)S(1)}, u32[]{:S(2)}, u32[]{:S(2)}) collective-permute-start(bf16[128,4096]{1,0:T(8,128)(2,1)} %refs_0_.4), channel_id=1, source_target_pairs={{0,4},{4,0},{8,12},{12,8},{16,20},{20,16},{24,28},{28,24},{1,5},{5... | collective-permute-start | bytes 3145736 | tf_op jit(solution)/shard_map/ppermute | solution.py:901
  66.2 25.9 %collective-permute-start.8 = (bf16[128,4096]{1,0:T(8,128)(2,1)}, bf16[128,4096]{1,0:T(8,128)(2,1)S(1)}, u32[]{:S(2)}, u32[]{:S(2)}) collective-permute-start(bf16[128,4096]{1,0:T(8,128)(2,1)} %refs_0_.4), channel_id=1, source_target_pairs={{0,16},{4,20},{8,24},{12,28},{16,0},{20,4},{24,8},{28,12},{1,17},{... | collective-permute-start | bytes 3145736 | tf_op jit(solution)/shard_map/ppermute | solution.py:901
  67.6 25.2 %collective-permute-start.9 = (bf16[512,1024]{1,0:T(8,128)(2,1)}, bf16[512,1024]{1,0:T(8,128)(2,1)}, u32[]{:S(2)}, u32[]{:S(2)}) collective-permute-start(bf16[512,1024]{1,0:T(8,128)(2,1)} %refs_0_.3), channel_id=1, source_target_pairs={{0,8},{4,12},{8,0},{12,4},{16,24},{20,28},{24,16},{28,20},{1,9},{5... | collective-permute-start | bytes 3145736 | tf_op jit(solution)/shard_map/ppermute | solution.py:901
  69.1 23.7 %collective-permute-start.11 = (bf16[128,4096]{1,0:T(8,128)(2,1)}, bf16[128,4096]{1,0:T(8,128)(2,1)S(1)}, u32[]{:S(2)}, u32[]{:S(2)}) collective-permute-start(bf16[128,4096]{1,0:T(8,128)(2,1)} %collective-permute-done.3.refs_1_), channel_id=1, source_target_pairs={{0,4},{4,0},{8,12},{12,8},{16,20},{20,16},{24,28},{28,24},{1,5},{5... | collective-permute-start | bytes 3145736 | tf_op jit(solution)/shard_map/ppermute | solution.py:901
  92.8 25.1 %collective-permute-start.13 = (bf16[512,1024]{1,0:T(8,128)(2,1)S(1)}, bf16[512,1024]{1,0:T(8,128)(2,1)S(1)}, u32[]{:S(2)}, u32[]{:S(2)}) collective-permute-start(bf16[512,1024]{1,0:T(8,128)(2,1)S(1)} %copy-done.20), channel_id=1, source_target_pairs={{0,16},{4,20},{8,24},{12,28},{16,0},{20,4},{24,8},{28,12},{1,17},{... | collective-permute-start | bytes 3145736 | tf_op jit(solution)/shard_map/ppermute | solution.py:901
  93.5 24.4 %collective-permute-start.15 = (bf16[128,4096]{1,0:T(8,128)(2,1)S(1)}, bf16[128,4096]{1,0:T(8,128)(2,1)S(1)}, u32[]{:S(2)}, u32[]{:S(2)}) collective-permute-start(bf16[128,4096]{1,0:T(8,128)(2,1)S(1)} %collective-permute-done.8.refs_2_), channel_id=1, source_target_pairs={{0,4},{4,0},{8,12},{12,8},{16,20},{20,16},{24,28},{28,24},{1,5},{5... | collective-permute-start | bytes 3145736 | tf_op jit(solution)/shard_map/ppermute | solution.py:901
  93.5 25.6 %collective-permute-start.12 = (bf16[128,4096]{1,0:T(8,128)(2,1)S(1)}, bf16[128,4096]{1,0:T(8,128)(2,1)S(1)}, u32[]{:S(2)}, u32[]{:S(2)}) collective-permute-start(bf16[128,4096]{1,0:T(8,128)(2,1)S(1)} %collective-permute-done.8.refs_2_), channel_id=1, source_target_pairs={{0,8},{4,12},{8,0},{12,4},{16,24},{20,28},{24,16},{28,20},{1,9},{5... | collective-permute-start | bytes 3145736 | tf_op jit(solution)/shard_map/ppermute | solution.py:901
  121.7 18.1 %collective-permute-start.19 = (bf16[512,1024]{1,0:T(8,128)(2,1)}, bf16[512,1024]{1,0:T(8,128)(2,1)S(1)}, u32[]{:S(2)}, u32[]{:S(2)}) collective-permute-start(bf16[512,1024]{1,0:T(8,128)(2,1)} %refs_0_.3), channel_id=1, source_target_pairs={{0,4},{4,0},{8,12},{12,8},{16,20},{20,16},{24,28},{28,24},{1,5},{5... | collective-permute-start | bytes 3145736 | tf_op jit(solution)/shard_map/ppermute | solution.py:901
  142.9 27.4 %collective-permute-start.24 = (bf16[4,512,512]{2,1,0:T(8,128)(2,1)}, bf16[4,512,512]{2,1,0:T(8,128)(2,1)S(1)}, u32[]{:S(2)}, u32[]{:S(2)}) collective-permute-start(bf16[4,512,512]{2,1,0:T(8,128)(2,1)} %get-tuple-element.382), channel_id=1, source_target_pairs={{0,4},{4,0},{8,12},{12,8},{16,20},{20,16},{24,28},{28,24},{1,5},{5... | collective-permute-start | bytes 6291464 | tf_op jit(solution)/shard_map/ppermute | solution.py:901
  181.7 32.0 %collective-permute-start.28 = (bf16[2,512,512]{2,1,0:T(8,128)(2,1)}, bf16[2,512,512]{2,1,0:T(8,128)(2,1)S(1)}, u32[]{:S(2)}, u32[]{:S(2)}) collective-permute-start(bf16[2,512,512]{2,1,0:T(8,128)(2,1)} %get-tuple-element.416), channel_id=1, source_target_pairs={{0,16},{4,20},{8,24},{12,28},{16,0},{20,4},{24,8},{28,12},{1,17},{... | collective-permute-start | bytes 3145736 | tf_op jit(solution)/shard_map/ppermute | solution.py:901
  183.7 30.1 %collective-permute-start.29 = (bf16[2,512,512]{2,1,0:T(8,128)(2,1)}, bf16[2,512,512]{2,1,0:T(8,128)(2,1)S(1)}, u32[]{:S(2)}, u32[]{:S(2)}) collective-permute-start(bf16[2,512,512]{2,1,0:T(8,128)(2,1)} %get-tuple-element.417), channel_id=1, source_target_pairs={{0,8},{4,12},{8,0},{12,4},{16,24},{20,28},{24,16},{28,20},{1,9},{5... | collective-permute-start | bytes 3145736 | tf_op jit(solution)/shard_map/ppermute | solution.py:901
  213.8 36.5 %collective-permute-start.30 = (bf16[2,128,2048]{2,1,0:T(8,128)(2,1)}, bf16[2,128,2048]{2,1,0:T(8,128)(2,1)}, u32[]{:S(2)}, u32[]{:S(2)}) collective-permute-start(bf16[2,128,2048]{2,1,0:T(8,128)(2,1)} %get-tuple-element.439), channel_id=1, source_target_pairs={{0,16},{4,20},{8,24},{12,28},{16,0},{20,4},{24,8},{28,12},{1,17},{... | collective-permute-start | bytes 3145736 | tf_op jit(solution)/shard_map/ppermute | solution.py:901
  213.9 37.3 %collective-permute-start.31 = (bf16[2,128,2048]{2,1,0:T(8,128)(2,1)}, bf16[2,128,2048]{2,1,0:T(8,128)(2,1)}, u32[]{:S(2)}, u32[]{:S(2)}) collective-permute-start(bf16[2,128,2048]{2,1,0:T(8,128)(2,1)} %get-tuple-element.440), channel_id=1, source_target_pairs={{0,8},{4,12},{8,0},{12,4},{16,24},{20,28},{24,16},{28,20},{1,9},{5... | collective-permute-start | bytes 3145736 | tf_op jit(solution)/shard_map/ppermute | solution.py:901
  214.2 36.0 %collective-permute-start.32 = (bf16[512,512]{1,0:T(8,128)(2,1)S(1)}, bf16[512,512]{1,0:T(8,128)(2,1)S(1)}, u32[]{:S(2)}, u32[]{:S(2)}) collective-permute-start(bf16[512,512]{1,0:T(8,128)(2,1)S(1)} %fusion.5), channel_id=1, source_target_pairs={{0,8},{4,12},{8,0},{12,4},{16,24},{20,28},{24,16},{28,20},{1,9},{5... | collective-permute-start | bytes 1572872 | tf_op jit(solution)/shard_map/ppermute | solution.py:901
  216.3 33.9 %collective-permute-start.33 = (bf16[512,512]{1,0:T(8,128)(2,1)S(1)}, bf16[512,512]{1,0:T(8,128)(2,1)S(1)}, u32[]{:S(2)}, u32[]{:S(2)}) collective-permute-start(bf16[512,512]{1,0:T(8,128)(2,1)S(1)} %fusion.4), channel_id=1, source_target_pairs={{0,16},{4,20},{8,24},{12,28},{16,0},{20,4},{24,8},{28,12},{1,17},{... | collective-permute-start | bytes 1572872 | tf_op jit(solution)/shard_map/ppermute | solution.py:901
  281.0 23.4 %collective-permute-start.50 = (bf16[128,2048]{1,0:T(8,128)(2,1)S(1)}, bf16[128,2048]{1,0:T(8,128)(2,1)S(1)}, u32[]{:S(2)}, u32[]{:S(2)}) collective-permute-start(bf16[128,2048]{1,0:T(8,128)(2,1)S(1)} %get-tuple-element.531), channel_id=1, source_target_pairs={{0,1},{1,0},{2,3},{3,2},{4,5},{5,4},{6,7},{7,6},{8,9},{9,8},{10,11... | collective-permute-start | bytes 1572872 | tf_op jit(solution)/shard_map/ppermute | solution.py:936
  282.6 24.1 %collective-permute-start.49 = (bf16[512,512]{1,0:T(8,128)(2,1)S(1)}, bf16[512,512]{1,0:T(8,128)(2,1)S(1)}, u32[]{:S(2)}, u32[]{:S(2)}) collective-permute-start(bf16[512,512]{1,0:T(8,128)(2,1)S(1)} %add_convert_fusion.3), channel_id=1, source_target_pairs={{0,2},{1,3},{2,0},{3,1},{4,6},{5,7},{6,4},{7,5},{8,10},{9,11},{10,... | collective-permute-start | bytes 1572872 | tf_op jit(solution)/shard_map/ppermute | solution.py:936
  285.2 23.3 %collective-permute-start.42 = (bf16[2,272,512]{2,1,0:T(8,128)(2,1)S(1)}, bf16[2,272,512]{2,1,0:T(8,128)(2,1)S(1)}, u32[]{:S(2)}, u32[]{:S(2)}) collective-permute-start(bf16[2,272,512]{2,1,0:T(8,128)(2,1)S(1)} %copy-done.45), channel_id=1, source_target_pairs={{0,16},{4,20},{8,24},{12,28},{16,0},{20,4},{24,8},{28,12},{1,17},{... | collective-permute-start | bytes 1671176 | tf_op jit(solution)/shard_map/ppermute | solution.py:901
  311.3 20.5 %collective-permute-start.51 = (bf16[128,2048]{1,0:T(8,128)(2,1)S(1)}, bf16[128,2048]{1,0:T(8,128)(2,1)S(1)}, u32[]{:S(2)}, u32[]{:S(2)}) collective-permute-start(bf16[128,2048]{1,0:T(8,128)(2,1)S(1)} %add_convert_fusion.1), channel_id=1, source_target_pairs={{0,2},{1,3},{2,0},{3,1},{4,6},{5,7},{6,4},{7,5},{8,10},{9,11},{10,... | collective-permute-start | bytes 1572872 | tf_op jit(solution)/shard_map/ppermute | solution.py:936
  314.5 26.8 %collective-permute-start.52 = (bf16[512,512]{1,0:T(8,128)(2,1)S(1)}, bf16[512,512]{1,0:T(8,128)(2,1)S(1)}, u32[]{:S(2)}, u32[]{:S(2)}) collective-permute-start(bf16[512,512]{1,0:T(8,128)(2,1)S(1)} %add_convert_fusion.2), channel_id=1, source_target_pairs={{0,1},{1,0},{2,3},{3,2},{4,5},{5,4},{6,7},{7,6},{8,9},{9,8},{10,11... | collective-permute-start | bytes 1572872 | tf_op jit(solution)/shard_map/ppermute | solution.py:936
  317.5 32.8 %collective-permute-start.46 = (bf16[256,512]{1,0:T(8,128)(2,1)S(1)}, bf16[256,512]{1,0:T(8,128)(2,1)S(1)}, u32[]{:S(2)}, u32[]{:S(2)}) collective-permute-start(bf16[256,512]{1,0:T(8,128)(2,1)S(1)} %get-tuple-element.528), channel_id=1, source_target_pairs={{0,1},{1,0},{2,3},{3,2},{4,5},{5,4},{6,7},{7,6},{8,9},{9,8},{10,11... | collective-permute-start | bytes 786440 | tf_op jit(solution)/shard_map/ppermute | solution.py:936
  317.9 38.5 %collective-permute-start.56 = (bf16[272,512]{1,0:T(8,128)(2,1)S(1)}, bf16[272,512]{1,0:T(8,128)(2,1)S(1)}, u32[]{:S(2)}, u32[]{:S(2)}) collective-permute-start(bf16[272,512]{1,0:T(8,128)(2,1)S(1)} %get-tuple-element.549), channel_id=1, source_target_pairs={{0,1},{1,0},{2,3},{3,2},{4,5},{5,4},{6,7},{7,6},{8,9},{9,8},{10,11... | collective-permute-start | bytes 835592 | tf_op jit(solution)/shard_map/ppermute | solution.py:936
  350.5 24.0 %collective-permute-start.53 = (bf16[128,2048]{1,0:T(8,128)(2,1)S(1)}, bf16[128,2048]{1,0:T(8,128)(2,1)S(1)}, u32[]{:S(2)}, u32[]{:S(2)}) collective-permute-start(bf16[128,2048]{1,0:T(8,128)(2,1)S(1)} %add_convert_fusion), channel_id=1, source_target_pairs={{0,1},{1,0},{2,3},{3,2},{4,5},{5,4},{6,7},{7,6},{8,9},{9,8},{10,11... | collective-permute-start | bytes 1572872 | tf_op jit(solution)/shard_map/ppermute | solution.py:936
  (75 other events, 839.9 us)
Sparse Core Ops, SparseCore 0:
  42.0 81.0 all-gather.2
  171.1 83.0 all-gather.4

commit v5 on v4

--- a/solution.py
+++ b/solution.py
@@ -291,7 +291,7 @@
 def feed_up(meta, low, up, bias):
     total, width = low.shape
     wide = up[0].shape[1]
-    strip, tile = 1024, 512
+    strip, tile = 512, 512
     strips, inner = wide // strip, strip // tile
 
     def kernel(meta, x_ref, bias_ref, *refs):
@@ -368,14 +368,19 @@
         rest = [pltpu.make_async_copy(unit_ref, unit, more.at[0])] + [
             pltpu.make_async_copy(cot_ref.at[meta[3 + i]], cot.at[i], more.at[1 + i]) for i in range(batches)
         ]
-        for copy in rest:
-            copy.start()
-        for b in range(8):
-            pltpu.make_async_copy(slope_ref.at[:, pl.ds(512 * b, 512)], right.at[b], right_sems.at[b]).start()
 
         def add(b, carry):
             arrived(left.at[b], left_sems.at[b])
             arrived(held.at[b], sems.at[b])
+
+            @pl.when(b == 4)
+            def _():
+                for copy in rest:
+                    copy.start()
+                for c in range(8):
+                    at = pl.ds(512 * c, 512)
+                    pltpu.make_async_copy(slope_ref.at[:, at], right.at[c], right_sems.at[c]).start()
+
             part = dot_nn(left[b], held[b])
 
             @pl.when(b == 0)
@@ -1044,11 +1049,11 @@
         feed_down(order.meta, act, slope, down, unit_one, cot_pool, vecs, batches, rows)
     )
     sum_got = swap(sum_low, CORE)
-    out, act_got, both_got, sum_got, pre = order.then((out, act_got, both_got, sum_got, pre))
+    out, act_got, sum_got, pre = order.then((out, act_got, sum_got, pre))
     pre_got = swap(pre, CORE)
     out_pool = lax.all_gather(out.reshape(batches, rows, width), "rep", axis=0, tiled=True)
     far_down, own_down, rest_down = order.then(down_grad(order.meta, act, act_got, sum_low, sum_got))
-    pre_got, far_down = order.then((pre_got, far_down))
+    pre_got, both_got, far_down = order.then((pre_got, both_got, far_down))
     got_down = sent(far_down)
     grad_resid, resid_low, grad_mixed, grads_one = order.then(
         back_up(order.meta, pre, up, first, grad_sum, unit_one, inverse_one, vecs)
@@ -1098,10 +1103,12 @@
     taken_a = order.then(taken_a)
     half_a = order.then(plus(kept_a, taken_a))
     over_a = pairs(half_a, 2)
-    over_up, other_down = pairs(half_up, 2), pairs(total_down, 1)
+    over_up = pairs(half_up, 2)
     taken_b = order.then(taken_b)
     half_b = order.then(plus(kept_b, taken_b))
     over_b = pairs(half_b, 2)
+    total_down = order.then(total_down)
+    other_down = pairs(total_down, 1)
     over_a = order.then(over_a)
     total_a = order.then(plus(half_a, over_a))
     other_a = pairs(total_a, 1)

time: 390 us -> 386 us (0.990)
  transfers between devices with their start and end apart: 61 -> 61, of which waited for: 27 -> 26; matrix products, arithmetic and copies ran while one was open for 3% -> 3% of each run, Pallas kernels for 38% -> 38%
where the time goes in v5:
time: 386 us; the launch traced here: 385 us
  Pallas kernels  149 us (39%)
  waiting for transfers between devices  144 us (37%)
  starting transfers between devices  53.2 us (14%)
  between operations  14.9 us (4%)
  local copies, waits for them, and re-layouts  13.3 us (3%)
  other arithmetic  10.2 us (3%)
    pallas_call x13, Pallas kernels, run(): pl.pallas_call(kernel, grid_spec=pltpu.PrefetchScalarGridSpec(num_scalar_...  147 us
    ppermute x47, waiting for transfers between devices, swap(): return lax.ppermute(value, 'shard', [(i, i ^ mask) for i in range(8)])  81.2 us
    ppermute x12, waiting for transfers between devices, pairs(): return lax.ppermute(value, 'rep', [(i, i ^ mask) for i in range(4)])  62.8 us
    ppermute x47, starting transfers between devices, swap(): return lax.ppermute(value, 'shard', [(i, i ^ mask) for i in range(8)])  37.1 us
    ppermute x12, starting transfers between devices, pairs(): return lax.ppermute(value, 'rep', [(i, i ^ mask) for i in range(4)])  16 us
  transfers between devices with their start and end apart: 61, of which 26 were waited for; matrix products, arithmetic and copies ran while one was open for 3% of the time, Pallas kernels for 38%

profile of v5, /device:TPU:0, one launch (start us, length us, event | category | flops | bytes accessed | tf_op | source)
XLA Modules:
  0.0 384.8 jit_solution(12710647348509743833)
XLA Ops:
  10.9 3.0 collective-permute-start.1
  17.5 20.4 %collective-permute-done.1.refs_2_.refs_10_ = bf16[528,1024]{1,0:T(8,128)(2,1)S(1)} collective-permute-done((bf16[528,1024]{1,0:T(8,128)(2,1)}, bf16[528,1024]{1,0:T(8,128)(2,1)S(1)}, u32[]{:S(2)}, u32[]{:S(2)}) %collective-permute-start.1) | collective-permute-done | bytes 1081376 | tf_op jit(solution)/shard_map/ppermute | solution.py:906
  42.0 23.4 %collective-permute-done.3.refs_1_ = bf16[128,4096]{1,0:T(8,128)(2,1)} collective-permute-done((bf16[128,4096]{1,0:T(8,128)(2,1)}, bf16[128,4096]{1,0:T(8,128)(2,1)}, u32[]{:S(2)}, u32[]{:S(2)}) %collective-permute-start.3) | collective-permute-done | bytes 1048608 | tf_op jit(solution)/shard_map/ppermute | solution.py:906
  70.1 11.2 %shard_map.315 = (bf16[3,512,1024]{2,1,0:T(8,128)(2,1)}, f32[8,1024]{1,0:T(8,128)}, f32[1,4096]{1,0:T(1,128)}, bf16[4,512,128]{2,1,0:T(8,128)(2,1)}) custom-call(s32[8]{0:T(128)} %concatenate.24.meta, bf16[512,1024]{1,0:T(8,128)(2,1)} %bitcast.90, bf16[528,1024]{1,0:T(8,128)(2,1)} %shard_map.314.refs_0_.refs_8_, bf16[528,1024]{1,0:T(8,128)(2,1)} %copy-done.4, ...), custom_call_target="tpu_custom_call" | custom-call | flops 1024 | bytes 1024 | tf_op jit(solution)/shard_map/pallas_call | solution.py:89
  81.3 10.8 %shard_map.316 = (bf16[512,1024]{1,0:T(8,128)(2,1)}, bf16[2,16,256,256]{3,2,1,0:T(8,128)(2,1)}, f32[512,1024]{1,0:T(8,128)}) custom-call(s32[8]{0:T(128)} %concatenate.24.meta, bf16[3,512,1024]{2,1,0:T(8,128)(2,1)} %get-tuple-element.301.q_ref.k_ref.v_ref, bf16[3,512,1024]{2,1,0:T(8,128)(2,1)} %get-tuple-element.301.q_ref.k_ref.v_ref, ...), custom_call_target="tpu_custom_call" | custom-call | flops 1024 | bytes 1024 | tf_op jit(solution)/shard_map/pallas_call | solution.py:89
  95.2 9.4 %shard_map.317 = (f32[512,1024]{1,0:T(8,128)}, f32[512,128]{1,0:T(8,128)}, bf16[512,1024]{1,0:T(8,128)(2,1)}, bf16[2,4,512,128]{3,2,1,0:T(8,128)(2,1)}) custom-call(s32[8]{0:T(128)} %concatenate.24.meta, bf16[512,1024]{1,0:T(8,128)(2,1)} %get-tuple-element.311.mixed_ref.m_ref, bf16[512,1024]{1,0:T(8,128)(2,1)} %bitcast.91, ...), custom_call_target="tpu_custom_call" | custom-call | flops 1024 | bytes 1024 | tf_op jit(solution)/shard_map/pallas_call | solution.py:89
  106.5 11.4 %collective-permute-done.13.refs_2_ = bf16[512,1024]{1,0:T(8,128)(2,1)S(1)} collective-permute-done((bf16[512,1024]{1,0:T(8,128)(2,1)S(1)}, bf16[512,1024]{1,0:T(8,128)(2,1)S(1)}, u32[]{:S(2)}, u32[]{:S(2)}) %collective-permute-start.13) | collective-permute-done | bytes 1048608 | tf_op jit(solution)/shard_map/ppermute | solution.py:906
  119.0 2.7 collective-permute-done.16.refs_7_
  126.1 13.8 %shard_map.318 = (bf16[512,4096]{1,0:T(8,128)(2,1)}, bf16[512,4096]{1,0:T(8,128)(2,1)}, bf16[4,512,512]{2,1,0:T(8,128)(2,1)}) custom-call(s32[8]{0:T(128)} %concatenate.24.meta, bf16[512,1024]{1,0:T(8,128)(2,1)} %get-tuple-element.334.x_ref, f32[1,4096]{1,0:T(1,128)} %get-tuple-element.335.bias_ref, bf16[128,4096]{1,0:T(8,128)(2,1)} %refs_0_.4, ...), custom_call_target="tpu_custom_call" | custom-call | flops 1024 | bytes 1024 | tf_op jit(solution)/shard_map/pallas_call | solution.py:89
  143.7 21.3 %shard_map.319 = (bf16[512,1024]{1,0:T(8,128)(2,1)}, f32[512,1024]{1,0:T(8,128)}, bf16[512,1024]{1,0:T(8,128)(2,1)}, f32[8,1024]{1,0:T(8,128)}, bf16[512,4096]{1,0:T(8,128)(2,1)}, /*index=5*/f32[1,4096]{1,0:T(1,128)}) custom-call(s32[8]{0:T(128)} %concatenate.24.meta, bf16[512,4096]{1,0:T(8,128)(2,1)} %get-tuple-element.363.act_ref.left_ref, ...), custom_call_target="tpu_custom_call" | custom-call | flops 1024 | bytes 1024 | tf_op jit(solution)/shard_map/pallas_call | solution.py:89
  166.0 2.5 collective-permute-done.25.right_got
  170.9 9.6 %shard_map.320 = (bf16[2,512,512]{2,1,0:T(8,128)(2,1)}, bf16[2,512,512]{2,1,0:T(8,128)(2,1)}, bf16[512,512]{1,0:T(8,128)(2,1)}, bf16[512,512]{1,0:T(8,128)(2,1)}...) custom-call(s32[8]{0:T(128)} %concatenate.24.meta, bf16[512,4096]{1,0:T(8,128)(2,1)} %get-tuple-element.363.act_ref.left_ref, ...), custom_call_target="tpu_custom_call" | custom-call | flops 1024 | bytes 1024 | tf_op jit(solution)/shard_map/pallas_call | solution.py:89
  183.3 16.8 %shard_map.321 = (f32[512,1024]{1,0:T(8,128)}, bf16[512,1024]{1,0:T(8,128)(2,1)}, bf16[512,1024]{1,0:T(8,128)(2,1)}, f32[8,1024]{1,0:T(8,128)}) custom-call(s32[8]{0:T(128)} %concatenate.24.meta, bf16[512,4096]{1,0:T(8,128)(2,1)} %get-tuple-element.397.pre_ref, f32[512,1024]{1,0:T(8,128)} %get-tuple-element.402.sum_ref, ...), custom_call_target="tpu_custom_call" | custom-call | flops 1024 | bytes 1024 | tf_op jit(solution)/shard_map/pallas_call | solution.py:89
  200.1 11.1 %shard_map.322 = (bf16[2,128,2048]{2,1,0:T(8,128)(2,1)}, bf16[2,128,2048]{2,1,0:T(8,128)(2,1)}, bf16[128,2048]{1,0:T(8,128)(2,1)}, bf16[128,2048]{1,0:T(8,128)(2...) custom-call(s32[8]{0:T(128)} %concatenate.24.meta, bf16[512,1024]{1,0:T(8,128)(2,1)} %get-tuple-element.334.x_ref, ...), custom_call_target="tpu_custom_call" | custom-call | flops 1024 | bytes 1024 | tf_op jit(solution)/shard_map/pallas_call | solution.py:89
  215.7 14.7 %shard_map.323 = (bf16[3,512,1024]{2,1,0:T(8,128)(2,1)}, bf16[8,16,1024]{2,1,0:T(8,128)(2,1)}) custom-call(s32[8]{0:T(128)} %concatenate.24.meta, bf16[3,512,1024]{2,1,0:T(8,128)(2,1)} %get-tuple-element.301.q_ref.k_ref.v_ref, bf16[3,512,1024]{2,1,0:T(8,128)(2,1)} %get-tuple-element.301.q_ref.k_ref.v_ref, ...), custom_call_target="tpu_custom_call" | custom-call | flops 1024 | bytes 1024 | tf_op jit(solution)/shard_map/pallas_call | solution.py:89
  230.5 10.7 %shard_map.324 = bf16[512,1024]{1,0:T(8,128)(2,1)} custom-call(s32[8]{0:T(128)} %concatenate.24.meta, bf16[3,512,1024]{2,1,0:T(8,128)(2,1)} %get-tuple-element.462.g_ref, f32[512,1024]{1,0:T(8,128)} %get-tuple-element.439.resid_ref, bf16[528,1024]{1,0:T(8,128)(2,1)} %shard_map.314.refs_0_.refs_8_, bf16[528,1024]{1,0:T(8,128)(2,1)} %copy-done.4, ...), custom_call_target="tpu_custom_call" | custom-call | flops 1024 | bytes 1024 | tf_op jit(solution)/shard_map/pallas_call | solution.py:89
  241.2 6.5 %collective-permute-done.32.late_a = bf16[512,512]{1,0:T(8,128)(2,1)S(1)} collective-permute-done((bf16[512,512]{1,0:T(8,128)(2,1)S(1)}, bf16[512,512]{1,0:T(8,128)(2,1)S(1)}, u32[]{:S(2)}, u32[]{:S(2)}) %collective-permute-start.32) | collective-permute-done | bytes 524320 | tf_op jit(solution)/shard_map/ppermute | solution.py:906
  249.3 5.2 %shard_map.325 = (bf16[512,512]{1,0:T(8,128)(2,1)}, bf16[512,512]{1,0:T(8,128)(2,1)}, bf16[128,2048]{1,0:T(8,128)(2,1)}, bf16[128,2048]{1,0:T(8,128)(2,1)}) custom-call(s32[8]{0:T(128)} %concatenate.24.meta, bf16[512,512]{1,0:T(8,128)(2,1)} %get-tuple-element.448.own_a, bf16[512,512]{1,0:T(8,128)(2,1)} %get-tuple-element.449.own_b, ...), custom_call_target="tpu_custom_call" | custom-call | flops 1024 | bytes 1024 | tf_op jit(solution)/shard_map/pallas_call | solution.py:89
  261.0 9.5 %shard_map.326 = (bf16[2,256,512]{2,1,0:T(8,128)(2,1)}, bf16[2,256,512]{2,1,0:T(8,128)(2,1)}, bf16[256,512]{1,0:T(8,128)(2,1)}, bf16[256,512]{1,0:T(8,128)(2,1)}...) custom-call(s32[8]{0:T(128)} %concatenate.24.meta, ...), custom_call_target="tpu_custom_call" | custom-call | flops 1024 | bytes 1024 | tf_op jit(solution)/shard_map/pallas_call | solution.py:89
  276.1 2.4 broadcast_select_fusion.4
  280.2 2.6 collective-permute-start.46
  284.4 5.3 %collective-permute-done.40 = bf16[2,256,512]{2,1,0:T(8,128)(2,1)S(1)} collective-permute-done((bf16[2,256,512]{2,1,0:T(8,128)(2,1)}, bf16[2,256,512]{2,1,0:T(8,128)(2,1)S(1)}, u32[]{:S(2)}, u32[]{:S(2)}) %collective-permute-start.40) | collective-permute-done | bytes 524320 | tf_op jit(solution)/shard_map/ppermute | solution.py:906
  291.0 10.9 %collective-permute-done.47 = bf16[128,2048]{1,0:T(8,128)(2,1)S(1)} collective-permute-done((bf16[128,2048]{1,0:T(8,128)(2,1)S(1)}, bf16[128,2048]{1,0:T(8,128)(2,1)S(1)}, u32[]{:S(2)}, u32[]{:S(2)}) %collective-permute-start.47) | collective-permute-done | bytes 524320 | tf_op jit(solution)/shard_map/ppermute | solution.py:941
  301.9 2.4 collective-permute-done.46
  309.3 2.7 shard_map.327
  312.1 2.7 collective-permute-start.53
  317.4 19.2 %collective-permute-done.54 = bf16[512,512]{1,0:T(8,128)(2,1)S(1)} collective-permute-done((bf16[512,512]{1,0:T(8,128)(2,1)S(1)}, bf16[512,512]{1,0:T(8,128)(2,1)S(1)}, u32[]{:S(2)}, u32[]{:S(2)}) %collective-permute-start.54) | collective-permute-done | bytes 524320 | tf_op jit(solution)/shard_map/ppermute | solution.py:941
  336.7 8.9 %collective-permute-done.50 = bf16[256,512]{1,0:T(8,128)(2,1)S(1)} collective-permute-done((bf16[256,512]{1,0:T(8,128)(2,1)S(1)}, bf16[256,512]{1,0:T(8,128)(2,1)S(1)}, u32[]{:S(2)}, u32[]{:S(2)}) %collective-permute-start.50) | collective-permute-done | bytes 262176 | tf_op jit(solution)/shard_map/ppermute | solution.py:941
  345.9 6.3 %collective-permute-done.56 = bf16[272,512]{1,0:T(8,128)(2,1)S(1)} collective-permute-done((bf16[272,512]{1,0:T(8,128)(2,1)S(1)}, bf16[272,512]{1,0:T(8,128)(2,1)S(1)}, u32[]{:S(2)}, u32[]{:S(2)}) %collective-permute-start.56) | collective-permute-done | bytes 278560 | tf_op jit(solution)/shard_map/ppermute | solution.py:941
  354.3 4.1 %collective-permute-done.51 = bf16[256,512]{1,0:T(8,128)(2,1)S(1)} collective-permute-done((bf16[256,512]{1,0:T(8,128)(2,1)S(1)}, bf16[256,512]{1,0:T(8,128)(2,1)S(1)}, u32[]{:S(2)}, u32[]{:S(2)}) %collective-permute-start.51) | collective-permute-done | bytes 262176 | tf_op jit(solution)/shard_map/ppermute | solution.py:941
  360.1 8.3 %collective-permute-done.57 = bf16[272,512]{1,0:T(8,128)(2,1)S(1)} collective-permute-done((bf16[272,512]{1,0:T(8,128)(2,1)S(1)}, bf16[272,512]{1,0:T(8,128)(2,1)S(1)}, u32[]{:S(2)}, u32[]{:S(2)}) %collective-permute-start.57) | collective-permute-done | bytes 278560 | tf_op jit(solution)/shard_map/ppermute | solution.py:941
  368.5 2.6 collective-permute-start.58
  (238 shorter events, 77.9 us)
Async XLA Ops:
  7.2 135.9 %all-gather.3.cloned.1.call-start = ((), (), s32[]{:S(2)}) async-start(), calls=%async_computation | async-start | bytes 5242880 | tf_op jit(solution)/shard_map/all_gather | solution.py:1028
  10.9 27.0 %collective-permute-start.1 = (bf16[528,1024]{1,0:T(8,128)(2,1)}, bf16[528,1024]{1,0:T(8,128)(2,1)S(1)}, u32[]{:S(2)}, u32[]{:S(2)}) collective-permute-start(bf16[528,1024]{1,0:T(8,128)(2,1)} %shard_map.314.refs_0_.refs_8_), channel_id=1, source_target_pairs={{0,16},{4,20},{8,24},{12,28},{16,0},{20,4},{24,8},{28,12},{1,17},{... | collective-permute-start | bytes 3244040 | tf_op jit(solution)/shard_map/ppermute | solution.py:906
  13.8 25.5 %collective-permute-start = (bf16[528,1024]{1,0:T(8,128)(2,1)}, bf16[528,1024]{1,0:T(8,128)(2,1)S(1)}, u32[]{:S(2)}, u32[]{:S(2)}) collective-permute-start(bf16[528,1024]{1,0:T(8,128)(2,1)} %shard_map.314.refs_0_.refs_8_), channel_id=1, source_target_pairs={{0,8},{4,12},{8,0},{12,4},{16,24},{20,28},{24,16},{28,20},{1,9},{5... | collective-permute-start | bytes 3244040 | tf_op jit(solution)/shard_map/ppermute | solution.py:906
  15.3 26.6 %collective-permute-start.4 = (bf16[528,1024]{1,0:T(8,128)(2,1)}, bf16[528,1024]{1,0:T(8,128)(2,1)S(1)}, u32[]{:S(2)}, u32[]{:S(2)}) collective-permute-start(bf16[528,1024]{1,0:T(8,128)(2,1)} %shard_map.314.refs_0_.refs_8_), channel_id=1, source_target_pairs={{0,4},{4,0},{8,12},{12,8},{16,20},{20,16},{24,28},{28,24},{1,5},{5... | collective-permute-start | bytes 3244040 | tf_op jit(solution)/shard_map/ppermute | solution.py:906
  39.4 26.0 %collective-permute-start.6 = (bf16[528,1024]{1,0:T(8,128)(2,1)S(1)}, bf16[528,1024]{1,0:T(8,128)(2,1)}, u32[]{:S(2)}, u32[]{:S(2)}) collective-permute-start(bf16[528,1024]{1,0:T(8,128)(2,1)S(1)} %collective-permute-done.1.refs_2_.refs_10_), channel_id=1, source_target_pairs={{0,4},{4,0},{8,12},{12,8},{16,20},{20,16},{24,28},{28,24},{1,5},{5... | collective-permute-start | bytes 3244040 | tf_op jit(solution)/shard_map/ppermute | solution.py:906
  39.4 26.0 %collective-permute-start.5 = (bf16[528,1024]{1,0:T(8,128)(2,1)S(1)}, bf16[528,1024]{1,0:T(8,128)(2,1)}, u32[]{:S(2)}, u32[]{:S(2)}) collective-permute-start(bf16[528,1024]{1,0:T(8,128)(2,1)S(1)} %collective-permute-done.refs_1_.refs_9_), channel_id=1, source_target_pairs={{0,4},{4,0},{8,12},{12,8},{16,20},{20,16},{24,28},{28,24},{1,5},{5... | collective-permute-start | bytes 3244040 | tf_op jit(solution)/shard_map/ppermute | solution.py:906
  39.9 25.9 %collective-permute-start.2 = (bf16[528,1024]{1,0:T(8,128)(2,1)S(1)}, bf16[528,1024]{1,0:T(8,128)(2,1)}, u32[]{:S(2)}, u32[]{:S(2)}) collective-permute-start(bf16[528,1024]{1,0:T(8,128)(2,1)S(1)} %collective-permute-done.refs_1_.refs_9_), channel_id=1, source_target_pairs={{0,16},{4,20},{8,24},{12,28},{16,0},{20,4},{24,8},{28,12},{1,17},{... | collective-permute-start | bytes 3244040 | tf_op jit(solution)/shard_map/ppermute | solution.py:906
  40.2 25.2 %collective-permute-start.3 = (bf16[128,4096]{1,0:T(8,128)(2,1)}, bf16[128,4096]{1,0:T(8,128)(2,1)}, u32[]{:S(2)}, u32[]{:S(2)}) collective-permute-start(bf16[128,4096]{1,0:T(8,128)(2,1)} %refs_0_.4), channel_id=1, source_target_pairs={{0,8},{4,12},{8,0},{12,4},{16,24},{20,28},{24,16},{28,20},{1,9},{5... | collective-permute-start | bytes 3145736 | tf_op jit(solution)/shard_map/ppermute | solution.py:906
  41.9 228.7 %all-gather.5.cloned.1.call-start = ((), (), s32[]{:S(2)}) async-start(), calls=%async_computation.1 | async-start | bytes 5242880 | tf_op jit(solution)/shard_map/all_gather | solution.py:1054
  65.7 26.4 %collective-permute-start.10 = (bf16[128,4096]{1,0:T(8,128)(2,1)}, bf16[128,4096]{1,0:T(8,128)(2,1)S(1)}, u32[]{:S(2)}, u32[]{:S(2)}) collective-permute-start(bf16[128,4096]{1,0:T(8,128)(2,1)} %refs_0_.4), channel_id=1, source_target_pairs={{0,4},{4,0},{8,12},{12,8},{16,20},{20,16},{24,28},{28,24},{1,5},{5... | collective-permute-start | bytes 3145736 | tf_op jit(solution)/shard_map/ppermute | solution.py:906
  66.2 25.9 %collective-permute-start.8 = (bf16[128,4096]{1,0:T(8,128)(2,1)}, bf16[128,4096]{1,0:T(8,128)(2,1)S(1)}, u32[]{:S(2)}, u32[]{:S(2)}) collective-permute-start(bf16[128,4096]{1,0:T(8,128)(2,1)} %refs_0_.4), channel_id=1, source_target_pairs={{0,16},{4,20},{8,24},{12,28},{16,0},{20,4},{24,8},{28,12},{1,17},{... | collective-permute-start | bytes 3145736 | tf_op jit(solution)/shard_map/ppermute | solution.py:906
  67.6 25.2 %collective-permute-start.9 = (bf16[512,1024]{1,0:T(8,128)(2,1)}, bf16[512,1024]{1,0:T(8,128)(2,1)}, u32[]{:S(2)}, u32[]{:S(2)}) collective-permute-start(bf16[512,1024]{1,0:T(8,128)(2,1)} %refs_0_.3), channel_id=1, source_target_pairs={{0,8},{4,12},{8,0},{12,4},{16,24},{20,28},{24,16},{28,20},{1,9},{5... | collective-permute-start | bytes 3145736 | tf_op jit(solution)/shard_map/ppermute | solution.py:906
  69.1 23.7 %collective-permute-start.11 = (bf16[128,4096]{1,0:T(8,128)(2,1)}, bf16[128,4096]{1,0:T(8,128)(2,1)S(1)}, u32[]{:S(2)}, u32[]{:S(2)}) collective-permute-start(bf16[128,4096]{1,0:T(8,128)(2,1)} %collective-permute-done.3.refs_1_), channel_id=1, source_target_pairs={{0,4},{4,0},{8,12},{12,8},{16,20},{20,16},{24,28},{28,24},{1,5},{5... | collective-permute-start | bytes 3145736 | tf_op jit(solution)/shard_map/ppermute | solution.py:906
  92.8 25.1 %collective-permute-start.13 = (bf16[512,1024]{1,0:T(8,128)(2,1)S(1)}, bf16[512,1024]{1,0:T(8,128)(2,1)S(1)}, u32[]{:S(2)}, u32[]{:S(2)}) collective-permute-start(bf16[512,1024]{1,0:T(8,128)(2,1)S(1)} %copy-done.20), channel_id=1, source_target_pairs={{0,16},{4,20},{8,24},{12,28},{16,0},{20,4},{24,8},{28,12},{1,17},{... | collective-permute-start | bytes 3145736 | tf_op jit(solution)/shard_map/ppermute | solution.py:906
  93.5 24.4 %collective-permute-start.15 = (bf16[128,4096]{1,0:T(8,128)(2,1)S(1)}, bf16[128,4096]{1,0:T(8,128)(2,1)S(1)}, u32[]{:S(2)}, u32[]{:S(2)}) collective-permute-start(bf16[128,4096]{1,0:T(8,128)(2,1)S(1)} %collective-permute-done.8.refs_2_), channel_id=1, source_target_pairs={{0,4},{4,0},{8,12},{12,8},{16,20},{20,16},{24,28},{28,24},{1,5},{5... | collective-permute-start | bytes 3145736 | tf_op jit(solution)/shard_map/ppermute | solution.py:906
  93.5 25.6 %collective-permute-start.12 = (bf16[128,4096]{1,0:T(8,128)(2,1)S(1)}, bf16[128,4096]{1,0:T(8,128)(2,1)S(1)}, u32[]{:S(2)}, u32[]{:S(2)}) collective-permute-start(bf16[128,4096]{1,0:T(8,128)(2,1)S(1)} %collective-permute-done.8.refs_2_), channel_id=1, source_target_pairs={{0,8},{4,12},{8,0},{12,4},{16,24},{20,28},{24,16},{28,20},{1,9},{5... | collective-permute-start | bytes 3145736 | tf_op jit(solution)/shard_map/ppermute | solution.py:906
  121.7 18.2 %collective-permute-start.19 = (bf16[512,1024]{1,0:T(8,128)(2,1)}, bf16[512,1024]{1,0:T(8,128)(2,1)S(1)}, u32[]{:S(2)}, u32[]{:S(2)}) collective-permute-start(bf16[512,1024]{1,0:T(8,128)(2,1)} %refs_0_.3), channel_id=1, source_target_pairs={{0,4},{4,0},{8,12},{12,8},{16,20},{20,16},{24,28},{28,24},{1,5},{5... | collective-permute-start | bytes 3145736 | tf_op jit(solution)/shard_map/ppermute | solution.py:906
  142.9 25.6 %collective-permute-start.24 = (bf16[4,512,512]{2,1,0:T(8,128)(2,1)}, bf16[4,512,512]{2,1,0:T(8,128)(2,1)S(1)}, u32[]{:S(2)}, u32[]{:S(2)}) collective-permute-start(bf16[4,512,512]{2,1,0:T(8,128)(2,1)} %get-tuple-element.384), channel_id=1, source_target_pairs={{0,4},{4,0},{8,12},{12,8},{16,20},{20,16},{24,28},{28,24},{1,5},{5... | collective-permute-start | bytes 6291464 | tf_op jit(solution)/shard_map/ppermute | solution.py:906
  180.6 30.6 %collective-permute-start.28 = (bf16[2,512,512]{2,1,0:T(8,128)(2,1)}, bf16[2,512,512]{2,1,0:T(8,128)(2,1)S(1)}, u32[]{:S(2)}, u32[]{:S(2)}) collective-permute-start(bf16[2,512,512]{2,1,0:T(8,128)(2,1)} %get-tuple-element.418), channel_id=1, source_target_pairs={{0,16},{4,20},{8,24},{12,28},{16,0},{20,4},{24,8},{28,12},{1,17},{... | collective-permute-start | bytes 3145736 | tf_op jit(solution)/shard_map/ppermute | solution.py:906
  182.2 29.1 %collective-permute-start.29 = (bf16[2,512,512]{2,1,0:T(8,128)(2,1)}, bf16[2,512,512]{2,1,0:T(8,128)(2,1)S(1)}, u32[]{:S(2)}, u32[]{:S(2)}) collective-permute-start(bf16[2,512,512]{2,1,0:T(8,128)(2,1)} %get-tuple-element.419), channel_id=1, source_target_pairs={{0,8},{4,12},{8,0},{12,4},{16,24},{20,28},{24,16},{28,20},{1,9},{5... | collective-permute-start | bytes 3145736 | tf_op jit(solution)/shard_map/ppermute | solution.py:906
  211.2 36.5 %collective-permute-start.30 = (bf16[2,128,2048]{2,1,0:T(8,128)(2,1)}, bf16[2,128,2048]{2,1,0:T(8,128)(2,1)}, u32[]{:S(2)}, u32[]{:S(2)}) collective-permute-start(bf16[2,128,2048]{2,1,0:T(8,128)(2,1)} %get-tuple-element.441), channel_id=1, source_target_pairs={{0,16},{4,20},{8,24},{12,28},{16,0},{20,4},{24,8},{28,12},{1,17},{... | collective-permute-start | bytes 3145736 | tf_op jit(solution)/shard_map/ppermute | solution.py:906
  211.6 37.1 %collective-permute-start.31 = (bf16[2,128,2048]{2,1,0:T(8,128)(2,1)}, bf16[2,128,2048]{2,1,0:T(8,128)(2,1)}, u32[]{:S(2)}, u32[]{:S(2)}) collective-permute-start(bf16[2,128,2048]{2,1,0:T(8,128)(2,1)} %get-tuple-element.442), channel_id=1, source_target_pairs={{0,8},{4,12},{8,0},{12,4},{16,24},{20,28},{24,16},{28,20},{1,9},{5... | collective-permute-start | bytes 3145736 | tf_op jit(solution)/shard_map/ppermute | solution.py:906
  212.9 34.8 %collective-permute-start.32 = (bf16[512,512]{1,0:T(8,128)(2,1)S(1)}, bf16[512,512]{1,0:T(8,128)(2,1)S(1)}, u32[]{:S(2)}, u32[]{:S(2)}) collective-permute-start(bf16[512,512]{1,0:T(8,128)(2,1)S(1)} %fusion.5), channel_id=1, source_target_pairs={{0,8},{4,12},{8,0},{12,4},{16,24},{20,28},{24,16},{28,20},{1,9},{5... | collective-permute-start | bytes 1572872 | tf_op jit(solution)/shard_map/ppermute | solution.py:906
  214.0 33.7 %collective-permute-start.33 = (bf16[512,512]{1,0:T(8,128)(2,1)S(1)}, bf16[512,512]{1,0:T(8,128)(2,1)S(1)}, u32[]{:S(2)}, u32[]{:S(2)}) collective-permute-start(bf16[512,512]{1,0:T(8,128)(2,1)S(1)} %fusion.4), channel_id=1, source_target_pairs={{0,16},{4,20},{8,24},{12,28},{16,0},{20,4},{24,8},{28,12},{1,17},{... | collective-permute-start | bytes 1572872 | tf_op jit(solution)/shard_map/ppermute | solution.py:906
  278.5 23.3 %collective-permute-start.47 = (bf16[128,2048]{1,0:T(8,128)(2,1)S(1)}, bf16[128,2048]{1,0:T(8,128)(2,1)S(1)}, u32[]{:S(2)}, u32[]{:S(2)}) collective-permute-start(bf16[128,2048]{1,0:T(8,128)(2,1)S(1)} %get-tuple-element.532), channel_id=1, source_target_pairs={{0,1},{1,0},{2,3},{3,2},{4,5},{5,4},{6,7},{7,6},{8,9},{9,8},{10,11... | collective-permute-start | bytes 1572872 | tf_op jit(solution)/shard_map/ppermute | solution.py:941
  280.2 24.1 %collective-permute-start.46 = (bf16[512,512]{1,0:T(8,128)(2,1)S(1)}, bf16[512,512]{1,0:T(8,128)(2,1)S(1)}, u32[]{:S(2)}, u32[]{:S(2)}) collective-permute-start(bf16[512,512]{1,0:T(8,128)(2,1)S(1)} %add_convert_fusion.3), channel_id=1, source_target_pairs={{0,2},{1,3},{2,0},{3,1},{4,6},{5,7},{6,4},{7,5},{8,10},{9,11},{10,... | collective-permute-start | bytes 1572872 | tf_op jit(solution)/shard_map/ppermute | solution.py:941
  282.8 23.9 %collective-permute-start.42 = (bf16[2,272,512]{2,1,0:T(8,128)(2,1)S(1)}, bf16[2,272,512]{2,1,0:T(8,128)(2,1)S(1)}, u32[]{:S(2)}, u32[]{:S(2)}) collective-permute-start(bf16[2,272,512]{2,1,0:T(8,128)(2,1)S(1)} %copy-done.44), channel_id=1, source_target_pairs={{0,16},{4,20},{8,24},{12,28},{16,0},{20,4},{24,8},{28,12},{1,17},{... | collective-permute-start | bytes 1671176 | tf_op jit(solution)/shard_map/ppermute | solution.py:906
  308.9 27.7 %collective-permute-start.54 = (bf16[512,512]{1,0:T(8,128)(2,1)S(1)}, bf16[512,512]{1,0:T(8,128)(2,1)S(1)}, u32[]{:S(2)}, u32[]{:S(2)}) collective-permute-start(bf16[512,512]{1,0:T(8,128)(2,1)S(1)} %add_convert_fusion.2), channel_id=1, source_target_pairs={{0,1},{1,0},{2,3},{3,2},{4,5},{5,4},{6,7},{7,6},{8,9},{9,8},{10,11... | collective-permute-start | bytes 1572872 | tf_op jit(solution)/shard_map/ppermute | solution.py:941
  312.1 24.5 %collective-permute-start.53 = (bf16[128,2048]{1,0:T(8,128)(2,1)S(1)}, bf16[128,2048]{1,0:T(8,128)(2,1)S(1)}, u32[]{:S(2)}, u32[]{:S(2)}) collective-permute-start(bf16[128,2048]{1,0:T(8,128)(2,1)S(1)} %add_convert_fusion.1), channel_id=1, source_target_pairs={{0,2},{1,3},{2,0},{3,1},{4,6},{5,7},{6,4},{7,5},{8,10},{9,11},{10,... | collective-permute-start | bytes 1572872 | tf_op jit(solution)/shard_map/ppermute | solution.py:941
  315.0 30.6 %collective-permute-start.50 = (bf16[256,512]{1,0:T(8,128)(2,1)S(1)}, bf16[256,512]{1,0:T(8,128)(2,1)S(1)}, u32[]{:S(2)}, u32[]{:S(2)}) collective-permute-start(bf16[256,512]{1,0:T(8,128)(2,1)S(1)} %get-tuple-element.546), channel_id=1, source_target_pairs={{0,1},{1,0},{2,3},{3,2},{4,5},{5,4},{6,7},{7,6},{8,9},{9,8},{10,11... | collective-permute-start | bytes 786440 | tf_op jit(solution)/shard_map/ppermute | solution.py:941
  315.6 36.6 %collective-permute-start.56 = (bf16[272,512]{1,0:T(8,128)(2,1)S(1)}, bf16[272,512]{1,0:T(8,128)(2,1)S(1)}, u32[]{:S(2)}, u32[]{:S(2)}) collective-permute-start(bf16[272,512]{1,0:T(8,128)(2,1)S(1)} %get-tuple-element.553), channel_id=1, source_target_pairs={{0,1},{1,0},{2,3},{3,2},{4,5},{5,4},{6,7},{7,6},{8,9},{9,8},{10,11... | collective-permute-start | bytes 835592 | tf_op jit(solution)/shard_map/ppermute | solution.py:941
  345.9 25.3 %collective-permute-start.55 = (bf16[128,2048]{1,0:T(8,128)(2,1)S(1)}, bf16[128,2048]{1,0:T(8,128)(2,1)S(1)}, u32[]{:S(2)}, u32[]{:S(2)}) collective-permute-start(bf16[128,2048]{1,0:T(8,128)(2,1)S(1)} %add_convert_fusion), channel_id=1, source_target_pairs={{0,1},{1,0},{2,3},{3,2},{4,5},{5,4},{6,7},{7,6},{8,9},{9,8},{10,11... | collective-permute-start | bytes 1572872 | tf_op jit(solution)/shard_map/ppermute | solution.py:941
  (74 other events, 833.0 us)
Sparse Core Ops, SparseCore 0:
  42.0 81.0 all-gather.2
  170.1 81.7 all-gather.4

commit v6 on v5

--- a/solution.py
+++ b/solution.py
@@ -962,7 +962,7 @@
 def merge(meta, own, got, late, rest, got_next):
     rows, cols = own[0].shape
     high, wide = rest[0].shape
-    steps = 4
+    steps = 2
 
     def kernel(meta, own_a, own_b, got_a, got_b, late_a, late_b, rest_a, rest_b, next_a, next_b, *outs):
         kept_ref, given_ref, pass_a, pass_b = outs
@@ -1089,9 +1089,9 @@
     got_a = order.then(got_a)
     late_a = passed(order.then(turned(rest_a, got_a)))
     taken_up = pairs(given_up, 1)
-    layer_out = order.then(chosen(order.meta, out_pool, 5))
     got_b = order.then(got_b)
     late_b = passed(order.then(turned(rest_b, got_b)))
+    layer_out = order.then(chosen(order.meta, out_pool, 5))
     late_a = order.then(late_a)
     kept_a, given_a = order.then(summed(own_a, got_a, late_a))
     taken_a = pairs(given_a, 1)

time: 386 us -> 386 us (level)
  no operation moved by 1% of the time
where the time goes in v6:
time: 386 us; the launch traced here: 385 us
  Pallas kernels  148 us (38%)
  waiting for transfers between devices  145 us (38%)
  starting transfers between devices  53.2 us (14%)
  between operations  14.9 us (4%)
  local copies, waits for them, and re-layouts  13.3 us (3%)
  other arithmetic  10.2 us (3%)
    pallas_call x13, Pallas kernels, run(): pl.pallas_call(kernel, grid_spec=pltpu.PrefetchScalarGridSpec(num_scalar_...  146 us
    ppermute x47, waiting for transfers between devices, swap(): return lax.ppermute(value, 'shard', [(i, i ^ mask) for i in range(8)])  81.9 us
    ppermute x12, waiting for transfers between devices, pairs(): return lax.ppermute(value, 'rep', [(i, i ^ mask) for i in range(4)])  62.8 us
    ppermute x47, starting transfers between devices, swap(): return lax.ppermute(value, 'shard', [(i, i ^ mask) for i in range(8)])  37.1 us
    ppermute x12, starting transfers between devices, pairs(): return lax.ppermute(value, 'rep', [(i, i ^ mask) for i in range(4)])  16 us
  transfers between devices with their start and end apart: 61, of which 26 were waited for; matrix products, arithmetic and copies ran while one was open for 3% of the time, Pallas kernels for 38%

profile of v6, /device:TPU:0, one launch (start us, length us, event | category | flops | bytes accessed | tf_op | source)
XLA Modules:
  0.0 384.8 jit_solution(14911420706148953814)
XLA Ops:
  10.9 3.0 collective-permute-start.1
  17.5 20.4 %collective-permute-done.1.refs_2_.refs_10_ = bf16[528,1024]{1,0:T(8,128)(2,1)S(1)} collective-permute-done((bf16[528,1024]{1,0:T(8,128)(2,1)}, bf16[528,1024]{1,0:T(8,128)(2,1)S(1)}, u32[]{:S(2)}, u32[]{:S(2)}) %collective-permute-start.1) | collective-permute-done | bytes 1081376 | tf_op jit(solution)/shard_map/ppermute | solution.py:906
  42.0 23.4 %collective-permute-done.3.refs_1_ = bf16[128,4096]{1,0:T(8,128)(2,1)} collective-permute-done((bf16[128,4096]{1,0:T(8,128)(2,1)}, bf16[128,4096]{1,0:T(8,128)(2,1)}, u32[]{:S(2)}, u32[]{:S(2)}) %collective-permute-start.3) | collective-permute-done | bytes 1048608 | tf_op jit(solution)/shard_map/ppermute | solution.py:906
  70.1 11.2 %shard_map.315 = (bf16[3,512,1024]{2,1,0:T(8,128)(2,1)}, f32[8,1024]{1,0:T(8,128)}, f32[1,4096]{1,0:T(1,128)}, bf16[4,512,128]{2,1,0:T(8,128)(2,1)}) custom-call(s32[8]{0:T(128)} %concatenate.24.meta, bf16[512,1024]{1,0:T(8,128)(2,1)} %bitcast.90, bf16[528,1024]{1,0:T(8,128)(2,1)} %shard_map.314.refs_0_.refs_8_, bf16[528,1024]{1,0:T(8,128)(2,1)} %copy-done.4, ...), custom_call_target="tpu_custom_call" | custom-call | flops 1024 | bytes 1024 | tf_op jit(solution)/shard_map/pallas_call | solution.py:89
  81.3 10.8 %shard_map.316 = (bf16[512,1024]{1,0:T(8,128)(2,1)}, bf16[2,16,256,256]{3,2,1,0:T(8,128)(2,1)}, f32[512,1024]{1,0:T(8,128)}) custom-call(s32[8]{0:T(128)} %concatenate.24.meta, bf16[3,512,1024]{2,1,0:T(8,128)(2,1)} %get-tuple-element.301.q_ref.k_ref.v_ref, bf16[3,512,1024]{2,1,0:T(8,128)(2,1)} %get-tuple-element.301.q_ref.k_ref.v_ref, ...), custom_call_target="tpu_custom_call" | custom-call | flops 1024 | bytes 1024 | tf_op jit(solution)/shard_map/pallas_call | solution.py:89
  95.2 9.4 %shard_map.317 = (f32[512,1024]{1,0:T(8,128)}, f32[512,128]{1,0:T(8,128)}, bf16[512,1024]{1,0:T(8,128)(2,1)}, bf16[2,4,512,128]{3,2,1,0:T(8,128)(2,1)}) custom-call(s32[8]{0:T(128)} %concatenate.24.meta, bf16[512,1024]{1,0:T(8,128)(2,1)} %get-tuple-element.311.mixed_ref.m_ref, bf16[512,1024]{1,0:T(8,128)(2,1)} %bitcast.91, ...), custom_call_target="tpu_custom_call" | custom-call | flops 1024 | bytes 1024 | tf_op jit(solution)/shard_map/pallas_call | solution.py:89
  106.5 11.4 %collective-permute-done.13.refs_2_ = bf16[512,1024]{1,0:T(8,128)(2,1)S(1)} collective-permute-done((bf16[512,1024]{1,0:T(8,128)(2,1)S(1)}, bf16[512,1024]{1,0:T(8,128)(2,1)S(1)}, u32[]{:S(2)}, u32[]{:S(2)}) %collective-permute-start.13) | collective-permute-done | bytes 1048608 | tf_op jit(solution)/shard_map/ppermute | solution.py:906
  119.0 2.7 collective-permute-done.16.refs_7_
  126.1 13.8 %shard_map.318 = (bf16[512,4096]{1,0:T(8,128)(2,1)}, bf16[512,4096]{1,0:T(8,128)(2,1)}, bf16[4,512,512]{2,1,0:T(8,128)(2,1)}) custom-call(s32[8]{0:T(128)} %concatenate.24.meta, bf16[512,1024]{1,0:T(8,128)(2,1)} %get-tuple-element.334.x_ref, f32[1,4096]{1,0:T(1,128)} %get-tuple-element.335.bias_ref, bf16[128,4096]{1,0:T(8,128)(2,1)} %refs_0_.4, ...), custom_call_target="tpu_custom_call" | custom-call | flops 1024 | bytes 1024 | tf_op jit(solution)/shard_map/pallas_call | solution.py:89
  143.7 21.3 %shard_map.319 = (bf16[512,1024]{1,0:T(8,128)(2,1)}, f32[512,1024]{1,0:T(8,128)}, bf16[512,1024]{1,0:T(8,128)(2,1)}, f32[8,1024]{1,0:T(8,128)}, bf16[512,4096]{1,0:T(8,128)(2,1)}, /*index=5*/f32[1,4096]{1,0:T(1,128)}) custom-call(s32[8]{0:T(128)} %concatenate.24.meta, bf16[512,4096]{1,0:T(8,128)(2,1)} %get-tuple-element.363.act_ref.left_ref, ...), custom_call_target="tpu_custom_call" | custom-call | flops 1024 | bytes 1024 | tf_op jit(solution)/shard_map/pallas_call | solution.py:89
  166.0 2.5 collective-permute-done.25.right_got
  170.9 9.6 %shard_map.320 = (bf16[2,512,512]{2,1,0:T(8,128)(2,1)}, bf16[2,512,512]{2,1,0:T(8,128)(2,1)}, bf16[512,512]{1,0:T(8,128)(2,1)}, bf16[512,512]{1,0:T(8,128)(2,1)}...) custom-call(s32[8]{0:T(128)} %concatenate.24.meta, bf16[512,4096]{1,0:T(8,128)(2,1)} %get-tuple-element.363.act_ref.left_ref, ...), custom_call_target="tpu_custom_call" | custom-call | flops 1024 | bytes 1024 | tf_op jit(solution)/shard_map/pallas_call | solution.py:89
  183.3 16.8 %shard_map.321 = (f32[512,1024]{1,0:T(8,128)}, bf16[512,1024]{1,0:T(8,128)(2,1)}, bf16[512,1024]{1,0:T(8,128)(2,1)}, f32[8,1024]{1,0:T(8,128)}) custom-call(s32[8]{0:T(128)} %concatenate.24.meta, bf16[512,4096]{1,0:T(8,128)(2,1)} %get-tuple-element.397.pre_ref, f32[512,1024]{1,0:T(8,128)} %get-tuple-element.402.sum_ref, ...), custom_call_target="tpu_custom_call" | custom-call | flops 1024 | bytes 1024 | tf_op jit(solution)/shard_map/pallas_call | solution.py:89
  200.1 11.1 %shard_map.322 = (bf16[2,128,2048]{2,1,0:T(8,128)(2,1)}, bf16[2,128,2048]{2,1,0:T(8,128)(2,1)}, bf16[128,2048]{1,0:T(8,128)(2,1)}, bf16[128,2048]{1,0:T(8,128)(2...) custom-call(s32[8]{0:T(128)} %concatenate.24.meta, bf16[512,1024]{1,0:T(8,128)(2,1)} %get-tuple-element.334.x_ref, ...), custom_call_target="tpu_custom_call" | custom-call | flops 1024 | bytes 1024 | tf_op jit(solution)/shard_map/pallas_call | solution.py:89
  215.7 14.7 %shard_map.323 = (bf16[3,512,1024]{2,1,0:T(8,128)(2,1)}, bf16[8,16,1024]{2,1,0:T(8,128)(2,1)}) custom-call(s32[8]{0:T(128)} %concatenate.24.meta, bf16[3,512,1024]{2,1,0:T(8,128)(2,1)} %get-tuple-element.301.q_ref.k_ref.v_ref, bf16[3,512,1024]{2,1,0:T(8,128)(2,1)} %get-tuple-element.301.q_ref.k_ref.v_ref, ...), custom_call_target="tpu_custom_call" | custom-call | flops 1024 | bytes 1024 | tf_op jit(solution)/shard_map/pallas_call | solution.py:89
  230.5 10.7 %shard_map.324 = bf16[512,1024]{1,0:T(8,128)(2,1)} custom-call(s32[8]{0:T(128)} %concatenate.24.meta, bf16[3,512,1024]{2,1,0:T(8,128)(2,1)} %get-tuple-element.462.g_ref, f32[512,1024]{1,0:T(8,128)} %get-tuple-element.439.resid_ref, bf16[528,1024]{1,0:T(8,128)(2,1)} %shard_map.314.refs_0_.refs_8_, bf16[528,1024]{1,0:T(8,128)(2,1)} %copy-done.4, ...), custom_call_target="tpu_custom_call" | custom-call | flops 1024 | bytes 1024 | tf_op jit(solution)/shard_map/pallas_call | solution.py:89
  241.2 6.5 %collective-permute-done.32.late_a = bf16[512,512]{1,0:T(8,128)(2,1)S(1)} collective-permute-done((bf16[512,512]{1,0:T(8,128)(2,1)S(1)}, bf16[512,512]{1,0:T(8,128)(2,1)S(1)}, u32[]{:S(2)}, u32[]{:S(2)}) %collective-permute-start.32) | collective-permute-done | bytes 524320 | tf_op jit(solution)/shard_map/ppermute | solution.py:906
  249.3 4.5 %shard_map.325 = (bf16[512,512]{1,0:T(8,128)(2,1)}, bf16[512,512]{1,0:T(8,128)(2,1)}, bf16[128,2048]{1,0:T(8,128)(2,1)}, bf16[128,2048]{1,0:T(8,128)(2,1)}) custom-call(s32[8]{0:T(128)} %concatenate.24.meta, bf16[512,512]{1,0:T(8,128)(2,1)} %get-tuple-element.448.own_a, bf16[512,512]{1,0:T(8,128)(2,1)} %get-tuple-element.449.own_b, ...), custom_call_target="tpu_custom_call" | custom-call | flops 1024 | bytes 1024 | tf_op jit(solution)/shard_map/pallas_call | solution.py:89
  253.8 2.4 collective-permute-done.36.vec_got
  261.0 9.5 %shard_map.326 = (bf16[2,256,512]{2,1,0:T(8,128)(2,1)}, bf16[2,256,512]{2,1,0:T(8,128)(2,1)}, bf16[256,512]{1,0:T(8,128)(2,1)}, bf16[256,512]{1,0:T(8,128)(2,1)}...) custom-call(s32[8]{0:T(128)} %concatenate.24.meta, ...), custom_call_target="tpu_custom_call" | custom-call | flops 1024 | bytes 1024 | tf_op jit(solution)/shard_map/pallas_call | solution.py:89
  280.2 2.6 collective-permute-start.46
  284.4 5.3 %collective-permute-done.40 = bf16[2,256,512]{2,1,0:T(8,128)(2,1)S(1)} collective-permute-done((bf16[2,256,512]{2,1,0:T(8,128)(2,1)}, bf16[2,256,512]{2,1,0:T(8,128)(2,1)S(1)}, u32[]{:S(2)}, u32[]{:S(2)}) %collective-permute-start.40) | collective-permute-done | bytes 524320 | tf_op jit(solution)/shard_map/ppermute | solution.py:906
  291.0 10.9 %collective-permute-done.47 = bf16[128,2048]{1,0:T(8,128)(2,1)S(1)} collective-permute-done((bf16[128,2048]{1,0:T(8,128)(2,1)S(1)}, bf16[128,2048]{1,0:T(8,128)(2,1)S(1)}, u32[]{:S(2)}, u32[]{:S(2)}) %collective-permute-start.47) | collective-permute-done | bytes 524320 | tf_op jit(solution)/shard_map/ppermute | solution.py:941
  301.9 2.4 collective-permute-done.46
  309.3 2.7 shard_map.327
  312.1 2.7 collective-permute-start.53
  317.4 19.2 %collective-permute-done.54 = bf16[512,512]{1,0:T(8,128)(2,1)S(1)} collective-permute-done((bf16[512,512]{1,0:T(8,128)(2,1)S(1)}, bf16[512,512]{1,0:T(8,128)(2,1)S(1)}, u32[]{:S(2)}, u32[]{:S(2)}) %collective-permute-start.54) | collective-permute-done | bytes 524320 | tf_op jit(solution)/shard_map/ppermute | solution.py:941
  336.7 8.9 %collective-permute-done.50 = bf16[256,512]{1,0:T(8,128)(2,1)S(1)} collective-permute-done((bf16[256,512]{1,0:T(8,128)(2,1)S(1)}, bf16[256,512]{1,0:T(8,128)(2,1)S(1)}, u32[]{:S(2)}, u32[]{:S(2)}) %collective-permute-start.50) | collective-permute-done | bytes 262176 | tf_op jit(solution)/shard_map/ppermute | solution.py:941
  345.9 6.3 %collective-permute-done.56 = bf16[272,512]{1,0:T(8,128)(2,1)S(1)} collective-permute-done((bf16[272,512]{1,0:T(8,128)(2,1)S(1)}, bf16[272,512]{1,0:T(8,128)(2,1)S(1)}, u32[]{:S(2)}, u32[]{:S(2)}) %collective-permute-start.56) | collective-permute-done | bytes 278560 | tf_op jit(solution)/shard_map/ppermute | solution.py:941
  354.3 4.1 %collective-permute-done.51 = bf16[256,512]{1,0:T(8,128)(2,1)S(1)} collective-permute-done((bf16[256,512]{1,0:T(8,128)(2,1)S(1)}, bf16[256,512]{1,0:T(8,128)(2,1)S(1)}, u32[]{:S(2)}, u32[]{:S(2)}) %collective-permute-start.51) | collective-permute-done | bytes 262176 | tf_op jit(solution)/shard_map/ppermute | solution.py:941
  360.1 8.3 %collective-permute-done.57 = bf16[272,512]{1,0:T(8,128)(2,1)S(1)} collective-permute-done((bf16[272,512]{1,0:T(8,128)(2,1)S(1)}, bf16[272,512]{1,0:T(8,128)(2,1)S(1)}, u32[]{:S(2)}, u32[]{:S(2)}) %collective-permute-start.57) | collective-permute-done | bytes 278560 | tf_op jit(solution)/shard_map/ppermute | solution.py:941
  368.5 2.6 collective-permute-start.58
  (238 shorter events, 78.6 us)
Async XLA Ops:
  7.2 135.9 %all-gather.3.cloned.1.call-start = ((), (), s32[]{:S(2)}) async-start(), calls=%async_computation | async-start | bytes 5242880 | tf_op jit(solution)/shard_map/all_gather | solution.py:1028
  10.9 27.0 %collective-permute-start.1 = (bf16[528,1024]{1,0:T(8,128)(2,1)}, bf16[528,1024]{1,0:T(8,128)(2,1)S(1)}, u32[]{:S(2)}, u32[]{:S(2)}) collective-permute-start(bf16[528,1024]{1,0:T(8,128)(2,1)} %shard_map.314.refs_0_.refs_8_), channel_id=1, source_target_pairs={{0,16},{4,20},{8,24},{12,28},{16,0},{20,4},{24,8},{28,12},{1,17},{... | collective-permute-start | bytes 3244040 | tf_op jit(solution)/shard_map/ppermute | solution.py:906
  13.8 25.5 %collective-permute-start = (bf16[528,1024]{1,0:T(8,128)(2,1)}, bf16[528,1024]{1,0:T(8,128)(2,1)S(1)}, u32[]{:S(2)}, u32[]{:S(2)}) collective-permute-start(bf16[528,1024]{1,0:T(8,128)(2,1)} %shard_map.314.refs_0_.refs_8_), channel_id=1, source_target_pairs={{0,8},{4,12},{8,0},{12,4},{16,24},{20,28},{24,16},{28,20},{1,9},{5... | collective-permute-start | bytes 3244040 | tf_op jit(solution)/shard_map/ppermute | solution.py:906
  15.3 26.6 %collective-permute-start.4 = (bf16[528,1024]{1,0:T(8,128)(2,1)}, bf16[528,1024]{1,0:T(8,128)(2,1)S(1)}, u32[]{:S(2)}, u32[]{:S(2)}) collective-permute-start(bf16[528,1024]{1,0:T(8,128)(2,1)} %shard_map.314.refs_0_.refs_8_), channel_id=1, source_target_pairs={{0,4},{4,0},{8,12},{12,8},{16,20},{20,16},{24,28},{28,24},{1,5},{5... | collective-permute-start | bytes 3244040 | tf_op jit(solution)/shard_map/ppermute | solution.py:906
  39.4 26.0 %collective-permute-start.6 = (bf16[528,1024]{1,0:T(8,128)(2,1)S(1)}, bf16[528,1024]{1,0:T(8,128)(2,1)}, u32[]{:S(2)}, u32[]{:S(2)}) collective-permute-start(bf16[528,1024]{1,0:T(8,128)(2,1)S(1)} %collective-permute-done.1.refs_2_.refs_10_), channel_id=1, source_target_pairs={{0,4},{4,0},{8,12},{12,8},{16,20},{20,16},{24,28},{28,24},{1,5},{5... | collective-permute-start | bytes 3244040 | tf_op jit(solution)/shard_map/ppermute | solution.py:906
  39.4 26.0 %collective-permute-start.5 = (bf16[528,1024]{1,0:T(8,128)(2,1)S(1)}, bf16[528,1024]{1,0:T(8,128)(2,1)}, u32[]{:S(2)}, u32[]{:S(2)}) collective-permute-start(bf16[528,1024]{1,0:T(8,128)(2,1)S(1)} %collective-permute-done.refs_1_.refs_9_), channel_id=1, source_target_pairs={{0,4},{4,0},{8,12},{12,8},{16,20},{20,16},{24,28},{28,24},{1,5},{5... | collective-permute-start | bytes 3244040 | tf_op jit(solution)/shard_map/ppermute | solution.py:906
  39.9 25.9 %collective-permute-start.2 = (bf16[528,1024]{1,0:T(8,128)(2,1)S(1)}, bf16[528,1024]{1,0:T(8,128)(2,1)}, u32[]{:S(2)}, u32[]{:S(2)}) collective-permute-start(bf16[528,1024]{1,0:T(8,128)(2,1)S(1)} %collective-permute-done.refs_1_.refs_9_), channel_id=1, source_target_pairs={{0,16},{4,20},{8,24},{12,28},{16,0},{20,4},{24,8},{28,12},{1,17},{... | collective-permute-start | bytes 3244040 | tf_op jit(solution)/shard_map/ppermute | solution.py:906
  40.2 25.2 %collective-permute-start.3 = (bf16[128,4096]{1,0:T(8,128)(2,1)}, bf16[128,4096]{1,0:T(8,128)(2,1)}, u32[]{:S(2)}, u32[]{:S(2)}) collective-permute-start(bf16[128,4096]{1,0:T(8,128)(2,1)} %refs_0_.4), channel_id=1, source_target_pairs={{0,8},{4,12},{8,0},{12,4},{16,24},{20,28},{24,16},{28,20},{1,9},{5... | collective-permute-start | bytes 3145736 | tf_op jit(solution)/shard_map/ppermute | solution.py:906
  41.9 228.7 %all-gather.5.cloned.1.call-start = ((), (), s32[]{:S(2)}) async-start(), calls=%async_computation.1 | async-start | bytes 5242880 | tf_op jit(solution)/shard_map/all_gather | solution.py:1054
  65.7 26.4 %collective-permute-start.10 = (bf16[128,4096]{1,0:T(8,128)(2,1)}, bf16[128,4096]{1,0:T(8,128)(2,1)S(1)}, u32[]{:S(2)}, u32[]{:S(2)}) collective-permute-start(bf16[128,4096]{1,0:T(8,128)(2,1)} %refs_0_.4), channel_id=1, source_target_pairs={{0,4},{4,0},{8,12},{12,8},{16,20},{20,16},{24,28},{28,24},{1,5},{5... | collective-permute-start | bytes 3145736 | tf_op jit(solution)/shard_map/ppermute | solution.py:906
  66.2 25.9 %collective-permute-start.8 = (bf16[128,4096]{1,0:T(8,128)(2,1)}, bf16[128,4096]{1,0:T(8,128)(2,1)S(1)}, u32[]{:S(2)}, u32[]{:S(2)}) collective-permute-start(bf16[128,4096]{1,0:T(8,128)(2,1)} %refs_0_.4), channel_id=1, source_target_pairs={{0,16},{4,20},{8,24},{12,28},{16,0},{20,4},{24,8},{28,12},{1,17},{... | collective-permute-start | bytes 3145736 | tf_op jit(solution)/shard_map/ppermute | solution.py:906
  67.6 25.2 %collective-permute-start.9 = (bf16[512,1024]{1,0:T(8,128)(2,1)}, bf16[512,1024]{1,0:T(8,128)(2,1)}, u32[]{:S(2)}, u32[]{:S(2)}) collective-permute-start(bf16[512,1024]{1,0:T(8,128)(2,1)} %refs_0_.3), channel_id=1, source_target_pairs={{0,8},{4,12},{8,0},{12,4},{16,24},{20,28},{24,16},{28,20},{1,9},{5... | collective-permute-start | bytes 3145736 | tf_op jit(solution)/shard_map/ppermute | solution.py:906
  69.1 23.7 %collective-permute-start.11 = (bf16[128,4096]{1,0:T(8,128)(2,1)}, bf16[128,4096]{1,0:T(8,128)(2,1)S(1)}, u32[]{:S(2)}, u32[]{:S(2)}) collective-permute-start(bf16[128,4096]{1,0:T(8,128)(2,1)} %collective-permute-done.3.refs_1_), channel_id=1, source_target_pairs={{0,4},{4,0},{8,12},{12,8},{16,20},{20,16},{24,28},{28,24},{1,5},{5... | collective-permute-start | bytes 3145736 | tf_op jit(solution)/shard_map/ppermute | solution.py:906
  92.8 25.1 %collective-permute-start.13 = (bf16[512,1024]{1,0:T(8,128)(2,1)S(1)}, bf16[512,1024]{1,0:T(8,128)(2,1)S(1)}, u32[]{:S(2)}, u32[]{:S(2)}) collective-permute-start(bf16[512,1024]{1,0:T(8,128)(2,1)S(1)} %copy-done.20), channel_id=1, source_target_pairs={{0,16},{4,20},{8,24},{12,28},{16,0},{20,4},{24,8},{28,12},{1,17},{... | collective-permute-start | bytes 3145736 | tf_op jit(solution)/shard_map/ppermute | solution.py:906
  93.5 24.4 %collective-permute-start.15 = (bf16[128,4096]{1,0:T(8,128)(2,1)S(1)}, bf16[128,4096]{1,0:T(8,128)(2,1)S(1)}, u32[]{:S(2)}, u32[]{:S(2)}) collective-permute-start(bf16[128,4096]{1,0:T(8,128)(2,1)S(1)} %collective-permute-done.8.refs_2_), channel_id=1, source_target_pairs={{0,4},{4,0},{8,12},{12,8},{16,20},{20,16},{24,28},{28,24},{1,5},{5... | collective-permute-start | bytes 3145736 | tf_op jit(solution)/shard_map/ppermute | solution.py:906
  93.5 25.6 %collective-permute-start.12 = (bf16[128,4096]{1,0:T(8,128)(2,1)S(1)}, bf16[128,4096]{1,0:T(8,128)(2,1)S(1)}, u32[]{:S(2)}, u32[]{:S(2)}) collective-permute-start(bf16[128,4096]{1,0:T(8,128)(2,1)S(1)} %collective-permute-done.8.refs_2_), channel_id=1, source_target_pairs={{0,8},{4,12},{8,0},{12,4},{16,24},{20,28},{24,16},{28,20},{1,9},{5... | collective-permute-start | bytes 3145736 | tf_op jit(solution)/shard_map/ppermute | solution.py:906
  121.7 18.2 %collective-permute-start.19 = (bf16[512,1024]{1,0:T(8,128)(2,1)}, bf16[512,1024]{1,0:T(8,128)(2,1)S(1)}, u32[]{:S(2)}, u32[]{:S(2)}) collective-permute-start(bf16[512,1024]{1,0:T(8,128)(2,1)} %refs_0_.3), channel_id=1, source_target_pairs={{0,4},{4,0},{8,12},{12,8},{16,20},{20,16},{24,28},{28,24},{1,5},{5... | collective-permute-start | bytes 3145736 | tf_op jit(solution)/shard_map/ppermute | solution.py:906
  142.9 25.6 %collective-permute-start.24 = (bf16[4,512,512]{2,1,0:T(8,128)(2,1)}, bf16[4,512,512]{2,1,0:T(8,128)(2,1)S(1)}, u32[]{:S(2)}, u32[]{:S(2)}) collective-permute-start(bf16[4,512,512]{2,1,0:T(8,128)(2,1)} %get-tuple-element.384), channel_id=1, source_target_pairs={{0,4},{4,0},{8,12},{12,8},{16,20},{20,16},{24,28},{28,24},{1,5},{5... | collective-permute-start | bytes 6291464 | tf_op jit(solution)/shard_map/ppermute | solution.py:906
  180.6 30.6 %collective-permute-start.28 = (bf16[2,512,512]{2,1,0:T(8,128)(2,1)}, bf16[2,512,512]{2,1,0:T(8,128)(2,1)S(1)}, u32[]{:S(2)}, u32[]{:S(2)}) collective-permute-start(bf16[2,512,512]{2,1,0:T(8,128)(2,1)} %get-tuple-element.418), channel_id=1, source_target_pairs={{0,16},{4,20},{8,24},{12,28},{16,0},{20,4},{24,8},{28,12},{1,17},{... | collective-permute-start | bytes 3145736 | tf_op jit(solution)/shard_map/ppermute | solution.py:906
  182.2 29.1 %collective-permute-start.29 = (bf16[2,512,512]{2,1,0:T(8,128)(2,1)}, bf16[2,512,512]{2,1,0:T(8,128)(2,1)S(1)}, u32[]{:S(2)}, u32[]{:S(2)}) collective-permute-start(bf16[2,512,512]{2,1,0:T(8,128)(2,1)} %get-tuple-element.419), channel_id=1, source_target_pairs={{0,8},{4,12},{8,0},{12,4},{16,24},{20,28},{24,16},{28,20},{1,9},{5... | collective-permute-start | bytes 3145736 | tf_op jit(solution)/shard_map/ppermute | solution.py:906
  211.2 36.5 %collective-permute-start.30 = (bf16[2,128,2048]{2,1,0:T(8,128)(2,1)}, bf16[2,128,2048]{2,1,0:T(8,128)(2,1)}, u32[]{:S(2)}, u32[]{:S(2)}) collective-permute-start(bf16[2,128,2048]{2,1,0:T(8,128)(2,1)} %get-tuple-element.441), channel_id=1, source_target_pairs={{0,16},{4,20},{8,24},{12,28},{16,0},{20,4},{24,8},{28,12},{1,17},{... | collective-permute-start | bytes 3145736 | tf_op jit(solution)/shard_map/ppermute | solution.py:906
  211.6 37.1 %collective-permute-start.31 = (bf16[2,128,2048]{2,1,0:T(8,128)(2,1)}, bf16[2,128,2048]{2,1,0:T(8,128)(2,1)}, u32[]{:S(2)}, u32[]{:S(2)}) collective-permute-start(bf16[2,128,2048]{2,1,0:T(8,128)(2,1)} %get-tuple-element.442), channel_id=1, source_target_pairs={{0,8},{4,12},{8,0},{12,4},{16,24},{20,28},{24,16},{28,20},{1,9},{5... | collective-permute-start | bytes 3145736 | tf_op jit(solution)/shard_map/ppermute | solution.py:906
  212.9 34.8 %collective-permute-start.32 = (bf16[512,512]{1,0:T(8,128)(2,1)S(1)}, bf16[512,512]{1,0:T(8,128)(2,1)S(1)}, u32[]{:S(2)}, u32[]{:S(2)}) collective-permute-start(bf16[512,512]{1,0:T(8,128)(2,1)S(1)} %fusion.5), channel_id=1, source_target_pairs={{0,8},{4,12},{8,0},{12,4},{16,24},{20,28},{24,16},{28,20},{1,9},{5... | collective-permute-start | bytes 1572872 | tf_op jit(solution)/shard_map/ppermute | solution.py:906
  214.0 33.7 %collective-permute-start.33 = (bf16[512,512]{1,0:T(8,128)(2,1)S(1)}, bf16[512,512]{1,0:T(8,128)(2,1)S(1)}, u32[]{:S(2)}, u32[]{:S(2)}) collective-permute-start(bf16[512,512]{1,0:T(8,128)(2,1)S(1)} %fusion.4), channel_id=1, source_target_pairs={{0,16},{4,20},{8,24},{12,28},{16,0},{20,4},{24,8},{28,12},{1,17},{... | collective-permute-start | bytes 1572872 | tf_op jit(solution)/shard_map/ppermute | solution.py:906
  278.5 23.3 %collective-permute-start.47 = (bf16[128,2048]{1,0:T(8,128)(2,1)S(1)}, bf16[128,2048]{1,0:T(8,128)(2,1)S(1)}, u32[]{:S(2)}, u32[]{:S(2)}) collective-permute-start(bf16[128,2048]{1,0:T(8,128)(2,1)S(1)} %get-tuple-element.532), channel_id=1, source_target_pairs={{0,1},{1,0},{2,3},{3,2},{4,5},{5,4},{6,7},{7,6},{8,9},{9,8},{10,11... | collective-permute-start | bytes 1572872 | tf_op jit(solution)/shard_map/ppermute | solution.py:941
  280.2 24.1 %collective-permute-start.46 = (bf16[512,512]{1,0:T(8,128)(2,1)S(1)}, bf16[512,512]{1,0:T(8,128)(2,1)S(1)}, u32[]{:S(2)}, u32[]{:S(2)}) collective-permute-start(bf16[512,512]{1,0:T(8,128)(2,1)S(1)} %add_convert_fusion.3), channel_id=1, source_target_pairs={{0,2},{1,3},{2,0},{3,1},{4,6},{5,7},{6,4},{7,5},{8,10},{9,11},{10,... | collective-permute-start | bytes 1572872 | tf_op jit(solution)/shard_map/ppermute | solution.py:941
  282.8 23.9 %collective-permute-start.42 = (bf16[2,272,512]{2,1,0:T(8,128)(2,1)S(1)}, bf16[2,272,512]{2,1,0:T(8,128)(2,1)S(1)}, u32[]{:S(2)}, u32[]{:S(2)}) collective-permute-start(bf16[2,272,512]{2,1,0:T(8,128)(2,1)S(1)} %copy-done.44), channel_id=1, source_target_pairs={{0,16},{4,20},{8,24},{12,28},{16,0},{20,4},{24,8},{28,12},{1,17},{... | collective-permute-start | bytes 1671176 | tf_op jit(solution)/shard_map/ppermute | solution.py:906
  308.9 27.7 %collective-permute-start.54 = (bf16[512,512]{1,0:T(8,128)(2,1)S(1)}, bf16[512,512]{1,0:T(8,128)(2,1)S(1)}, u32[]{:S(2)}, u32[]{:S(2)}) collective-permute-start(bf16[512,512]{1,0:T(8,128)(2,1)S(1)} %add_convert_fusion.2), channel_id=1, source_target_pairs={{0,1},{1,0},{2,3},{3,2},{4,5},{5,4},{6,7},{7,6},{8,9},{9,8},{10,11... | collective-permute-start | bytes 1572872 | tf_op jit(solution)/shard_map/ppermute | solution.py:941
  312.1 24.5 %collective-permute-start.53 = (bf16[128,2048]{1,0:T(8,128)(2,1)S(1)}, bf16[128,2048]{1,0:T(8,128)(2,1)S(1)}, u32[]{:S(2)}, u32[]{:S(2)}) collective-permute-start(bf16[128,2048]{1,0:T(8,128)(2,1)S(1)} %add_convert_fusion.1), channel_id=1, source_target_pairs={{0,2},{1,3},{2,0},{3,1},{4,6},{5,7},{6,4},{7,5},{8,10},{9,11},{10,... | collective-permute-start | bytes 1572872 | tf_op jit(solution)/shard_map/ppermute | solution.py:941
  315.0 30.6 %collective-permute-start.50 = (bf16[256,512]{1,0:T(8,128)(2,1)S(1)}, bf16[256,512]{1,0:T(8,128)(2,1)S(1)}, u32[]{:S(2)}, u32[]{:S(2)}) collective-permute-start(bf16[256,512]{1,0:T(8,128)(2,1)S(1)} %get-tuple-element.546), channel_id=1, source_target_pairs={{0,1},{1,0},{2,3},{3,2},{4,5},{5,4},{6,7},{7,6},{8,9},{9,8},{10,11... | collective-permute-start | bytes 786440 | tf_op jit(solution)/shard_map/ppermute | solution.py:941
  315.6 36.6 %collective-permute-start.56 = (bf16[272,512]{1,0:T(8,128)(2,1)S(1)}, bf16[272,512]{1,0:T(8,128)(2,1)S(1)}, u32[]{:S(2)}, u32[]{:S(2)}) collective-permute-start(bf16[272,512]{1,0:T(8,128)(2,1)S(1)} %get-tuple-element.553), channel_id=1, source_target_pairs={{0,1},{1,0},{2,3},{3,2},{4,5},{5,4},{6,7},{7,6},{8,9},{9,8},{10,11... | collective-permute-start | bytes 835592 | tf_op jit(solution)/shard_map/ppermute | solution.py:941
  345.9 25.3 %collective-permute-start.55 = (bf16[128,2048]{1,0:T(8,128)(2,1)S(1)}, bf16[128,2048]{1,0:T(8,128)(2,1)S(1)}, u32[]{:S(2)}, u32[]{:S(2)}) collective-permute-start(bf16[128,2048]{1,0:T(8,128)(2,1)S(1)} %add_convert_fusion), channel_id=1, source_target_pairs={{0,1},{1,0},{2,3},{3,2},{4,5},{5,4},{6,7},{7,6},{8,9},{9,8},{10,11... | collective-permute-start | bytes 1572872 | tf_op jit(solution)/shard_map/ppermute | solution.py:941
  (74 other events, 832.5 us)
Sparse Core Ops, SparseCore 0:
  42.0 81.0 all-gather.2
  170.1 81.7 all-gather.4
